TPU v7x, 256 devices: a whole 4x4x8 slice. The times are simulated.
256 devices in a mesh: pair: 128 (over x, y, z_lo, core), aux: 2 (over z_hi).
Axes of the slice: x: 4, y: 4, z: 8 (z_hi: 2, z_lo: 4; z = z_hi * 4 + z_lo), core: 2. Of those that a mesh axis runs over, the one named last changes fastest.
Arguments:
- amplitudes: bfloat16 [256, 512, 512], P(None, 'pair'), may hold values from -6 to 6
- ladder: bfloat16 [256, 256], replicated, may hold values from -0.375 to 0.375
- cholesky: bfloat16 [16, 512, 512], P('aux'), may hold values from -0.25 to 0.25
- pair_ids: int32 [256], P('pair'), may hold values from 0 to 255, each once
- occ_energy: float32 [16], replicated, may hold values from -2 to -0.5
- vir_energy: float32 [512], replicated, may hold values from 0.5 to 3
Outputs:
- update: float32 [256, 512, 512], P('pair', None, 'aux')
Inputs may be any that keep to these rules, and one draw needn't show every extreme that they name: `pair_ids`: every value 0 to 255 appears once.
All inputs are finite; a program needn't handle non-finite values.
Results may differ from a plain program's by a relative error of at most 0.0029.
Values may be sent and summed in bfloat16 or wider, within the bound.
No kernel may reach another device: no remote copies, remote signals or barrier semaphores. Data moves between devices by JAX's collectives and lax.ppermute only.
A program may use at most 64 MiB of HBM per device.

v0:
```python
import jax
import jax.numpy as jnp
from jax import lax
from jax.sharding import PartitionSpec as P

NO = 16


def hole_ladder(ladder, amp_block):
    rows = amp_block.shape[0]
    flat_block = amp_block.reshape(rows, -1)
    result = jnp.dot(ladder, flat_block, preferred_element_type=jnp.float32).astype(jnp.bfloat16)
    return result.reshape(amp_block.shape)


def shards(amplitudes, ladder, cholesky, pair_ids, occ_energy, vir_energy):
    n_virt = amplitudes.shape[2]
    half_width = n_virt // lax.axis_size("aux")
    aux_index = lax.axis_index("aux")
    hole_term = hole_ladder(ladder, amplitudes)
    pair_amps, pair_hole = (
        lax.all_to_all(amplitudes, "pair", split_axis=0, concat_axis=1, tiled=True),
        lax.all_to_all(hole_term, "pair", split_axis=0, concat_axis=1, tiled=True),
    )
    pair_hole = lax.dynamic_slice_in_dim(pair_hole, aux_index * half_width, half_width, 2)
    mixed_terms = jnp.einsum(
        "qac,pcd->qpad", cholesky, pair_amps, preferred_element_type=jnp.float32
    ).astype(jnp.bfloat16)
    partial_value = jnp.einsum(
        "qpad,qbd->pab", mixed_terms, cholesky, preferred_element_type=jnp.float32
    )
    summed = lax.psum_scatter(partial_value, "aux", scatter_dimension=2, tiled=True)
    first_occ = pair_ids // NO
    second_occ = pair_ids % NO
    orbitals = jnp.arange(NO, dtype=jnp.int32)
    first_hot = (first_occ[:, None] == orbitals[None, :]).astype(jnp.float32)
    second_hot = (second_occ[:, None] == orbitals[None, :]).astype(jnp.float32)
    occ_sum = jnp.sum((first_hot + second_hot) * occ_energy[None, :], axis=1)
    vir_cols = lax.dynamic_slice_in_dim(vir_energy, aux_index * half_width, half_width, 0)
    denominator = vir_energy[None, :, None] + vir_cols[None, None, :] - occ_sum[:, None, None]
    return (pair_hole.astype(jnp.float32) + summed) / denominator


def solution(mesh):
    in_specs = (P(None, "pair", None), P(), P("aux", None, None), P("pair"), P(), P())
    out_specs = P("pair", None, "aux")
    return jax.shard_map(shards, mesh=mesh, in_specs=in_specs, out_specs=out_specs, check_vma=False)
```

profile of v0, /device:TPU:1, one launch (start us, length us, event | category | flops | bytes accessed | tf_op | source)
XLA Modules:
  0.0 158.3 jit_solution(14704487854787653725)
XLA Ops:
  6.5 0.0 copy-start
  6.5 0.0 reduce-scatter.2.cloned.1.call-start
  6.5 43.5 %all_to_all.36 = bf16[256,4,512]{2,1,0:T(4,128)(2,1)S(1)} all-to-all(bf16[256,4,512]{2,1,0:T(4,128)(2,1)} %param.6), channel_id=1, replica_groups=mesh['pair'=128,'aux'=2] {'pair'}, dimensions={0} | all-to-all | bytes 2097152 | tf_op jit(solution)/shard_map/all_to_all | solution.py:22
  50.0 0.8 copy.11
  50.9 0.0 copy-start.1
  50.9 13.8 %fusion.10 = f32[2,512,512]{2,1,0:T(8,128)} fusion(bf16[8,512,512]{2,1,0:T(8,128)(2,1)} %param.8, bf16[2,512,512,1]{2,0,1,3:T(2,128)(2,1)S(1)} %bitcast.40), kind=kOutput, calls=%fused_computation.7 | convolution fusion | flops 8594128896 | bytes 7340032 | tf_op jit(solution)/shard_map/qpad,qbd->pab/dot_general | solution.py:29
  64.6 0.0 reduce-scatter.2.cloned.1.call-update
  64.7 0.0 copy-done.1
  64.7 0.0 copy-start.2
  64.7 0.0 copy-start.4
  64.7 0.0 copy-start.3
  64.7 0.3 copy.19
  65.0 0.0 copy-done
  65.0 0.4 convolution_convert_fusion
  65.4 1.6 reshape.43
  67.0 6.6 %all-to-all-start = ((bf16[256,4,512]{2,1,0:T(4,128)(2,1)}), bf16[256,4,512]{2,1,0:T(4,128)(2,1)S(1)}, u32[]{:S(2)}, u32[]{:S(2)}) async-start(bf16[256,4,512]{2,1,0:T(4,128)(2,1)} %reshape.43), calls=%async_computation | async-start | bytes 2097152 | tf_op jit(solution)/shard_map/all_to_all | solution.py:23
  73.6 0.0 copy-done.2
  73.6 0.1 dynamic_slice.7
  73.7 0.0 copy-done.4
  73.7 0.0 copy-done.3
  73.7 0.2 fusion.21
  73.9 0.1 broadcast_add_fusion
  74.0 74.3 %all-to-all-done = bf16[256,4,512]{2,1,0:T(4,128)(2,1)S(1)} async-done(((bf16[256,4,512]{2,1,0:T(4,128)(2,1)}), bf16[256,4,512]{2,1,0:T(4,128)(2,1)S(1)}, u32[]{:S(2)}, u32[]{:S(2)}) %all-to-all-start) | async-done | bytes 1048608 | tf_op jit(solution)/shard_map/all_to_all | solution.py:23
  148.3 0.4 copy.24
  148.7 0.3 all_to_all.29
  149.0 0.0 reduce-scatter.2.cloned.1.call-done
  149.0 2.5 %subtract_divide_fusion = f32[2,512,256]{2,1,0:T(8,128)} fusion(f32[2,512,256]{2,1,0:T(8,128)} %reduce-scatter.2.cloned.1.call-done, f32[2]{0:T(128)S(1)} %fusion.21, f32[512,256]{1,0:T(8,128)S(1)} %broadcast_add_fusion, bf16[2,512,512]{2,1,0:T(8,128)(2,1)S(1)} %all_to_all.29, s32[]{:T(128)S(6)} %select_n.16), kind=kLoop, calls=%fused_computation.10 | loop fusion | flops 1048576 | bytes 3145740 | tf_op jit(solution)/shard_map/div | solution.py:41
  (1 shorter events, 0.0 us)
Async XLA Ops:
  6.5 58.4 %copy-start = (bf16[256,256]{1,0:T(8,128)(2,1)S(1)}, bf16[256,256]{1,0:T(8,128)(2,1)}, u32[]{:S(2)}) copy-start(bf16[256,256]{1,0:T(8,128)(2,1)} %param.7) | copy-start | bytes 393220
  6.5 142.5 %reduce-scatter.2.cloned.1.call-start = ((), (), s32[]{:S(2)}) async-start(), calls=%async_computation.3 | async-start | bytes 3145728 | tf_op jit(solution)/shard_map/reduce_scatter | solution.py:32
  50.9 13.8 %copy-start.1 = (bf16[256,4,512]{2,1,0:T(4,128)(2,1)S(1)}, bf16[256,4,512]{2,1,0:T(4,128)(2,1)}, u32[]{:S(2)}) copy-start(bf16[256,4,512]{2,1,0:T(4,128)(2,1)} %param.6) | copy-start | bytes 3145732
  64.7 8.9 %copy-start.2 = (f32[512]{0:T(512)S(1)}, f32[512]{0:T(512)}, u32[]{:S(2)}) copy-start(f32[512]{0:T(512)} %param.11) | copy-start | bytes 6148
  64.7 9.0 %copy-start.4 = (s32[2]{0:T(128)S(1)}, s32[2]{0:T(128)}, u32[]{:S(2)}) copy-start(s32[2]{0:T(128)} %param.9) | copy-start | bytes 28
  64.7 9.0 %copy-start.3 = (f32[16]{0:T(128)S(1)}, f32[16]{0:T(128)}, u32[]{:S(2)}) copy-start(f32[16]{0:T(128)} %param.10) | copy-start | bytes 196
  67.0 81.3 %all-to-all-start = ((bf16[256,4,512]{2,1,0:T(4,128)(2,1)}), bf16[256,4,512]{2,1,0:T(4,128)(2,1)S(1)}, u32[]{:S(2)}, u32[]{:S(2)}) async-start(bf16[256,4,512]{2,1,0:T(4,128)(2,1)} %reshape.43), calls=%async_computation | async-start | bytes 2097152 | tf_op jit(solution)/shard_map/all_to_all | solution.py:23
Sparse Core Ops, SparseCore 0:
  64.8 76.6 reduce-scatter.1
where the time goes:
time: 159 us; the launch traced here: 158 us
  waiting for transfers between devices  74.3 us (47%)
  blocking collectives  43.5 us (27%)
  matrix products  14.2 us (9%)
  between operations  13.5 us (8%)
  starting transfers between devices  6.57 us (4%)
  local copies, waits for them, and re-layouts  3.43 us (2%)
  other arithmetic  2.79 us (2%)
    all_to_all x1, waiting for transfers between devices, shards(): lax.all_to_all(hole_term, 'pair', split_axis=0, concat_axis=1, tiled=True)  74.3 us
    all_to_all x1, blocking collectives, shards(): lax.all_to_all(amplitudes, 'pair', split_axis=0, concat_axis=1, tiled=True)  43.5 us
    dot_general x1, matrix products, shards(): jnp.einsum('qpad,qbd->pab', mixed_terms, cholesky, preferred_element_type...  13.8 us
    all_to_all x1, starting transfers between devices, shards(): lax.all_to_all(hole_term, 'pair', split_axis=0, concat_axis=1, tiled=True)  6.57 us
  transfers between devices with their start and end apart: 2, of which 1 were waited for; matrix products, arithmetic and copies ran while one was open for 2% of the time, Pallas kernels for 0%

commit v1 on v0

v1 whole, which is shorter than its diff:
```python
import jax
import jax.numpy as jnp
from jax import lax
from jax.sharding import PartitionSpec as P

NO = 16


def denominators(pair_ids, occ_energy, vir_rows, vir_cols):
    orbitals = jnp.arange(NO, dtype=jnp.int32)
    first_hot = (pair_ids[:, None] // NO == orbitals[None, :]).astype(jnp.float32)
    second_hot = (pair_ids[:, None] % NO == orbitals[None, :]).astype(jnp.float32)
    occ_sum = jnp.sum((first_hot + second_hot) * occ_energy[None, :], axis=1)
    return vir_rows[None, :, None] + vir_cols[None, None, :] - occ_sum[:, None, None]


def shards(amplitudes, ladder, cholesky, pair_ids, occ_energy, vir_energy):
    n_virt = amplitudes.shape[2]
    rows = amplitudes.shape[1]
    half_width = n_virt // lax.axis_size("aux")
    aux_index = lax.axis_index("aux")
    mine = aux_index * half_width
    amp_half = lax.dynamic_slice_in_dim(amplitudes, mine, half_width, 2)
    hole_half = jnp.dot(
        ladder, amp_half.reshape(amp_half.shape[0], -1), preferred_element_type=jnp.float32
    ).astype(jnp.bfloat16).reshape(-1, rows, half_width)
    pair_amps = lax.all_to_all(amplitudes, "pair", split_axis=0, concat_axis=1, tiled=True)
    pair_hole = lax.all_to_all(hole_half, "pair", split_axis=0, concat_axis=1, tiled=True)
    mixed = jnp.einsum(
        "qac,pcd->qpad", cholesky, pair_amps, preferred_element_type=jnp.float32
    ).astype(jnp.bfloat16)
    other_cols = lax.dynamic_slice_in_dim(cholesky, half_width - mine, half_width, 1)
    own_cols = lax.dynamic_slice_in_dim(cholesky, mine, half_width, 1)
    theirs = jnp.einsum("qpad,qbd->pab", mixed, other_cols, preferred_element_type=jnp.float32)
    received = lax.ppermute(theirs.astype(jnp.bfloat16), "aux", [(0, 1), (1, 0)])
    own = jnp.einsum("qpad,qbd->pab", mixed, own_cols, preferred_element_type=jnp.float32)
    vir_cols = lax.dynamic_slice_in_dim(vir_energy, mine, half_width, 0)
    denominator = denominators(pair_ids, occ_energy, vir_energy, vir_cols)
    total = pair_hole.astype(jnp.float32) + own + received.astype(jnp.float32)
    return total / denominator


def solution(mesh):
    in_specs = (P(None, "pair", None), P(), P("aux", None, None), P("pair"), P(), P())
    out_specs = P("pair", None, "aux")
    return jax.shard_map(shards, mesh=mesh, in_specs=in_specs, out_specs=out_specs, check_vma=False)
```

time: 159 us -> 103 us (0.65)
  the two profiles are of different devices: /device:TPU:1 before, /device:TPU:71 now
where the time goes in v1:
time: 103 us; the launch traced here: 102 us
  waiting for transfers between devices  46.3 us (45%)
  starting transfers between devices  27.9 us (27%)
  matrix products  23.6 us (23%)
  local copies, waits for them, and re-layouts  3.92 us (4%)
    ppermute x1, waiting for transfers between devices, shards(): lax.ppermute(theirs.astype(jnp.bfloat16), 'aux', [(0, 1), (1, 0)])  23.9 us
    all_to_all x1, waiting for transfers between devices, shards(): lax.all_to_all(amplitudes, 'pair', split_axis=0, concat_axis=1, tiled=True)  22.5 us
    all_to_all x1, starting transfers between devices, shards(): lax.all_to_all(amplitudes, 'pair', split_axis=0, concat_axis=1, tiled=True)  12.9 us
    all_to_all x1, starting transfers between devices, shards(): lax.all_to_all(hole_half, 'pair', split_axis=0, concat_axis=1, tiled=True)  10.8 us
    dot_general x1, matrix products, shards(): jnp.einsum('qac,pcd->qpad', cholesky, pair_amps, preferred_element_type=j...  9.16 us
    dot_general x1, matrix products, shards(): jnp.einsum('qpad,qbd->pab', mixed, own_cols, preferred_element_type=jnp.f...  7.45 us
    dot_general x1, matrix products, shards(): jnp.einsum('qpad,qbd->pab', mixed, other_cols, preferred_element_type=jnp...  6.6 us
    ppermute x1, starting transfers between devices, shards(): lax.ppermute(theirs.astype(jnp.bfloat16), 'aux', [(0, 1), (1, 0)])  4.21 us
  transfers between devices with their start and end apart: 3, of which 2 were waited for; matrix products, arithmetic and copies ran while one was open for 20% of the time, Pallas kernels for 0%

profile of v1, /device:TPU:71, one launch (start us, length us, event | category | flops | bytes accessed | tf_op | source)
XLA Modules:
  0.0 102.3 jit_solution(12122775324194357588)
XLA Ops:
  0.0 0.0 copy-start
  0.0 0.0 copy-start.4
  0.0 12.9 %all-to-all-start.1 = ((bf16[256,4,512]{2,1,0:T(4,128)(2,1)}), bf16[256,4,512]{2,1,0:T(4,128)(2,1)S(1)}, u32[]{:S(2)}, u32[]{:S(2)}) async-start(bf16[256,4,512]{2,1,0:T(4,128)(2,1)} %param.6), calls=%async_computation.1 | async-start | bytes 2097152 | tf_op jit(solution)/shard_map/all_to_all | solution.py:27
  12.9 1.3 %constant_dynamic-slice_fusion = bf16[256,4,256]{2,1,0:T(4,128)(2,1)S(1)} fusion(bf16[256,4,512]{2,1,0:T(4,128)(2,1)} %param.6, s32[]{:T(128)S(6)} %select_n.22), kind=kLoop, calls=%fused_computation.31 | loop fusion | bytes 1048580 | tf_op jit(solution)/shard_map/dynamic_slice | solution.py:23
  14.2 0.1 copy.30
  14.3 0.0 copy-done
  14.3 0.4 convolution_convert_fusion.1
  14.7 1.1 %copy.17 = bf16[256,4,256]{2,1,0:T(4,128)(2,1)} copy(bf16[256,4,256]{0,2,1:T(8,128)(2,1)S(1)} %bitcast.66) | data formatting | bytes 1048576 | tf_op jit(solution)/shard_map/reshape | solution.py:26
  15.8 0.0 copy-done.4
  15.8 22.5 %all-to-all-done.1 = bf16[256,4,512]{2,1,0:T(4,128)(2,1)S(1)} async-done(((bf16[256,4,512]{2,1,0:T(4,128)(2,1)}), bf16[256,4,512]{2,1,0:T(4,128)(2,1)S(1)}, u32[]{:S(2)}, u32[]{:S(2)}) %all-to-all-start.1) | async-done | bytes 1048608 | tf_op jit(solution)/shard_map/all_to_all | solution.py:27
  38.2 10.8 %all-to-all-start = ((bf16[256,4,256]{2,1,0:T(4,128)(2,1)}), bf16[256,4,256]{2,1,0:T(4,128)(2,1)S(1)}, u32[]{:S(2)}, u32[]{:S(2)}) async-start(bf16[256,4,256]{2,1,0:T(4,128)(2,1)} %copy.17), calls=%async_computation | async-start | bytes 1048576 | tf_op jit(solution)/shard_map/all_to_all | solution.py:28
  49.0 0.8 copy.19
  49.9 0.0 copy-start.3
  49.9 9.2 %convolution_convert_fusion = bf16[2,512,8,512]{3,1,2,0:T(8,128)(2,1)} fusion(bf16[8,512,512]{2,1,0:T(8,128)(2,1)} %param.8, bf16[2,512,512,1]{2,0,1,3:T(2,128)(2,1)S(1)} %bitcast.68), kind=kOutput, calls=%fused_computation.4 | convolution fusion | flops 4299161600 | bytes 13631488 | tf_op jit(solution)/shard_map/qac,pcd->qpad/dot_general | solution.py:29
  59.0 0.0 copy-done.3
  59.0 0.0 copy-start.2
  59.0 0.0 copy-start.1
  59.0 6.6 %fusion.24 = bf16[2,512,256]{2,1,0:T(8,128)(2,1)} fusion(bf16[8,512,512]{2,1,0:T(8,128)(2,1)S(1)} %copy-done.3, s32[]{:T(128)S(6)} %select_n.23, bf16[2,512,8,512]{3,1,2,0:T(8,128)(2,1)} %convolution_convert_fusion), kind=kOutput, calls=%fused_computation.13 | convolution fusion | flops 2147745792 | bytes 11010052 | tf_op jit(solution)/shard_map/qpad,qbd->pab/dot_general | solution.py:34
  65.6 4.2 %collective-permute-start = (bf16[2,512,256]{2,1,0:T(8,128)(2,1)}, bf16[2,512,256]{2,1,0:T(8,128)(2,1)S(1)}, u32[]{:S(2)}, u32[]{:S(2)}) collective-permute-start(bf16[2,512,256]{2,1,0:T(8,128)(2,1)} %fusion.24), channel_id=1, source_target_pairs={{0,1},{1,0},{2,3},{3,2},{4,5},{5,4},{6,7},{7,6},{8,9},{9,8},{10,11... | collective-permute-start | bytes 1572872 | tf_op jit(solution)/shard_map/ppermute | solution.py:35
  69.8 0.0 copy-done.2
  69.8 0.2 fusion.32
  70.0 0.0 copy-done.1
  70.0 0.1 dynamic_slice.15
  70.1 0.1 broadcast_add_fusion
  70.3 0.0 all-to-all-done
  70.3 0.1 convert_bitcast_fusion
  70.4 0.2 copy.18
  70.6 0.4 reshape.72
  71.0 23.9 %collective-permute-done = bf16[2,512,256]{2,1,0:T(8,128)(2,1)S(1)} collective-permute-done((bf16[2,512,256]{2,1,0:T(8,128)(2,1)}, bf16[2,512,256]{2,1,0:T(8,128)(2,1)S(1)}, u32[]{:S(2)}, u32[]{:S(2)}) %collective-permute-start) | collective-permute-done | bytes 524320 | tf_op jit(solution)/shard_map/ppermute | solution.py:35
  94.8 7.4 %subtract_divide_fusion = f32[2,512,256]{2,1,0:T(8,128)} fusion(bf16[2,512,256]{2,1,0:T(8,128)(2,1)S(1)} %collective-permute-done, f32[2]{0:T(128)S(1)} %fusion.32, f32[512,256]{1,0:T(8,128)S(1)} %broadcast_add_fusion, f32[2,512,256]{2,1,0:T(8,128)S(1)} %reshape.72, bf16[8,512,512]{2,1,0:T(8,128)(2,1)} %param.8, s32[]{:T(128)S(6)} %select_n.22, ...), kind=kOutput, calls=%fused_computation.17 | convolution fusion | flops 2148794368 | bytes 13631500 | tf_op jit(solution)/shard_map/qpad,qbd->pab/dot_general | solution.py:36
  (1 shorter events, 0.0 us)
Async XLA Ops:
  0.0 14.3 %copy-start = (bf16[256,256]{1,0:T(8,128)(2,1)S(1)}, bf16[256,256]{1,0:T(8,128)(2,1)}, u32[]{:S(2)}) copy-start(bf16[256,256]{1,0:T(8,128)(2,1)} %param.7) | copy-start | bytes 393220
  0.0 15.8 %copy-start.4 = (s32[2]{0:T(128)S(1)}, s32[2]{0:T(128)}, u32[]{:S(2)}) copy-start(s32[2]{0:T(128)} %param.9) | copy-start | bytes 28
  0.0 38.2 %all-to-all-start.1 = ((bf16[256,4,512]{2,1,0:T(4,128)(2,1)}), bf16[256,4,512]{2,1,0:T(4,128)(2,1)S(1)}, u32[]{:S(2)}, u32[]{:S(2)}) async-start(bf16[256,4,512]{2,1,0:T(4,128)(2,1)} %param.6), calls=%async_computation.1 | async-start | bytes 2097152 | tf_op jit(solution)/shard_map/all_to_all | solution.py:27
  38.2 32.0 %all-to-all-start = ((bf16[256,4,256]{2,1,0:T(4,128)(2,1)}), bf16[256,4,256]{2,1,0:T(4,128)(2,1)S(1)}, u32[]{:S(2)}, u32[]{:S(2)}) async-start(bf16[256,4,256]{2,1,0:T(4,128)(2,1)} %copy.17), calls=%async_computation | async-start | bytes 1048576 | tf_op jit(solution)/shard_map/all_to_all | solution.py:28
  49.9 9.2 %copy-start.3 = (bf16[8,512,512]{2,1,0:T(8,128)(2,1)S(1)}, bf16[8,512,512]{2,1,0:T(8,128)(2,1)}, u32[]{:S(2)}) copy-start(bf16[8,512,512]{2,1,0:T(8,128)(2,1)} %param.8) | copy-start | bytes 12582916
  59.0 10.8 %copy-start.2 = (f32[16]{0:T(128)S(1)}, f32[16]{0:T(128)}, u32[]{:S(2)}) copy-start(f32[16]{0:T(128)} %param.10) | copy-start | bytes 196
  59.0 11.0 %copy-start.1 = (f32[512]{0:T(512)S(1)}, f32[512]{0:T(512)}, u32[]{:S(2)}) copy-start(f32[512]{0:T(512)} %param.11) | copy-start | bytes 6148
  65.6 29.2 %collective-permute-start = (bf16[2,512,256]{2,1,0:T(8,128)(2,1)}, bf16[2,512,256]{2,1,0:T(8,128)(2,1)S(1)}, u32[]{:S(2)}, u32[]{:S(2)}) collective-permute-start(bf16[2,512,256]{2,1,0:T(8,128)(2,1)} %fusion.24), channel_id=1, source_target_pairs={{0,1},{1,0},{2,3},{3,2},{4,5},{5,4},{6,7},{7,6},{8,9},{9,8},{10,11... | collective-permute-start | bytes 1572872 | tf_op jit(solution)/shard_map/ppermute | solution.py:35

commit v2 on v1

v2 whole, which is shorter than its diff:
```python
import jax
import jax.numpy as jnp
from jax import lax
from jax.experimental import pallas as pl
from jax.experimental.pallas import tpu as pltpu
from jax.sharding import Mesh, PartitionSpec as P

NO = 16
AXES = ("x", "y", "z", "core", "aux")
PAIR = AXES[:4]
VMEM_LIMIT = 24 * 1024 * 1024
NT = (((1,), (1,)), ((), ()))


def add_vector(vector, cols, amps_ref, total_ref):
    turned = [
        lax.dot_general(amps_ref[p], cols, NT, preferred_element_type=jnp.float32).astype(jnp.bfloat16)
        for p in range(amps_ref.shape[0])
    ]
    total_ref[...] += jnp.dot(
        vector, jnp.concatenate(turned, axis=1), preferred_element_type=jnp.float32
    )


def own_kernel(place_ref, amps_ref, vec_ref, total_ref):
    half = total_ref.shape[1] // 2

    @pl.when(pl.program_id(0) == 0)
    def _():
        total_ref[...] = jnp.zeros_like(total_ref)

    start = pl.multiple_of(place_ref[0] * half, half)
    add_vector(vec_ref[0], vec_ref[0, pl.ds(start, half), :], amps_ref, total_ref)


def own_vectors(place, amps, cholesky):
    nq, nv, _ = cholesky.shape
    return pl.pallas_call(
        own_kernel,
        grid_spec=pltpu.PrefetchScalarGridSpec(
            num_scalar_prefetch=1,
            grid=(nq,),
            in_specs=[
                pl.BlockSpec(amps.shape, lambda q, _: (0, 0, 0)),
                pl.BlockSpec((1, nv, nv), lambda q, _: (q, 0, 0)),
            ],
            out_specs=pl.BlockSpec((nv, nv), lambda q, _: (0, 0)),
        ),
        out_shape=jax.ShapeDtypeStruct((nv, nv), jnp.float32),
        compiler_params=pltpu.CompilerParams(vmem_limit_bytes=VMEM_LIMIT),
        cost_estimate=pl.CostEstimate(
            flops=4 * nq * nv**3, bytes_accessed=2 * nq * nv * nv, transcendentals=0
        ),
        name="own_vectors",
    )(place, amps, cholesky)


def other_kernel(
    place_ref, occ_ref, amps_ref, near0, far0, near1, far1, base_ref, hole_ref, rows_ref, cols_ref, out_ref, vec, total, sems
):
    nq, slots, strip, nv = vec.shape
    half = nv // 2
    core, first = place_ref[1], (place_ref[2], place_ref[3])
    part = nq // 2

    for h, sources in enumerate(((near0, far0), (near1, far1))):
        for side, src in enumerate(sources):
            base = (core if side == 0 else 1 - core) * (slots // 2)
            for outer in range(4):
                for inner in range(4):
                    dx, dy = (inner, outer) if h == 0 else (outer, inner)
                    x = lax.rem(first[0] + 4 - dx, 4)
                    y = lax.rem(first[1] + 4 - dy, 4)
                    pltpu.make_async_copy(
                        src.at[outer, inner],
                        vec.at[pl.ds(h * part, part), base + x * 4 + y],
                        sems.at[h],
                    ).start()
    total[...] = base_ref[...]
    for q in range(nq):
        if q % part == 0:
            block = vec.at[pl.ds(q, part)]
            pltpu.make_async_copy(block, block, sems.at[q // part]).wait()
        cols = vec[q, pl.ds(place_ref[0] * (slots // 2), slots // 2)].reshape(half, nv)
        add_vector(vec[q].reshape(nv, nv), cols, amps_ref, total)
    level = rows_ref[...] + cols_ref[...]
    for p in range(out_ref.shape[0]):
        value = hole_ref[p].astype(jnp.float32) + total[:, p * half : (p + 1) * half]
        out_ref[p] = value / (level - occ_ref[p])


def other_vectors(place, occ_sum, amps, gathered, base, hole, rows, cols):
    part, strip, nv = gathered[0].shape[2:]
    nq = 2 * part
    vmem = pl.BlockSpec(memory_space=pltpu.VMEM)
    smem = pl.BlockSpec(memory_space=pltpu.SMEM)
    anywhere = pl.BlockSpec(memory_space=pl.ANY)
    return pl.pallas_call(
        other_kernel,
        in_specs=[smem, smem, vmem, *[anywhere] * 4, vmem, vmem, vmem, vmem],
        out_specs=vmem,
        out_shape=jax.ShapeDtypeStruct(hole.shape, jnp.float32),
        scratch_shapes=[
            pltpu.VMEM((nq, nv // strip, strip, nv), jnp.bfloat16),
            pltpu.VMEM((nv, nv), jnp.float32),
            pltpu.SemaphoreType.DMA((2,)),
        ],
        compiler_params=pltpu.CompilerParams(vmem_limit_bytes=VMEM_LIMIT),
        cost_estimate=pl.CostEstimate(
            flops=4 * nq * nv**3, bytes_accessed=2 * nq * nv * nv, transcendentals=0
        ),
        name="other_vectors",
    )(place, occ_sum, amps, *gathered, base, hole, rows, cols)


def gather_axis(block, axis):
    return jnp.stack(
        [block] + [lax.ppermute(block, axis, [(i, (i + d) % 4) for i in range(4)]) for d in (1, 2, 3)]
    )


def shards(amplitudes, ladder, cholesky, pair_ids, occ_energy, vir_energy):
    rows, n_virt = amplitudes.shape[1:]
    half_width = n_virt // lax.axis_size("aux")
    aux_index, core = lax.axis_index("aux"), lax.axis_index("core")
    planes = lax.axis_size("x") * lax.axis_size("y")
    strip = half_width // planes
    mine = aux_index * half_width

    slot = core * planes + lax.axis_index("x") * lax.axis_size("y") + lax.axis_index("y")
    piece = lax.dynamic_slice_in_dim(cholesky, slot * strip, strip, 1)
    piece = lax.ppermute(piece, "aux", [(0, 1), (1, 0)])
    gathered = []
    part = piece.shape[0] // 2
    for h, order in enumerate((("x", "y"), ("y", "x"))):
        near = piece[h * part : (h + 1) * part]
        for axis in order:
            near = gather_axis(near, axis)
        gathered += [near, lax.ppermute(near, "core", [(0, 1), (1, 0)])]

    amp_half = lax.dynamic_slice_in_dim(amplitudes, mine, half_width, 2)
    hole_half = jnp.dot(
        ladder, amp_half.reshape(amp_half.shape[0], -1), preferred_element_type=jnp.float32
    ).astype(jnp.bfloat16).reshape(-1, rows, half_width)
    both = jnp.concatenate([amplitudes, hole_half], axis=2)
    both = lax.all_to_all(both, PAIR, split_axis=0, concat_axis=1, tiled=True)
    pair_amps, pair_hole = both[:, :, :n_virt], both[:, :, n_virt:]

    orbitals = jnp.arange(NO, dtype=jnp.int32)
    first_hot = (pair_ids[:, None] // NO == orbitals[None, :]).astype(jnp.float32)
    second_hot = (pair_ids[:, None] % NO == orbitals[None, :]).astype(jnp.float32)
    occ_sum = jnp.sum((first_hot + second_hot) * occ_energy[None, :], axis=1)
    vir_cols = lax.dynamic_slice_in_dim(vir_energy, mine, half_width, 0)
    place = jnp.stack([aux_index, core, lax.axis_index("x"), lax.axis_index("y")]).astype(jnp.int32)

    base = own_vectors(place, pair_amps, cholesky)
    return other_vectors(
        place, occ_sum, pair_amps, gathered, base, pair_hole, vir_energy[:, None], vir_cols[None, :]
    )


def solution(mesh):
    fine = Mesh(mesh.devices.reshape(4, 4, 4, 2, 2), AXES)
    in_specs = (P(None, PAIR, None), P(), P("aux", None, None), P(PAIR), P(), P())
    out_specs = P(PAIR, None, "aux")
    return jax.shard_map(shards, mesh=fine, in_specs=in_specs, out_specs=out_specs, check_vma=False)
```

time: 103 us -> 118 us (1.15)
  the two profiles are of different devices: /device:TPU:71 before, /device:TPU:1 now
where the time goes in v2:
time: 118 us; the launch traced here: 117 us
  starting transfers between devices  43.6 us (37%)
  waiting for transfers between devices  40.2 us (34%)
  Pallas kernels  15.3 us (13%)
  local copies, waits for them, and re-layouts  14.6 us (12%)
  other arithmetic  2.49 us (2%)
    ppermute x1, waiting for transfers between devices, shards(): piece = lax.ppermute(piece, 'aux', [(0, 1), (1, 0)])  29.2 us
    ppermute x12, starting transfers between devices, gather_axis(): lax.ppermute(block, axis, [(i, (i + d) % 4) for i in range(4)])  19.3 us
    all_to_all x1, starting transfers between devices, shards(): both = lax.all_to_all(both, PAIR, split_axis=0, concat_axis=1, tiled=True)  14.2 us
    ppermute x12, waiting for transfers between devices, gather_axis(): lax.ppermute(block, axis, [(i, (i + d) % 4) for i in range(4)])  11 us
    pallas_call x1, Pallas kernels, other_vectors(): pl.pallas_call(other_kernel, in_specs=[smem, smem, vmem, *[anywhere] * 4,...  8.01 us
    pallas_call x1, Pallas kernels, own_vectors(): pl.pallas_call(own_kernel, grid_spec=pltpu.PrefetchScalarGridSpec(num_sca...  7.25 us
    all_to_all x2, local copies, waits for them, and re-layouts, shards(): both = lax.all_to_all(both, PAIR, split_axis=0, concat_axis=1, tiled=True)  6.81 us
    ppermute x2, starting transfers between devices, shards(): gathered += [near, lax.ppermute(near, 'core', [(0, 1), (1, 0)])]  5.78 us
  transfers between devices with their start and end apart: 16, of which 6 were waited for; matrix products, arithmetic and copies ran while one was open for 6% of the time, Pallas kernels for 6%

profile of v2, /device:TPU:1, one launch (start us, length us, event | category | flops | bytes accessed | tf_op | source)
XLA Modules:
  0.0 117.0 jit_solution(2974116523929532842)
XLA Ops:
  0.0 1.3 %constant_dynamic-slice_fusion.1 = bf16[256,4,256]{2,1,0:T(4,128)(2,1)S(1)} fusion(bf16[256,4,512]{2,1,0:T(4,128)(2,1)} %param.6, s32[]{:T(128)S(6)} %select_n.23), kind=kLoop, calls=%fused_computation.19 | loop fusion | bytes 1048580 | tf_op jit(solution)/shard_map/dynamic_slice | solution.py:141
  1.4 0.4 convolution_convert_fusion
  1.7 0.3 copy.12
  2.0 0.4 copy-done.2
  2.5 1.9 %pad_maximum_fusion = bf16[256,4,768]{2,1,0:T(4,128)(2,1)} fusion(bf16[256,4,256]{2,1,0:T(4,128)(2,1)S(1)} %copy.12, bf16[256,4,512]{2,1,0:T(4,128)(2,1)S(1)} %copy-done.2), kind=kLoop, calls=%fused_computation | loop fusion | flops 3145728 | bytes 3145728 | tf_op jit(solution)/shard_map/concatenate | solution.py:145
  4.3 14.2 %all-to-all-start = ((bf16[256,4,768]{2,1,0:T(4,128)(2,1)}), bf16[256,4,768]{2,1,0:T(4,128)(2,1)}, u32[]{:S(2)}, u32[]{:S(2)}) async-start(bf16[256,4,768]{2,1,0:T(4,128)(2,1)} %pad_maximum_fusion), calls=%async_computation | async-start | bytes 3145728 | tf_op jit(solution)/shard_map/all_to_all | solution.py:146
  18.6 0.9 constant_dynamic-slice_fusion
  19.5 4.3 %collective-permute-start = (bf16[8,16,512]{2,1,0:T(8,128)(2,1)S(1)}, bf16[8,16,512]{2,1,0:T(8,128)(2,1)S(1)}, u32[]{:S(2)}, u32[]{:S(2)}) collective-permute-start(bf16[8,16,512]{2,1,0:T(8,128)(2,1)S(1)} %constant_dynamic-slice_fusion), channel_id=1, source_target_pairs={{0,1},{1,0},{2,3},{3,2},{4,5},{5,4},{6,7},{7,6},{8,9},{9,8},{10,11... | collective-permute-start | bytes 393224 | tf_op jit(solution)/shard_map/ppermute | solution.py:132
  23.8 29.2 %collective-permute-done = bf16[8,16,512]{2,1,0:T(8,128)(2,1)S(1)} collective-permute-done((bf16[8,16,512]{2,1,0:T(8,128)(2,1)S(1)}, bf16[8,16,512]{2,1,0:T(8,128)(2,1)S(1)}, u32[]{:S(2)}, u32[]{:S(2)}) %collective-permute-start) | collective-permute-done | bytes 131104 | tf_op jit(solution)/shard_map/ppermute | solution.py:132
  53.1 3.7 %collective-permute-start.2 = (bf16[4,16,512]{2,1,0:T(8,128)(2,1)S(1)}, bf16[4,16,512]{2,1,0:T(8,128)(2,1)S(1)}, u32[]{:S(2)}, u32[]{:S(2)}) collective-permute-start(bf16[4,16,512]{2,1,0:T(8,128)(2,1)S(1)} %get-tuple-element.12), channel_id=1, source_target_pairs={{0,128},{64,192},{128,0},{192,64},{1,129},{65,193},{129,1},{193,65... | collective-permute-start | bytes 196616 | tf_op jit(solution)/shard_map/ppermute | solution.py:118
  56.7 0.5 collective-permute-start.1
  57.2 2.2 %collective-permute-start.3 = (bf16[4,16,512]{2,1,0:T(8,128)(2,1)S(1)}, bf16[4,16,512]{2,1,0:T(8,128)(2,1)S(1)}, u32[]{:S(2)}, u32[]{:S(2)}) collective-permute-start(bf16[4,16,512]{2,1,0:T(8,128)(2,1)S(1)} %get-tuple-element.12), channel_id=1, source_target_pairs={{0,192},{64,0},{128,64},{192,128},{1,193},{65,1},{129,65},{193,129... | collective-permute-start | bytes 196616 | tf_op jit(solution)/shard_map/ppermute | solution.py:118
  59.4 2.2 %collective-permute-done.1 = bf16[4,16,512]{2,1,0:T(8,128)(2,1)S(1)} collective-permute-done((bf16[4,16,512]{2,1,0:T(8,128)(2,1)S(1)}, bf16[4,16,512]{2,1,0:T(8,128)(2,1)S(1)}, u32[]{:S(2)}, u32[]{:S(2)}) %collective-permute-start.1) | collective-permute-done | bytes 65568 | tf_op jit(solution)/shard_map/ppermute | solution.py:118
  61.8 2.8 %collective-permute-start.5 = (bf16[4,4,16,512]{3,2,1,0:T(8,128)(2,1)S(1)}, bf16[4,4,16,512]{3,2,1,0:T(8,128)(2,1)S(1)}, u32[]{:S(2)}, u32[]{:S(2)}) collective-permute-start(bf16[4,4,16,512]{3,2,1,0:T(8,128)(2,1)S(1)} %get-tuple-element.8), channel_id=1, source_target_pairs={{0,32},{16,48},{32,0},{48,16},{1,33},{17,49},{33,1},{49,17},{2,34}... | collective-permute-start | bytes 786440 | tf_op jit(solution)/shard_map/ppermute | solution.py:118
  64.8 1.2 collective-permute-start.8
  66.0 1.5 %collective-permute-start.10 = (bf16[4,16,512]{2,1,0:T(8,128)(2,1)S(1)}, bf16[4,16,512]{2,1,0:T(8,128)(2,1)S(1)}, u32[]{:S(2)}, u32[]{:S(2)}) collective-permute-start(bf16[4,16,512]{2,1,0:T(8,128)(2,1)S(1)} %get-tuple-element.11), channel_id=1, source_target_pairs={{0,48},{16,0},{32,16},{48,32},{1,49},{17,1},{33,17},{49,33},{2,50}... | collective-permute-start | bytes 196616 | tf_op jit(solution)/shard_map/ppermute | solution.py:118
  67.5 3.3 %collective-permute-done.9 = bf16[4,16,512]{2,1,0:T(8,128)(2,1)S(1)} collective-permute-done((bf16[4,16,512]{2,1,0:T(8,128)(2,1)S(1)}, bf16[4,16,512]{2,1,0:T(8,128)(2,1)S(1)}, u32[]{:S(2)}, u32[]{:S(2)}) %collective-permute-start.9) | collective-permute-done | bytes 65568 | tf_op jit(solution)/shard_map/ppermute | solution.py:118
  70.8 2.6 %collective-permute-start.6 = (bf16[4,4,16,512]{3,2,1,0:T(8,128)(2,1)S(1)}, bf16[4,4,16,512]{3,2,1,0:T(8,128)(2,1)S(1)}, u32[]{:S(2)}, u32[]{:S(2)}) collective-permute-start(bf16[4,4,16,512]{3,2,1,0:T(8,128)(2,1)S(1)} %get-tuple-element.8), channel_id=1, source_target_pairs={{0,48},{16,0},{32,16},{48,32},{1,49},{17,1},{33,17},{49,33},{2,50}... | collective-permute-start | bytes 786440 | tf_op jit(solution)/shard_map/ppermute | solution.py:118
  73.4 1.6 %collective-permute-start.12 = (bf16[4,4,16,512]{3,2,1,0:T(8,128)(2,1)S(1)}, bf16[4,4,16,512]{3,2,1,0:T(8,128)(2,1)S(1)}, u32[]{:S(2)}, u32[]{:S(2)}) collective-permute-start(bf16[4,4,16,512]{3,2,1,0:T(8,128)(2,1)S(1)} %get-tuple-element.6), channel_id=1, source_target_pairs={{0,128},{64,192},{128,0},{192,64},{1,129},{65,193},{129,1},{193,65... | collective-permute-start | bytes 786440 | tf_op jit(solution)/shard_map/ppermute | solution.py:118
  75.1 0.7 collective-permute-start.11
  75.8 2.3 %collective-permute-start.13 = (bf16[4,4,16,512]{3,2,1,0:T(8,128)(2,1)S(1)}, bf16[4,4,16,512]{3,2,1,0:T(8,128)(2,1)S(1)}, u32[]{:S(2)}, u32[]{:S(2)}) collective-permute-start(bf16[4,4,16,512]{3,2,1,0:T(8,128)(2,1)S(1)} %get-tuple-element.6), channel_id=1, source_target_pairs={{0,192},{64,0},{128,64},{192,128},{1,193},{65,1},{129,65},{193,129... | collective-permute-start | bytes 786440 | tf_op jit(solution)/shard_map/ppermute | solution.py:118
  78.1 1.3 %collective-permute-done.4 = bf16[4,4,16,512]{3,2,1,0:T(8,128)(2,1)S(1)} collective-permute-done((bf16[4,4,16,512]{3,2,1,0:T(8,128)(2,1)S(1)}, bf16[4,4,16,512]{3,2,1,0:T(8,128)(2,1)S(1)}, u32[]{:S(2)}, u32[]{:S(2)}) %collective-permute-start.4) | collective-permute-done | bytes 262176 | tf_op jit(solution)/shard_map/ppermute | solution.py:118
  79.6 2.9 %collective-permute-start.7 = (bf16[4,4,4,16,512]{4,3,2,1,0:T(8,128)(2,1)S(1)}, bf16[4,4,4,16,512]{4,3,2,1,0:T(8,128)(2,1)S(1)}, u32[]{:S(2)}, u32[]{:S(2)}) collective-permute-start(bf16[4,4,4,16,512]{4,3,2,1,0:T(8,128)(2,1)S(1)} %pad_maximum_fusion.1.near0), channel_id=1, source_target_pairs={{0,2},{2,0},{1,3},{3,1},{4,6},{6,4},{5,7},{7,5},{8,10},{10,8},{9,1... | collective-permute-start | bytes 3145736 | tf_op jit(solution)/shard_map/ppermute | solution.py:139
  82.5 4.1 %collective-permute-done.11 = bf16[4,4,16,512]{3,2,1,0:T(8,128)(2,1)S(1)} collective-permute-done((bf16[4,4,16,512]{3,2,1,0:T(8,128)(2,1)S(1)}, bf16[4,4,16,512]{3,2,1,0:T(8,128)(2,1)S(1)}, u32[]{:S(2)}, u32[]{:S(2)}) %collective-permute-start.11) | collective-permute-done | bytes 262176 | tf_op jit(solution)/shard_map/ppermute | solution.py:118
  86.7 2.9 %collective-permute-start.14 = (bf16[4,4,4,16,512]{4,3,2,1,0:T(8,128)(2,1)S(1)}, bf16[4,4,4,16,512]{4,3,2,1,0:T(8,128)(2,1)}, u32[]{:S(2)}, u32[]{:S(2)}) collective-permute-start(bf16[4,4,4,16,512]{4,3,2,1,0:T(8,128)(2,1)S(1)} %pad_maximum_fusion.2.near1), channel_id=1, source_target_pairs={{0,2},{2,0},{1,3},{3,1},{4,6},{6,4},{5,7},{7,5},{8,10},{10,8},{9,1... | collective-permute-start | bytes 3145736 | tf_op jit(solution)/shard_map/ppermute | solution.py:139
  90.1 3.1 %copy.17 = bf16[128,2,4,768]{3,2,0,1:T(4,128)(2,1)} copy(bf16[128,2,4,768]{3,2,1,0:T(4,128)(2,1)} %bitcast.6) | data formatting | bytes 3145728 | tf_op jit(solution)/shard_map/all_to_all | solution.py:146
  93.2 3.7 %all_to_all.16 = bf16[2,512,768]{2,1,0:T(8,128)(2,1)} reshape(bf16[2,128,4,768]{3,2,1,0:T(4,128)(2,1)} %bitcast.38) | data formatting | bytes 3145728 | tf_op jit(solution)/shard_map/all_to_all | solution.py:146
  96.9 1.1 slice.19.hole_ref
  98.0 1.3 %slice.16.amps_ref = bf16[2,512,512]{2,1,0:T(8,128)(2,1)S(1)} slice(bf16[2,512,768]{2,1,0:T(8,128)(2,1)} %all_to_all.16), slice={[0:2], [0:512], [0:512]} | slice | bytes 2097152 | tf_op jit(solution)/shard_map/slice | solution.py:147
  99.3 2.2 %copy-done.1 = bf16[8,512,512]{2,1,0:T(8,128)(2,1)S(1)} copy-done((bf16[8,512,512]{2,1,0:T(8,128)(2,1)S(1)}, bf16[8,512,512]{2,1,0:T(8,128)(2,1)}, u32[]{:S(2)}) %copy-start.1) | copy-done | bytes 4194328
  101.5 7.2 %own_vectors.1.base_ref = f32[512,512]{1,0:T(8,128)S(1)} custom-call(s32[4]{0:T(128)S(1)} %pad_add_fusion.place_ref, bf16[2,512,512]{2,1,0:T(8,128)(2,1)S(1)} %slice.16.amps_ref, bf16[8,512,512]{2,1,0:T(8,128)(2,1)S(1)} %copy-done.1), custom_call_target="tpu_custom_call" | custom-call | flops 4294967296 | bytes 4194304 | tf_op jit(solution)/shard_map/own_vectors/pallas_call | solution.py:38
  108.8 8.0 %other_vectors.1 = f32[2,512,256]{2,1,0:T(8,128)} custom-call(s32[4]{0:T(128)S(1)} %pad_add_fusion.place_ref, f32[2]{0:T(128)S(1)} %fusion.2.occ_ref, bf16[2,512,512]{2,1,0:T(8,128)(2,1)S(1)} %slice.16.amps_ref, bf16[4,4,4,16,512]{4,3,2,1,0:T(8,128)(2,1)S(1)} %pad_maximum_fusion.1.near0, bf16[4,4,4,16,512]{4,3,2,1,0:T(8,128)(2,1)S(1)} %collective-permute-done.7.far0, ...), custom_call_target="tpu_custom_call" | custom-call | flops 4294967296 | bytes 4194304 | tf_op jit(solution)/shard_map/other_vectors/pallas_call | solution.py:98
  (34 shorter events, 1.3 us)
Async XLA Ops:
  0.0 1.4 %copy-start = (bf16[256,256]{1,0:T(8,128)(2,1)S(1)}, bf16[256,256]{1,0:T(8,128)(2,1)}, u32[]{:S(2)}) copy-start(bf16[256,256]{1,0:T(8,128)(2,1)} %param.7) | copy-start | bytes 393220
  1.3 1.2 %copy-start.2 = (bf16[256,4,512]{2,1,0:T(4,128)(2,1)S(1)}, bf16[256,4,512]{2,1,0:T(4,128)(2,1)}, u32[]{:S(2)}) copy-start(bf16[256,4,512]{2,1,0:T(4,128)(2,1)} %param.6) | copy-start | bytes 3145732
  4.3 85.8 %all-to-all-start = ((bf16[256,4,768]{2,1,0:T(4,128)(2,1)}), bf16[256,4,768]{2,1,0:T(4,128)(2,1)}, u32[]{:S(2)}, u32[]{:S(2)}) async-start(bf16[256,4,768]{2,1,0:T(4,128)(2,1)} %pad_maximum_fusion), calls=%async_computation | async-start | bytes 3145728 | tf_op jit(solution)/shard_map/all_to_all | solution.py:146
  19.5 33.5 %collective-permute-start = (bf16[8,16,512]{2,1,0:T(8,128)(2,1)S(1)}, bf16[8,16,512]{2,1,0:T(8,128)(2,1)S(1)}, u32[]{:S(2)}, u32[]{:S(2)}) collective-permute-start(bf16[8,16,512]{2,1,0:T(8,128)(2,1)S(1)} %constant_dynamic-slice_fusion), channel_id=1, source_target_pairs={{0,1},{1,0},{2,3},{3,2},{4,5},{5,4},{6,7},{7,6},{8,9},{9,8},{10,11... | collective-permute-start | bytes 393224 | tf_op jit(solution)/shard_map/ppermute | solution.py:132
  53.1 6.3 %collective-permute-start.2 = (bf16[4,16,512]{2,1,0:T(8,128)(2,1)S(1)}, bf16[4,16,512]{2,1,0:T(8,128)(2,1)S(1)}, u32[]{:S(2)}, u32[]{:S(2)}) collective-permute-start(bf16[4,16,512]{2,1,0:T(8,128)(2,1)S(1)} %get-tuple-element.12), channel_id=1, source_target_pairs={{0,128},{64,192},{128,0},{192,64},{1,129},{65,193},{129,1},{193,65... | collective-permute-start | bytes 196616 | tf_op jit(solution)/shard_map/ppermute | solution.py:118
  56.7 4.9 %collective-permute-start.1 = (bf16[4,16,512]{2,1,0:T(8,128)(2,1)S(1)}, bf16[4,16,512]{2,1,0:T(8,128)(2,1)S(1)}, u32[]{:S(2)}, u32[]{:S(2)}) collective-permute-start(bf16[4,16,512]{2,1,0:T(8,128)(2,1)S(1)} %get-tuple-element.12), channel_id=1, source_target_pairs={{0,64},{64,128},{128,192},{192,0},{1,65},{65,129},{129,193},{193,1... | collective-permute-start | bytes 196616 | tf_op jit(solution)/shard_map/ppermute | solution.py:118
  57.2 4.5 %collective-permute-start.3 = (bf16[4,16,512]{2,1,0:T(8,128)(2,1)S(1)}, bf16[4,16,512]{2,1,0:T(8,128)(2,1)S(1)}, u32[]{:S(2)}, u32[]{:S(2)}) collective-permute-start(bf16[4,16,512]{2,1,0:T(8,128)(2,1)S(1)} %get-tuple-element.12), channel_id=1, source_target_pairs={{0,192},{64,0},{128,64},{192,128},{1,193},{65,1},{129,65},{193,129... | collective-permute-start | bytes 196616 | tf_op jit(solution)/shard_map/ppermute | solution.py:118
  61.8 14.0 %collective-permute-start.5 = (bf16[4,4,16,512]{3,2,1,0:T(8,128)(2,1)S(1)}, bf16[4,4,16,512]{3,2,1,0:T(8,128)(2,1)S(1)}, u32[]{:S(2)}, u32[]{:S(2)}) collective-permute-start(bf16[4,4,16,512]{3,2,1,0:T(8,128)(2,1)S(1)} %get-tuple-element.8), channel_id=1, source_target_pairs={{0,32},{16,48},{32,0},{48,16},{1,33},{17,49},{33,1},{49,17},{2,34}... | collective-permute-start | bytes 786440 | tf_op jit(solution)/shard_map/ppermute | solution.py:118
  64.6 6.2 %collective-permute-start.9 = (bf16[4,16,512]{2,1,0:T(8,128)(2,1)S(1)}, bf16[4,16,512]{2,1,0:T(8,128)(2,1)S(1)}, u32[]{:S(2)}, u32[]{:S(2)}) collective-permute-start(bf16[4,16,512]{2,1,0:T(8,128)(2,1)S(1)} %get-tuple-element.11), channel_id=1, source_target_pairs={{0,32},{16,48},{32,0},{48,16},{1,33},{17,49},{33,1},{49,17},{2,34}... | collective-permute-start | bytes 196616 | tf_op jit(solution)/shard_map/ppermute | solution.py:118
  64.8 8.6 %collective-permute-start.8 = (bf16[4,16,512]{2,1,0:T(8,128)(2,1)S(1)}, bf16[4,16,512]{2,1,0:T(8,128)(2,1)S(1)}, u32[]{:S(2)}, u32[]{:S(2)}) collective-permute-start(bf16[4,16,512]{2,1,0:T(8,128)(2,1)S(1)} %get-tuple-element.11), channel_id=1, source_target_pairs={{0,16},{16,32},{32,48},{48,0},{1,17},{17,33},{33,49},{49,1},{2,18}... | collective-permute-start | bytes 196616 | tf_op jit(solution)/shard_map/ppermute | solution.py:118
  66.0 7.4 %collective-permute-start.10 = (bf16[4,16,512]{2,1,0:T(8,128)(2,1)S(1)}, bf16[4,16,512]{2,1,0:T(8,128)(2,1)S(1)}, u32[]{:S(2)}, u32[]{:S(2)}) collective-permute-start(bf16[4,16,512]{2,1,0:T(8,128)(2,1)S(1)} %get-tuple-element.11), channel_id=1, source_target_pairs={{0,48},{16,0},{32,16},{48,32},{1,49},{17,1},{33,17},{49,33},{2,50}... | collective-permute-start | bytes 196616 | tf_op jit(solution)/shard_map/ppermute | solution.py:118
  67.5 11.9 %collective-permute-start.4 = (bf16[4,4,16,512]{3,2,1,0:T(8,128)(2,1)S(1)}, bf16[4,4,16,512]{3,2,1,0:T(8,128)(2,1)S(1)}, u32[]{:S(2)}, u32[]{:S(2)}) collective-permute-start(bf16[4,4,16,512]{3,2,1,0:T(8,128)(2,1)S(1)} %get-tuple-element.8), channel_id=1, source_target_pairs={{0,16},{16,32},{32,48},{48,0},{1,17},{17,33},{33,49},{49,1},{2,18}... | collective-permute-start | bytes 786440 | tf_op jit(solution)/shard_map/ppermute | solution.py:118
  70.8 8.6 %collective-permute-start.6 = (bf16[4,4,16,512]{3,2,1,0:T(8,128)(2,1)S(1)}, bf16[4,4,16,512]{3,2,1,0:T(8,128)(2,1)S(1)}, u32[]{:S(2)}, u32[]{:S(2)}) collective-permute-start(bf16[4,4,16,512]{3,2,1,0:T(8,128)(2,1)S(1)} %get-tuple-element.8), channel_id=1, source_target_pairs={{0,48},{16,0},{32,16},{48,32},{1,49},{17,1},{33,17},{49,33},{2,50}... | collective-permute-start | bytes 786440 | tf_op jit(solution)/shard_map/ppermute | solution.py:118
  73.4 9.0 %collective-permute-start.12 = (bf16[4,4,16,512]{3,2,1,0:T(8,128)(2,1)S(1)}, bf16[4,4,16,512]{3,2,1,0:T(8,128)(2,1)S(1)}, u32[]{:S(2)}, u32[]{:S(2)}) collective-permute-start(bf16[4,4,16,512]{3,2,1,0:T(8,128)(2,1)S(1)} %get-tuple-element.6), channel_id=1, source_target_pairs={{0,128},{64,192},{128,0},{192,64},{1,129},{65,193},{129,1},{193,65... | collective-permute-start | bytes 786440 | tf_op jit(solution)/shard_map/ppermute | solution.py:118
  75.1 11.5 %collective-permute-start.11 = (bf16[4,4,16,512]{3,2,1,0:T(8,128)(2,1)S(1)}, bf16[4,4,16,512]{3,2,1,0:T(8,128)(2,1)S(1)}, u32[]{:S(2)}, u32[]{:S(2)}) collective-permute-start(bf16[4,4,16,512]{3,2,1,0:T(8,128)(2,1)S(1)} %get-tuple-element.6), channel_id=1, source_target_pairs={{0,64},{64,128},{128,192},{192,0},{1,65},{65,129},{129,193},{193,1... | collective-permute-start | bytes 786440 | tf_op jit(solution)/shard_map/ppermute | solution.py:118
  75.8 10.8 %collective-permute-start.13 = (bf16[4,4,16,512]{3,2,1,0:T(8,128)(2,1)S(1)}, bf16[4,4,16,512]{3,2,1,0:T(8,128)(2,1)S(1)}, u32[]{:S(2)}, u32[]{:S(2)}) collective-permute-start(bf16[4,4,16,512]{3,2,1,0:T(8,128)(2,1)S(1)} %get-tuple-element.6), channel_id=1, source_target_pairs={{0,192},{64,0},{128,64},{192,128},{1,193},{65,1},{129,65},{193,129... | collective-permute-start | bytes 786440 | tf_op jit(solution)/shard_map/ppermute | solution.py:118
  79.6 10.1 %copy-start.3 = (f32[512]{0:T(512)S(1)}, f32[512]{0:T(512)}, u32[]{:S(2)}) copy-start(f32[512]{0:T(512)} %param.11) | copy-start | bytes 6148
  79.6 10.4 %copy-start.5 = (s32[2]{0:T(128)S(1)}, s32[2]{0:T(128)}, u32[]{:S(2)}) copy-start(s32[2]{0:T(128)} %param.9) | copy-start | bytes 28
  79.6 10.4 %copy-start.4 = (f32[16]{0:T(128)S(1)}, f32[16]{0:T(128)}, u32[]{:S(2)}) copy-start(f32[16]{0:T(128)} %param.10) | copy-start | bytes 196
  79.6 29.2 %collective-permute-start.7 = (bf16[4,4,4,16,512]{4,3,2,1,0:T(8,128)(2,1)S(1)}, bf16[4,4,4,16,512]{4,3,2,1,0:T(8,128)(2,1)S(1)}, u32[]{:S(2)}, u32[]{:S(2)}) collective-permute-start(bf16[4,4,4,16,512]{4,3,2,1,0:T(8,128)(2,1)S(1)} %pad_maximum_fusion.1.near0), channel_id=1, source_target_pairs={{0,2},{2,0},{1,3},{3,1},{4,6},{6,4},{5,7},{7,5},{8,10},{10,8},{9,1... | collective-permute-start | bytes 3145736 | tf_op jit(solution)/shard_map/ppermute | solution.py:139
  86.7 22.1 %collective-permute-start.14 = (bf16[4,4,4,16,512]{4,3,2,1,0:T(8,128)(2,1)S(1)}, bf16[4,4,4,16,512]{4,3,2,1,0:T(8,128)(2,1)}, u32[]{:S(2)}, u32[]{:S(2)}) collective-permute-start(bf16[4,4,4,16,512]{4,3,2,1,0:T(8,128)(2,1)S(1)} %pad_maximum_fusion.2.near1), channel_id=1, source_target_pairs={{0,2},{2,0},{1,3},{3,1},{4,6},{6,4},{5,7},{7,5},{8,10},{10,8},{9,1... | collective-permute-start | bytes 3145736 | tf_op jit(solution)/shard_map/ppermute | solution.py:139
  99.3 2.2 %copy-start.1 = (bf16[8,512,512]{2,1,0:T(8,128)(2,1)S(1)}, bf16[8,512,512]{2,1,0:T(8,128)(2,1)}, u32[]{:S(2)}) copy-start(bf16[8,512,512]{2,1,0:T(8,128)(2,1)} %vec_ref.1) | copy-start | bytes 12582916

commit v3 on v2

--- a/solution.py
+++ b/solution.py
@@ -22,31 +22,31 @@
     )
 
 
-def own_kernel(place_ref, amps_ref, vec_ref, total_ref):
-    half = total_ref.shape[1] // 2
-
-    @pl.when(pl.program_id(0) == 0)
-    def _():
-        total_ref[...] = jnp.zeros_like(total_ref)
-
+def own_kernel(place_ref, amps_ref, vec_ref, total_ref, vec, sems):
+    nq, nv, _ = vec.shape
+    half = nv // 2
+    copies = [pltpu.make_async_copy(vec_ref.at[q], vec.at[q], sems.at[q]) for q in range(nq)]
+    for copy in copies:
+        copy.start()
+    total_ref[...] = jnp.zeros_like(total_ref)
     start = pl.multiple_of(place_ref[0] * half, half)
-    add_vector(vec_ref[0], vec_ref[0, pl.ds(start, half), :], amps_ref, total_ref)
+    for q in range(nq):
+        copies[q].wait()
+        add_vector(vec[q], vec[q, pl.ds(start, half), :], amps_ref, total_ref)
 
 
 def own_vectors(place, amps, cholesky):
     nq, nv, _ = cholesky.shape
     return pl.pallas_call(
         own_kernel,
-        grid_spec=pltpu.PrefetchScalarGridSpec(
-            num_scalar_prefetch=1,
-            grid=(nq,),
-            in_specs=[
-                pl.BlockSpec(amps.shape, lambda q, _: (0, 0, 0)),
-                pl.BlockSpec((1, nv, nv), lambda q, _: (q, 0, 0)),
-            ],
-            out_specs=pl.BlockSpec((nv, nv), lambda q, _: (0, 0)),
-        ),
+        in_specs=[
+            pl.BlockSpec(memory_space=pltpu.SMEM),
+            pl.BlockSpec(memory_space=pltpu.VMEM),
+            pl.BlockSpec(memory_space=pltpu.HBM),
+        ],
+        out_specs=pl.BlockSpec(memory_space=pltpu.VMEM),
         out_shape=jax.ShapeDtypeStruct((nv, nv), jnp.float32),
+        scratch_shapes=[pltpu.VMEM((nq, nv, nv), jnp.bfloat16), pltpu.SemaphoreType.DMA((nq,))],
         compiler_params=pltpu.CompilerParams(vmem_limit_bytes=VMEM_LIMIT),
         cost_estimate=pl.CostEstimate(
             flops=4 * nq * nv**3, bytes_accessed=2 * nq * nv * nv, transcendentals=0
@@ -85,8 +85,8 @@
         add_vector(vec[q].reshape(nv, nv), cols, amps_ref, total)
     level = rows_ref[...] + cols_ref[...]
     for p in range(out_ref.shape[0]):
-        value = hole_ref[p].astype(jnp.float32) + total[:, p * half : (p + 1) * half]
-        out_ref[p] = value / (level - occ_ref[p])
+        side = slice(p * half, (p + 1) * half)
+        out_ref[p] = (hole_ref[:, side].astype(jnp.float32) + total[:, side]) / (level - occ_ref[p])
 
 
 def other_vectors(place, occ_sum, amps, gathered, base, hole, rows, cols):
@@ -99,7 +99,7 @@
         other_kernel,
         in_specs=[smem, smem, vmem, *[anywhere] * 4, vmem, vmem, vmem, vmem],
         out_specs=vmem,
-        out_shape=jax.ShapeDtypeStruct(hole.shape, jnp.float32),
+        out_shape=jax.ShapeDtypeStruct((amps.shape[0], nv, nv // 2), jnp.float32),
         scratch_shapes=[
             pltpu.VMEM((nq, nv // strip, strip, nv), jnp.bfloat16),
             pltpu.VMEM((nv, nv), jnp.float32),
@@ -120,16 +120,30 @@
 
 
 def shards(amplitudes, ladder, cholesky, pair_ids, occ_energy, vir_energy):
-    rows, n_virt = amplitudes.shape[1:]
+    n_pair, rows, n_virt = amplitudes.shape
     half_width = n_virt // lax.axis_size("aux")
     aux_index, core = lax.axis_index("aux"), lax.axis_index("core")
     planes = lax.axis_size("x") * lax.axis_size("y")
     strip = half_width // planes
     mine = aux_index * half_width
+    each = pair_ids.shape[0]
+    peers = n_pair // each
 
     slot = core * planes + lax.axis_index("x") * lax.axis_size("y") + lax.axis_index("y")
     piece = lax.dynamic_slice_in_dim(cholesky, slot * strip, strip, 1)
     piece = lax.ppermute(piece, "aux", [(0, 1), (1, 0)])
+
+    amp_half = lax.dynamic_slice_in_dim(amplitudes, mine, half_width, 2)
+    hole_half = jnp.dot(
+        ladder, amp_half.reshape(n_pair, -1), preferred_element_type=jnp.float32
+    ).astype(jnp.bfloat16)
+    hole_half = hole_half.reshape(peers, each, rows, half_width).transpose(0, 2, 1, 3)
+    both = jnp.concatenate(
+        [amplitudes.reshape(peers, each, rows, n_virt), hole_half.reshape(peers, 1, rows, n_virt)], axis=1
+    )
+    both, piece = lax.optimization_barrier((both, piece))
+    both = lax.all_to_all(both, PAIR, split_axis=0, concat_axis=0, tiled=True)
+
     gathered = []
     part = piece.shape[0] // 2
     for h, order in enumerate((("x", "y"), ("y", "x"))):
@@ -138,13 +152,8 @@
             near = gather_axis(near, axis)
         gathered += [near, lax.ppermute(near, "core", [(0, 1), (1, 0)])]
 
-    amp_half = lax.dynamic_slice_in_dim(amplitudes, mine, half_width, 2)
-    hole_half = jnp.dot(
-        ladder, amp_half.reshape(amp_half.shape[0], -1), preferred_element_type=jnp.float32
-    ).astype(jnp.bfloat16).reshape(-1, rows, half_width)
-    both = jnp.concatenate([amplitudes, hole_half], axis=2)
-    both = lax.all_to_all(both, PAIR, split_axis=0, concat_axis=1, tiled=True)
-    pair_amps, pair_hole = both[:, :, :n_virt], both[:, :, n_virt:]
+    both = both.transpose(1, 0, 2, 3).reshape(each + 1, n_virt, n_virt)
+    pair_amps, pair_hole = both[:each], both[each]
 
     orbitals = jnp.arange(NO, dtype=jnp.int32)
     first_hot = (pair_ids[:, None] // NO == orbitals[None, :]).astype(jnp.float32)

time: 118 us -> 101 us (0.86)
  waiting for transfers between devices: 40.2 us -> 27.2 us
  starting transfers between devices: 43.6 us -> 41.1 us
    ppermute x1, waiting for transfers between devices: 29.2 us -> 0.01 us  [shards(): piece = lax.ppermute(piece, 'aux', [(0, 1), (1, 0)])]
    ppermute x12, waiting for transfers between devices: 11 us -> 27.2 us  [gather_axis(): lax.ppermute(block, axis, [(i, (i + d) % 4) for i in range(4)])]
    all_to_all x2 -> x0, local copies, waits for them, and re-layouts: 6.81 us -> none  [shards(): both = lax.all_to_all(both, PAIR, split_axis=0, concat_axis=1, tiled=True)]
    ppermute x2, starting transfers between devices: 5.78 us -> 1.03 us  [shards(): gathered += [near, lax.ppermute(near, 'core', [(0, 1), (1, 0)])]]
    slice x2 -> x4, local copies, waits for them, and re-layouts: 2.37 us -> 6.3 us  [shards(): pair_amps, pair_hole = (both[:each], both[each])]
    ppermute x1, starting transfers between devices: 4.3 us -> 7.83 us  [shards(): piece = lax.ppermute(piece, 'aux', [(0, 1), (1, 0)])]
    squeeze x0 -> x1, local copies, waits for them, and re-layouts: none -> 1.96 us  [shards(): pair_amps, pair_hole = (both[:each], both[each])]
    all_to_all x1, starting transfers between devices: 14.2 us -> 12.5 us  [shards(): both = lax.all_to_all(both, PAIR, split_axis=0, concat_axis=0, tiled=True)]
  transfers between devices with their start and end apart: 16 -> 16, of which waited for: 6 -> 7; matrix products, arithmetic and copies ran while one was open for 6% -> 13% of each run, Pallas kernels for 6% -> 7%
where the time goes in v3:
time: 101 us
  starting transfers between devices  41.1 us (41%)
  waiting for transfers between devices  27.2 us (27%)
  Pallas kernels  15.1 us (15%)
  local copies, waits for them, and re-layouts  13.8 us (14%)
  other arithmetic  2.79 us (3%)
    ppermute x12, waiting for transfers between devices, gather_axis(): lax.ppermute(block, axis, [(i, (i + d) % 4) for i in range(4)])  27.2 us
    ppermute x12, starting transfers between devices, gather_axis(): lax.ppermute(block, axis, [(i, (i + d) % 4) for i in range(4)])  19.8 us
    all_to_all x1, starting transfers between devices, shards(): both = lax.all_to_all(both, PAIR, split_axis=0, concat_axis=0, tiled=True)  12.5 us
    pallas_call x1, Pallas kernels, other_vectors(): pl.pallas_call(other_kernel, in_specs=[smem, smem, vmem, *[anywhere] * 4,...  8.4 us
    ppermute x1, starting transfers between devices, shards(): piece = lax.ppermute(piece, 'aux', [(0, 1), (1, 0)])  7.83 us
    pallas_call x1, Pallas kernels, own_vectors(): pl.pallas_call(own_kernel, in_specs=[pl.BlockSpec(memory_space=pltpu.SMEM...  6.65 us
    slice x4, local copies, waits for them, and re-layouts, shards(): pair_amps, pair_hole = (both[:each], both[each])  6.3 us
    unnamed x15, local copies, waits for them, and re-layouts  2.57 us
  transfers between devices with their start and end apart: 16, of which 7 were waited for; matrix products, arithmetic and copies ran while one was open for 13% of the time, Pallas kernels for 7%

profile of v3, /device:TPU:1, one launch (start us, length us, event | category | flops | bytes accessed | tf_op | source)
XLA Modules:
  0.0 100.7 jit_solution(8980433183091385909)
XLA Ops:
  0.0 0.9 constant_dynamic-slice_fusion
  1.0 7.8 %collective-permute-start = (bf16[8,16,512]{2,1,0:T(8,128)(2,1)S(1)}, bf16[8,16,512]{2,1,0:T(8,128)(2,1)S(1)}, u32[]{:S(2)}, u32[]{:S(2)}) collective-permute-start(bf16[8,16,512]{2,1,0:T(8,128)(2,1)S(1)} %constant_dynamic-slice_fusion), channel_id=1, source_target_pairs={{0,1},{1,0},{2,3},{3,2},{4,5},{5,4},{6,7},{7,6},{8,9},{9,8},{10,11... | collective-permute-start | bytes 393224 | tf_op jit(solution)/shard_map/ppermute | solution.py:134
  8.8 1.2 %constant_dynamic-slice_fusion.1 = bf16[256,4,256]{2,1,0:T(4,128)(2,1)S(1)} fusion(bf16[256,4,512]{2,1,0:T(4,128)(2,1)} %param.6, s32[]{:T(128)S(6)} %select_n.23), kind=kLoop, calls=%fused_computation.19 | loop fusion | bytes 1048580 | tf_op jit(solution)/shard_map/dynamic_slice | solution.py:136
  10.7 0.4 reshape.45
  11.3 2.2 %pad_maximum_fusion = bf16[128,3,4,512]{3,2,1,0:T(4,128)(2,1)} fusion(bf16[128,1,4,512]{3,2,1,0:T(4,128)(2,1)S(1)} %bitcast.43, bf16[128,2,4,512]{3,2,1,0:T(4,128)(2,1)S(1)} %bitcast.40), kind=kLoop, calls=%fused_computation | loop fusion | flops 786432 | bytes 3145728 | tf_op jit(solution)/shard_map/concatenate | solution.py:141
  13.5 12.5 %all-to-all-start = ((bf16[128,3,4,512]{3,2,1,0:T(4,128)(2,1)}), bf16[128,3,4,512]{3,2,1,0:T(4,128)(2,1)}, u32[]{:S(2)}, u32[]{:S(2)}) async-start(bf16[128,3,4,512]{3,2,1,0:T(4,128)(2,1)} %pad_maximum_fusion), calls=%async_computation | async-start | bytes 3145728 | tf_op jit(solution)/shard_map/all_to_all | solution.py:145
  26.1 3.3 %collective-permute-start.2 = (bf16[4,16,512]{2,1,0:T(8,128)(2,1)S(1)}, bf16[4,16,512]{2,1,0:T(8,128)(2,1)S(1)}, u32[]{:S(2)}, u32[]{:S(2)}) collective-permute-start(bf16[4,16,512]{2,1,0:T(8,128)(2,1)S(1)} %get-tuple-element.16), channel_id=1, source_target_pairs={{0,128},{64,192},{128,0},{192,64},{1,129},{65,193},{129,1},{193,65... | collective-permute-start | bytes 196616 | tf_op jit(solution)/shard_map/ppermute | solution.py:118
  29.4 0.5 collective-permute-start.1
  29.9 2.2 %collective-permute-start.3 = (bf16[4,16,512]{2,1,0:T(8,128)(2,1)S(1)}, bf16[4,16,512]{2,1,0:T(8,128)(2,1)S(1)}, u32[]{:S(2)}, u32[]{:S(2)}) collective-permute-start(bf16[4,16,512]{2,1,0:T(8,128)(2,1)S(1)} %get-tuple-element.16), channel_id=1, source_target_pairs={{0,192},{64,0},{128,64},{192,128},{1,193},{65,1},{129,65},{193,129... | collective-permute-start | bytes 196616 | tf_op jit(solution)/shard_map/ppermute | solution.py:118
  32.0 7.1 %collective-permute-done.2 = bf16[4,16,512]{2,1,0:T(8,128)(2,1)S(1)} collective-permute-done((bf16[4,16,512]{2,1,0:T(8,128)(2,1)S(1)}, bf16[4,16,512]{2,1,0:T(8,128)(2,1)S(1)}, u32[]{:S(2)}, u32[]{:S(2)}) %collective-permute-start.2) | collective-permute-done | bytes 65568 | tf_op jit(solution)/shard_map/ppermute | solution.py:118
  39.1 2.5 %collective-permute-done.1 = bf16[4,16,512]{2,1,0:T(8,128)(2,1)S(1)} collective-permute-done((bf16[4,16,512]{2,1,0:T(8,128)(2,1)S(1)}, bf16[4,16,512]{2,1,0:T(8,128)(2,1)S(1)}, u32[]{:S(2)}, u32[]{:S(2)}) %collective-permute-start.1) | collective-permute-done | bytes 65568 | tf_op jit(solution)/shard_map/ppermute | solution.py:118
  41.7 3.6 %collective-permute-start.5 = (bf16[4,4,16,512]{3,2,1,0:T(8,128)(2,1)S(1)}, bf16[4,4,16,512]{3,2,1,0:T(8,128)(2,1)S(1)}, u32[]{:S(2)}, u32[]{:S(2)}) collective-permute-start(bf16[4,4,16,512]{3,2,1,0:T(8,128)(2,1)S(1)} %get-tuple-element.12), channel_id=1, source_target_pairs={{0,32},{16,48},{32,0},{48,16},{1,33},{17,49},{33,1},{49,17},{2,34}... | collective-permute-start | bytes 786440 | tf_op jit(solution)/shard_map/ppermute | solution.py:118
  45.4 0.8 collective-permute-start.8
  46.2 1.9 %collective-permute-start.10 = (bf16[4,16,512]{2,1,0:T(8,128)(2,1)S(1)}, bf16[4,16,512]{2,1,0:T(8,128)(2,1)S(1)}, u32[]{:S(2)}, u32[]{:S(2)}) collective-permute-start(bf16[4,16,512]{2,1,0:T(8,128)(2,1)S(1)} %get-tuple-element.15), channel_id=1, source_target_pairs={{0,48},{16,0},{32,16},{48,32},{1,49},{17,1},{33,17},{49,33},{2,50}... | collective-permute-start | bytes 196616 | tf_op jit(solution)/shard_map/ppermute | solution.py:118
  48.1 5.8 %collective-permute-done.9 = bf16[4,16,512]{2,1,0:T(8,128)(2,1)S(1)} collective-permute-done((bf16[4,16,512]{2,1,0:T(8,128)(2,1)S(1)}, bf16[4,16,512]{2,1,0:T(8,128)(2,1)S(1)}, u32[]{:S(2)}, u32[]{:S(2)}) %collective-permute-start.9) | collective-permute-done | bytes 65568 | tf_op jit(solution)/shard_map/ppermute | solution.py:118
  53.9 2.9 %collective-permute-start.6 = (bf16[4,4,16,512]{3,2,1,0:T(8,128)(2,1)S(1)}, bf16[4,4,16,512]{3,2,1,0:T(8,128)(2,1)S(1)}, u32[]{:S(2)}, u32[]{:S(2)}) collective-permute-start(bf16[4,4,16,512]{3,2,1,0:T(8,128)(2,1)S(1)} %get-tuple-element.12), channel_id=1, source_target_pairs={{0,48},{16,0},{32,16},{48,32},{1,49},{17,1},{33,17},{49,33},{2,50}... | collective-permute-start | bytes 786440 | tf_op jit(solution)/shard_map/ppermute | solution.py:118
  56.8 0.9 collective-permute-done.8
  57.7 1.8 %collective-permute-start.12 = (bf16[4,4,16,512]{3,2,1,0:T(8,128)(2,1)S(1)}, bf16[4,4,16,512]{3,2,1,0:T(8,128)(2,1)S(1)}, u32[]{:S(2)}, u32[]{:S(2)}) collective-permute-start(bf16[4,4,16,512]{3,2,1,0:T(8,128)(2,1)S(1)} %get-tuple-element.10), channel_id=1, source_target_pairs={{0,128},{64,192},{128,0},{192,64},{1,129},{65,193},{129,1},{193,65... | collective-permute-start | bytes 786440 | tf_op jit(solution)/shard_map/ppermute | solution.py:118
  59.5 2.7 %collective-permute-start.13 = (bf16[4,4,16,512]{3,2,1,0:T(8,128)(2,1)S(1)}, bf16[4,4,16,512]{3,2,1,0:T(8,128)(2,1)S(1)}, u32[]{:S(2)}, u32[]{:S(2)}) collective-permute-start(bf16[4,4,16,512]{3,2,1,0:T(8,128)(2,1)S(1)} %get-tuple-element.10), channel_id=1, source_target_pairs={{0,192},{64,0},{128,64},{192,128},{1,193},{65,1},{129,65},{193,129... | collective-permute-start | bytes 786440 | tf_op jit(solution)/shard_map/ppermute | solution.py:118
  62.2 2.8 %collective-permute-done.4 = bf16[4,4,16,512]{3,2,1,0:T(8,128)(2,1)S(1)} collective-permute-done((bf16[4,4,16,512]{3,2,1,0:T(8,128)(2,1)S(1)}, bf16[4,4,16,512]{3,2,1,0:T(8,128)(2,1)S(1)}, u32[]{:S(2)}, u32[]{:S(2)}) %collective-permute-start.4) | collective-permute-done | bytes 262176 | tf_op jit(solution)/shard_map/ppermute | solution.py:118
  65.2 0.5 collective-permute-start.7
  65.7 1.1 %collective-permute-done.12 = bf16[4,4,16,512]{3,2,1,0:T(8,128)(2,1)S(1)} collective-permute-done((bf16[4,4,16,512]{3,2,1,0:T(8,128)(2,1)S(1)}, bf16[4,4,16,512]{3,2,1,0:T(8,128)(2,1)S(1)}, u32[]{:S(2)}, u32[]{:S(2)}) %collective-permute-start.12) | collective-permute-done | bytes 262176 | tf_op jit(solution)/shard_map/ppermute | solution.py:118
  66.7 7.1 %collective-permute-done.11 = bf16[4,4,16,512]{3,2,1,0:T(8,128)(2,1)S(1)} collective-permute-done((bf16[4,4,16,512]{3,2,1,0:T(8,128)(2,1)S(1)}, bf16[4,4,16,512]{3,2,1,0:T(8,128)(2,1)S(1)}, u32[]{:S(2)}, u32[]{:S(2)}) %collective-permute-start.11) | collective-permute-done | bytes 262176 | tf_op jit(solution)/shard_map/ppermute | solution.py:118
  74.0 0.5 collective-permute-start.14
  75.0 2.0 %slice.22 = bf16[1,128,4,512]{3,2,0,1:T(4,128)(2,1)} slice(bf16[3,128,4,512]{3,2,0,1:T(4,128)(2,1)} %bitcast.8), slice={[2:3], [0:128], [0:4], [0:512]} | slice | bytes 1048576 | tf_op jit(solution)/shard_map/slice | solution.py:156
  77.1 1.6 %slice.21 = bf16[2,128,4,512]{3,2,0,1:T(4,128)(2,1)S(1)} slice(bf16[3,128,4,512]{3,2,0,1:T(4,128)(2,1)} %bitcast.8), slice={[0:2], [0:128], [0:4], [0:512]} | slice | bytes 2097152 | tf_op jit(solution)/shard_map/slice | solution.py:156
  78.7 1.3 %copy.16 = bf16[2,128,4,512]{3,2,1,0:T(4,128)(2,1)} copy(bf16[2,128,4,512]{3,2,0,1:T(4,128)(2,1)S(1)} %slice.21) | data formatting | bytes 2097152 | tf_op jit(solution)/shard_map/slice | solution.py:156
  80.0 1.3 %slice.17.amps_ref = bf16[2,512,512]{2,1,0:T(8,128)(2,1)S(1)} reshape(bf16[2,128,4,512]{3,2,1,0:T(4,128)(2,1)} %copy.16) | data formatting | bytes 2097152 | tf_op jit(solution)/shard_map/slice | solution.py:156
  81.3 2.0 %squeeze.3.hole_ref = bf16[512,512]{1,0:T(8,128)(2,1)} reshape(bf16[1,128,4,512]{3,2,0,1:T(4,128)(2,1)} %slice.22) | data formatting | bytes 1048576 | tf_op jit(solution)/shard_map/squeeze | solution.py:156
  83.3 2.2 %copy-done.2 = bf16[8,512,512]{2,1,0:T(8,128)(2,1)S(1)} copy-done((bf16[8,512,512]{2,1,0:T(8,128)(2,1)S(1)}, bf16[8,512,512]{2,1,0:T(8,128)(2,1)}, u32[]{:S(2)}) %copy-start.2) | copy-done | bytes 4194328
  85.5 6.7 %own_vectors.1.base_ref = f32[512,512]{1,0:T(8,128)S(1)} custom-call(s32[4]{0:T(128)S(1)} %pad_add_fusion.place_ref, bf16[2,512,512]{2,1,0:T(8,128)(2,1)S(1)} %slice.17.amps_ref, bf16[8,512,512]{2,1,0:T(8,128)(2,1)S(1)} %copy-done.2), custom_call_target="tpu_custom_call" | custom-call | flops 4294967296 | bytes 4194304 | tf_op jit(solution)/shard_map/own_vectors/pallas_call | solution.py:40
  92.2 8.4 %other_vectors.1 = f32[2,512,256]{2,1,0:T(8,128)} custom-call(s32[4]{0:T(128)S(1)} %pad_add_fusion.place_ref, f32[2]{0:T(128)S(1)} %fusion.3.occ_ref, bf16[2,512,512]{2,1,0:T(8,128)(2,1)S(1)} %slice.17.amps_ref, bf16[4,4,4,16,512]{4,3,2,1,0:T(8,128)(2,1)S(1)} %pad_maximum_fusion.1.near0, bf16[4,4,4,16,512]{4,3,2,1,0:T(8,128)(2,1)} %collective-permute-done.7.far0, ...), custom_call_target="tpu_custom_call" | custom-call | flops 4294967296 | bytes 4194304 | tf_op jit(solution)/shard_map/other_vectors/pallas_call | solution.py:98
  (38 shorter events, 1.9 us)
Async XLA Ops:
  0.0 10.1 %copy-start = (bf16[256,256]{1,0:T(8,128)(2,1)S(1)}, bf16[256,256]{1,0:T(8,128)(2,1)}, u32[]{:S(2)}) copy-start(bf16[256,256]{1,0:T(8,128)(2,1)} %param.7) | copy-start | bytes 393220
  1.0 12.6 %collective-permute-start = (bf16[8,16,512]{2,1,0:T(8,128)(2,1)S(1)}, bf16[8,16,512]{2,1,0:T(8,128)(2,1)S(1)}, u32[]{:S(2)}, u32[]{:S(2)}) collective-permute-start(bf16[8,16,512]{2,1,0:T(8,128)(2,1)S(1)} %constant_dynamic-slice_fusion), channel_id=1, source_target_pairs={{0,1},{1,0},{2,3},{3,2},{4,5},{5,4},{6,7},{7,6},{8,9},{9,8},{10,11... | collective-permute-start | bytes 393224 | tf_op jit(solution)/shard_map/ppermute | solution.py:134
  10.1 1.2 %copy-start.3 = (bf16[256,4,512]{2,1,0:T(4,128)(2,1)S(1)}, bf16[256,4,512]{2,1,0:T(4,128)(2,1)}, u32[]{:S(2)}) copy-start(bf16[256,4,512]{2,1,0:T(4,128)(2,1)} %param.6) | copy-start | bytes 3145732
  13.5 61.5 %all-to-all-start = ((bf16[128,3,4,512]{3,2,1,0:T(4,128)(2,1)}), bf16[128,3,4,512]{3,2,1,0:T(4,128)(2,1)}, u32[]{:S(2)}, u32[]{:S(2)}) async-start(bf16[128,3,4,512]{3,2,1,0:T(4,128)(2,1)} %pad_maximum_fusion), calls=%async_computation | async-start | bytes 3145728 | tf_op jit(solution)/shard_map/all_to_all | solution.py:145
  26.1 13.1 %collective-permute-start.2 = (bf16[4,16,512]{2,1,0:T(8,128)(2,1)S(1)}, bf16[4,16,512]{2,1,0:T(8,128)(2,1)S(1)}, u32[]{:S(2)}, u32[]{:S(2)}) collective-permute-start(bf16[4,16,512]{2,1,0:T(8,128)(2,1)S(1)} %get-tuple-element.16), channel_id=1, source_target_pairs={{0,128},{64,192},{128,0},{192,64},{1,129},{65,193},{129,1},{193,65... | collective-permute-start | bytes 196616 | tf_op jit(solution)/shard_map/ppermute | solution.py:118
  29.4 12.3 %collective-permute-start.1 = (bf16[4,16,512]{2,1,0:T(8,128)(2,1)S(1)}, bf16[4,16,512]{2,1,0:T(8,128)(2,1)S(1)}, u32[]{:S(2)}, u32[]{:S(2)}) collective-permute-start(bf16[4,16,512]{2,1,0:T(8,128)(2,1)S(1)} %get-tuple-element.16), channel_id=1, source_target_pairs={{0,64},{64,128},{128,192},{192,0},{1,65},{65,129},{129,193},{193,1... | collective-permute-start | bytes 196616 | tf_op jit(solution)/shard_map/ppermute | solution.py:118
  29.9 11.8 %collective-permute-start.3 = (bf16[4,16,512]{2,1,0:T(8,128)(2,1)S(1)}, bf16[4,16,512]{2,1,0:T(8,128)(2,1)S(1)}, u32[]{:S(2)}, u32[]{:S(2)}) collective-permute-start(bf16[4,16,512]{2,1,0:T(8,128)(2,1)S(1)} %get-tuple-element.16), channel_id=1, source_target_pairs={{0,192},{64,0},{128,64},{192,128},{1,193},{65,1},{129,65},{193,129... | collective-permute-start | bytes 196616 | tf_op jit(solution)/shard_map/ppermute | solution.py:118
  41.7 17.8 %collective-permute-start.5 = (bf16[4,4,16,512]{3,2,1,0:T(8,128)(2,1)S(1)}, bf16[4,4,16,512]{3,2,1,0:T(8,128)(2,1)S(1)}, u32[]{:S(2)}, u32[]{:S(2)}) collective-permute-start(bf16[4,4,16,512]{3,2,1,0:T(8,128)(2,1)S(1)} %get-tuple-element.12), channel_id=1, source_target_pairs={{0,32},{16,48},{32,0},{48,16},{1,33},{17,49},{33,1},{49,17},{2,34}... | collective-permute-start | bytes 786440 | tf_op jit(solution)/shard_map/ppermute | solution.py:118
  45.3 8.5 %collective-permute-start.9 = (bf16[4,16,512]{2,1,0:T(8,128)(2,1)S(1)}, bf16[4,16,512]{2,1,0:T(8,128)(2,1)S(1)}, u32[]{:S(2)}, u32[]{:S(2)}) collective-permute-start(bf16[4,16,512]{2,1,0:T(8,128)(2,1)S(1)} %get-tuple-element.15), channel_id=1, source_target_pairs={{0,32},{16,48},{32,0},{48,16},{1,33},{17,49},{33,1},{49,17},{2,34}... | collective-permute-start | bytes 196616 | tf_op jit(solution)/shard_map/ppermute | solution.py:118
  45.4 12.2 %collective-permute-start.8 = (bf16[4,16,512]{2,1,0:T(8,128)(2,1)S(1)}, bf16[4,16,512]{2,1,0:T(8,128)(2,1)S(1)}, u32[]{:S(2)}, u32[]{:S(2)}) collective-permute-start(bf16[4,16,512]{2,1,0:T(8,128)(2,1)S(1)} %get-tuple-element.15), channel_id=1, source_target_pairs={{0,16},{16,32},{32,48},{48,0},{1,17},{17,33},{33,49},{49,1},{2,18}... | collective-permute-start | bytes 196616 | tf_op jit(solution)/shard_map/ppermute | solution.py:118
  46.2 11.4 %collective-permute-start.10 = (bf16[4,16,512]{2,1,0:T(8,128)(2,1)S(1)}, bf16[4,16,512]{2,1,0:T(8,128)(2,1)S(1)}, u32[]{:S(2)}, u32[]{:S(2)}) collective-permute-start(bf16[4,16,512]{2,1,0:T(8,128)(2,1)S(1)} %get-tuple-element.15), channel_id=1, source_target_pairs={{0,48},{16,0},{32,16},{48,32},{1,49},{17,1},{33,17},{49,33},{2,50}... | collective-permute-start | bytes 196616 | tf_op jit(solution)/shard_map/ppermute | solution.py:118
  48.1 16.9 %collective-permute-start.4 = (bf16[4,4,16,512]{3,2,1,0:T(8,128)(2,1)S(1)}, bf16[4,4,16,512]{3,2,1,0:T(8,128)(2,1)S(1)}, u32[]{:S(2)}, u32[]{:S(2)}) collective-permute-start(bf16[4,4,16,512]{3,2,1,0:T(8,128)(2,1)S(1)} %get-tuple-element.12), channel_id=1, source_target_pairs={{0,16},{16,32},{32,48},{48,0},{1,17},{17,33},{33,49},{49,1},{2,18}... | collective-permute-start | bytes 786440 | tf_op jit(solution)/shard_map/ppermute | solution.py:118
  53.9 11.1 %collective-permute-start.6 = (bf16[4,4,16,512]{3,2,1,0:T(8,128)(2,1)S(1)}, bf16[4,4,16,512]{3,2,1,0:T(8,128)(2,1)S(1)}, u32[]{:S(2)}, u32[]{:S(2)}) collective-permute-start(bf16[4,4,16,512]{3,2,1,0:T(8,128)(2,1)S(1)} %get-tuple-element.12), channel_id=1, source_target_pairs={{0,48},{16,0},{32,16},{48,32},{1,49},{17,1},{33,17},{49,33},{2,50}... | collective-permute-start | bytes 786440 | tf_op jit(solution)/shard_map/ppermute | solution.py:118
  57.7 9.1 %collective-permute-start.12 = (bf16[4,4,16,512]{3,2,1,0:T(8,128)(2,1)S(1)}, bf16[4,4,16,512]{3,2,1,0:T(8,128)(2,1)S(1)}, u32[]{:S(2)}, u32[]{:S(2)}) collective-permute-start(bf16[4,4,16,512]{3,2,1,0:T(8,128)(2,1)S(1)} %get-tuple-element.10), channel_id=1, source_target_pairs={{0,128},{64,192},{128,0},{192,64},{1,129},{65,193},{129,1},{193,65... | collective-permute-start | bytes 786440 | tf_op jit(solution)/shard_map/ppermute | solution.py:118
  59.5 14.3 %collective-permute-start.11 = (bf16[4,4,16,512]{3,2,1,0:T(8,128)(2,1)S(1)}, bf16[4,4,16,512]{3,2,1,0:T(8,128)(2,1)S(1)}, u32[]{:S(2)}, u32[]{:S(2)}) collective-permute-start(bf16[4,4,16,512]{3,2,1,0:T(8,128)(2,1)S(1)} %get-tuple-element.10), channel_id=1, source_target_pairs={{0,64},{64,128},{128,192},{192,0},{1,65},{65,129},{129,193},{193,1... | collective-permute-start | bytes 786440 | tf_op jit(solution)/shard_map/ppermute | solution.py:118
  59.5 14.3 %collective-permute-start.13 = (bf16[4,4,16,512]{3,2,1,0:T(8,128)(2,1)S(1)}, bf16[4,4,16,512]{3,2,1,0:T(8,128)(2,1)S(1)}, u32[]{:S(2)}, u32[]{:S(2)}) collective-permute-start(bf16[4,4,16,512]{3,2,1,0:T(8,128)(2,1)S(1)} %get-tuple-element.10), channel_id=1, source_target_pairs={{0,192},{64,0},{128,64},{192,128},{1,193},{65,1},{129,65},{193,129... | collective-permute-start | bytes 786440 | tf_op jit(solution)/shard_map/ppermute | solution.py:118
  65.1 9.4 %copy-start.4 = (f32[512]{0:T(512)S(1)}, f32[512]{0:T(512)}, u32[]{:S(2)}) copy-start(f32[512]{0:T(512)} %param.11) | copy-start | bytes 6148
  65.1 9.7 %copy-start.6 = (s32[2]{0:T(128)S(1)}, s32[2]{0:T(128)}, u32[]{:S(2)}) copy-start(s32[2]{0:T(128)} %param.9) | copy-start | bytes 28
  65.2 9.7 %copy-start.5 = (f32[16]{0:T(128)S(1)}, f32[16]{0:T(128)}, u32[]{:S(2)}) copy-start(f32[16]{0:T(128)} %param.10) | copy-start | bytes 196
  65.2 27.0 %collective-permute-start.7 = (bf16[4,4,4,16,512]{4,3,2,1,0:T(8,128)(2,1)S(1)}, bf16[4,4,4,16,512]{4,3,2,1,0:T(8,128)(2,1)}, u32[]{:S(2)}, u32[]{:S(2)}) collective-permute-start(bf16[4,4,4,16,512]{4,3,2,1,0:T(8,128)(2,1)S(1)} %pad_maximum_fusion.1.near0), channel_id=1, source_target_pairs={{0,2},{2,0},{1,3},{3,1},{4,6},{6,4},{5,7},{7,5},{8,10},{10,8},{9,1... | collective-permute-start | bytes 3145736 | tf_op jit(solution)/shard_map/ppermute | solution.py:153
  74.0 18.2 %collective-permute-start.14 = (bf16[4,4,4,16,512]{4,3,2,1,0:T(8,128)(2,1)S(1)}, bf16[4,4,4,16,512]{4,3,2,1,0:T(8,128)(2,1)}, u32[]{:S(2)}, u32[]{:S(2)}) collective-permute-start(bf16[4,4,4,16,512]{4,3,2,1,0:T(8,128)(2,1)S(1)} %pad_maximum_fusion.2.near1), channel_id=1, source_target_pairs={{0,2},{2,0},{1,3},{3,1},{4,6},{6,4},{5,7},{7,5},{8,10},{10,8},{9,1... | collective-permute-start | bytes 3145736 | tf_op jit(solution)/shard_map/ppermute | solution.py:153
  83.3 2.2 %copy-start.2 = (bf16[8,512,512]{2,1,0:T(8,128)(2,1)S(1)}, bf16[8,512,512]{2,1,0:T(8,128)(2,1)}, u32[]{:S(2)}) copy-start(bf16[8,512,512]{2,1,0:T(8,128)(2,1)} %vec_ref.1) | copy-start | bytes 12582916
  85.5 6.7 %copy-start.1 = (bf16[512,512]{1,0:T(8,128)(2,1)S(1)}, bf16[512,512]{1,0:T(8,128)(2,1)}, u32[]{:S(2)}) copy-start(bf16[512,512]{1,0:T(8,128)(2,1)} %squeeze.3.hole_ref) | copy-start | bytes 1572868

commit v4 on v3

v4 whole, which is shorter than its diff:
```python
import jax
import jax.numpy as jnp
from jax import lax
from jax.experimental import pallas as pl
from jax.experimental.pallas import tpu as pltpu
from jax.sharding import Mesh, PartitionSpec as P

NO = 16
AXES = ("x", "y", "z", "core", "aux")
PAIR = AXES[:4]
SIDE = 4
VMEM_LIMIT = 24 * 1024 * 1024
NT = (((1,), (1,)), ((), ()))


def add_vector(vector, cols, amps_ref, total_ref):
    nv = vector.shape[0]
    turned = lax.dot_general(amps_ref[...], cols, NT, preferred_element_type=jnp.float32).astype(jnp.bfloat16)
    total_ref[...] += jnp.dot(
        vector, jnp.concatenate([turned[:nv], turned[nv:]], axis=1), preferred_element_type=jnp.float32
    )


def own_kernel(place_ref, amps_ref, vec_ref, total_ref, vec, sems):
    nq, nv, _ = vec.shape
    half = nv // 2
    copies = [pltpu.make_async_copy(vec_ref.at[q], vec.at[q], sems.at[q]) for q in range(nq)]
    for copy in copies:
        copy.start()
    total_ref[...] = jnp.zeros_like(total_ref)
    start = pl.multiple_of(place_ref[0] * half, half)
    for q in range(nq):
        copies[q].wait()
        add_vector(vec[q], vec[q, pl.ds(start, half), :], amps_ref, total_ref)


def estimate(nq, nv):
    return pl.CostEstimate(flops=4 * nq * nv**3, bytes_accessed=2 * nq * nv * nv, transcendentals=0)


def own_vectors(place, amps, cholesky):
    nq, nv, _ = cholesky.shape
    return pl.pallas_call(
        own_kernel,
        in_specs=[
            pl.BlockSpec(memory_space=pltpu.SMEM),
            pl.BlockSpec(memory_space=pltpu.VMEM),
            pl.BlockSpec(memory_space=pltpu.HBM),
        ],
        out_specs=pl.BlockSpec(memory_space=pltpu.VMEM),
        out_shape=jax.ShapeDtypeStruct((nv, nv), jnp.float32),
        scratch_shapes=[pltpu.VMEM((nq, nv, nv), jnp.bfloat16), pltpu.SemaphoreType.DMA((nq,))],
        compiler_params=pltpu.CompilerParams(vmem_limit_bytes=VMEM_LIMIT),
        cost_estimate=estimate(16 * nq, nv),
        name="own_vectors",
    )(place, amps, cholesky)


def other_kernel(
    place_ref, occ_ref, amps_ref, near_ref, far_ref, base_ref, hole_ref, rows_ref, cols_ref, out_ref, vec, total, sems
):
    nq, slots, strip, nv = vec.shape
    half, part = nv // 2, nq // 2
    core, x0, y0 = place_ref[1], place_ref[2], place_ref[3]

    for h in range(2):
        for owner, src in ((core, near_ref), (1 - core, far_ref)):
            for outer in range(SIDE):
                for inner in range(SIDE):
                    dx = inner + owner * (outer - inner)
                    dy = outer + owner * (inner - outer)
                    x, y = lax.rem(x0 + SIDE - dx, SIDE), lax.rem(y0 + SIDE - dy, SIDE)
                    pltpu.make_async_copy(
                        src.at[outer, inner, pl.ds(h * part, part)],
                        vec.at[pl.ds(h * part, part), (owner * SIDE + x) * SIDE + y],
                        sems.at[h],
                    ).start()
    total[...] = base_ref[...]
    for q in range(nq):
        if q % part == 0:
            block = vec.at[pl.ds(q, part)]
            pltpu.make_async_copy(block, block, sems.at[q // part]).wait()
        cols = vec[q, pl.ds(place_ref[0] * (slots // 2), slots // 2)].reshape(half, nv)
        add_vector(vec[q].reshape(nv, nv), cols, amps_ref, total)
    level = rows_ref[...] + cols_ref[...]
    for p in range(out_ref.shape[0]):
        value = hole_ref[p].astype(jnp.float32) + total[:, p * half : (p + 1) * half]
        out_ref[p] = value / (level - occ_ref[p])


def other_vectors(place, occ_sum, amps, near, far, base, hole, rows, cols):
    nq, strip, nv = near.shape[2:]
    vmem = pl.BlockSpec(memory_space=pltpu.VMEM)
    smem = pl.BlockSpec(memory_space=pltpu.SMEM)
    anywhere = pl.BlockSpec(memory_space=pl.ANY)
    return pl.pallas_call(
        other_kernel,
        in_specs=[smem, smem, vmem, anywhere, anywhere, vmem, vmem, vmem, vmem],
        out_specs=vmem,
        out_shape=jax.ShapeDtypeStruct(hole.shape, jnp.float32),
        scratch_shapes=[
            pltpu.VMEM((nq, nv // strip, strip, nv), jnp.bfloat16),
            pltpu.VMEM((nv, nv), jnp.float32),
            pltpu.SemaphoreType.DMA((2,)),
        ],
        compiler_params=pltpu.CompilerParams(vmem_limit_bytes=VMEM_LIMIT),
        cost_estimate=estimate(nq, nv),
        name="other_vectors",
    )(place, occ_sum, amps, near, far, base, hole, rows, cols)


def plane_shift(block, shift, first_core_axis):
    pairs = []
    for x in range(SIDE):
        for y in range(SIDE):
            for core in range(2):
                if core == first_core_axis:
                    to = x * SIDE + (y + shift) % SIDE
                else:
                    to = (x + shift) % SIDE * SIDE + y
                pairs.append(((x * SIDE + y) * 2 + core, to * 2 + core))
    return lax.ppermute(block, ("x", "y", "core"), pairs)


def gather_plane(block):
    for stage in range(2):
        block = jnp.stack([block] + [plane_shift(block, d, 1 - stage) for d in (1, 2, 3)])
    return block


def ring_pairs(step):
    steps = {1: (1, 1), 3: (-1, -1), 2: (2, -2)}[step]
    pairs = []
    for z8 in range(2 * SIDE):
        for core in range(2):
            to = (z8 + steps[core]) % (2 * SIDE)
            pairs.append(((z8 % SIDE * 2 + core) * 2 + z8 // SIDE, (to % SIDE * 2 + core) * 2 + to // SIDE))
    return pairs


def ring_target(z8, core, step):
    move = {0: 0, 1: 1, 3: -1}.get(step)
    move = 2 - 4 * core if move is None else move
    return lax.rem(z8 + move + 2 * SIDE, 2 * SIDE)


def spread(local, width, z, core, aux, after=None):
    n_pair, rows, full = local.shape
    cells = SIDE * SIDE
    view = local.reshape(cells, SIDE, n_pair // (cells * SIDE), rows, full)
    blocks = []
    for step in range(SIDE):
        target = ring_target(aux * SIDE + z, core, step)
        column = lax.div(target, SIDE) * width if width < full else 0
        block = lax.dynamic_slice(
            view, (0, lax.rem(target, SIDE), 0, 0, column), (cells, 1, view.shape[2], rows, width)
        )
        if step:
            block = lax.ppermute(block, ("z", "core", "aux"), ring_pairs(step))
        blocks.append(block.reshape(2 * cells, 1, -1, rows, width))
    packed = jnp.zeros((2 * cells, SIDE, blocks[0].shape[2], rows, width), local.dtype)
    for step, block in enumerate(blocks):
        packed = lax.dynamic_update_slice(packed, block, (0, lax.rem(z + SIDE - step, SIDE), 0, 0, 0))
    if after is not None:
        packed, after = lax.optimization_barrier((packed, after))
    got = lax.all_to_all(packed, ("x", "y", "core"), split_axis=0, concat_axis=0, tiled=True)
    return got, after


def by_pair(got):
    cells = SIDE * SIDE
    _, planes, each, rows, width = got.shape
    return got.reshape(cells, 2, planes, each, rows, width).transpose(3, 0, 2, 1, 4, 5).reshape(each, -1, width)


def shards(amplitudes, ladder, cholesky, pair_ids, occ_energy, vir_energy):
    n_pair, rows, n_virt = amplitudes.shape
    half_width = n_virt // lax.axis_size("aux")
    aux, core, z = lax.axis_index("aux"), lax.axis_index("core"), lax.axis_index("z")
    x, y = lax.axis_index("x"), lax.axis_index("y")
    strip = half_width // (SIDE * SIDE)

    slot = (core * SIDE + x) * SIDE + y
    piece = lax.dynamic_slice_in_dim(cholesky, slot * strip, strip, 1)
    near = gather_plane(lax.ppermute(piece, "aux", [(0, 1), (1, 0)]))
    far = lax.ppermute(near, "core", [(0, 1), (1, 0)])

    hole = jnp.dot(
        ladder, amplitudes.reshape(n_pair, -1), preferred_element_type=jnp.float32
    ).astype(jnp.bfloat16).reshape(amplitudes.shape)
    got_amps, _ = spread(amplitudes, n_virt, z, core, aux)
    got_hole, got_amps = spread(hole, half_width, z, core, aux, got_amps)
    pair_amps = by_pair(got_amps).reshape(-1, n_virt)
    pair_hole = by_pair(got_hole)

    orbitals = jnp.arange(NO, dtype=jnp.int32)
    first_hot = (pair_ids[:, None] // NO == orbitals[None, :]).astype(jnp.float32)
    second_hot = (pair_ids[:, None] % NO == orbitals[None, :]).astype(jnp.float32)
    occ_sum = jnp.sum((first_hot + second_hot) * occ_energy[None, :], axis=1)
    vir_cols = lax.dynamic_slice_in_dim(vir_energy, aux * half_width, half_width, 0)
    place = jnp.stack([aux, core, x, y]).astype(jnp.int32)

    base = own_vectors(place, pair_amps, cholesky)
    return other_vectors(
        place, occ_sum, pair_amps, near, far, base, pair_hole, vir_energy[:, None], vir_cols[None, :]
    )


def solution(mesh):
    fine = Mesh(mesh.devices.reshape(SIDE, SIDE, SIDE, 2, 2), AXES)
    in_specs = (P(None, PAIR, None), P(), P("aux", None, None), P(PAIR), P(), P())
    out_specs = P(PAIR, None, "aux")
    return jax.shard_map(shards, mesh=fine, in_specs=in_specs, out_specs=out_specs, check_vma=False)
```

time: 101 us -> 110 us (1.089)
  local copies, waits for them, and re-layouts: 13.8 us -> 27.5 us
  waiting for transfers between devices: 27.2 us -> 19.5 us
  Pallas kernels: 15.1 us -> 18.3 us
    ppermute x15 -> x14, waiting for transfers between devices: 27.2 us -> 19.5 us  [the longest x6 14.6 us: plane_shift(): return lax.ppermute(block, ('x', 'y', 'core'), pairs)]
    dynamic_update_slice x0 -> x8, local copies, waits for them, and re-layouts: none -> 7.14 us  [spread(): lax.dynamic_update_slice(packed, block, (0, lax.rem(z + SIDE - step, SIDE...]
    slice x4 -> x0, local copies, waits for them, and re-layouts: 6.3 us -> none  [shards(): pair_amps, pair_hole = (both[:each], both[each])]
    ppermute x15 -> x14, starting transfers between devices: 28.6 us -> 24.3 us  [the longest x6 11.4 us: plane_shift(): return lax.ppermute(block, ('x', 'y', 'core'), pairs)]
    unnamed x15 -> x25, local copies, waits for them, and re-layouts: 2.57 us -> 6.49 us
    all_to_all x1 -> x2, starting transfers between devices: 12.5 us -> 16.2 us  [spread(): lax.all_to_all(packed, ('x', 'y', 'core'), split_axis=0, concat_axis=0, t...]
    transpose x0 -> x2, local copies, waits for them, and re-layouts: none -> 3.66 us  [by_pair(): got.reshape(cells, 2, planes, each, rows, width).transpose(3, 0, 2, 1, 4, 5)]
    pallas_call x1, Pallas kernels: 6.65 us -> 9.58 us  [own_vectors(): pl.pallas_call(own_kernel, in_specs=[pl.BlockSpec(memory_space=pltpu.SMEM...]
  transfers between devices with their start and end apart: 16 -> 16, of which waited for: 7 -> 4; matrix products, arithmetic and copies ran while one was open for 13% -> 21% of each run, Pallas kernels for 7% -> 9%
where the time goes in v4:
time: 110 us
  starting transfers between devices  40.5 us (37%)
  local copies, waits for them, and re-layouts  27.5 us (25%)
  waiting for transfers between devices  19.5 us (18%)
  Pallas kernels  18.3 us (17%)
  other arithmetic  2.95 us (3%)
    all_to_all x2, starting transfers between devices, spread(): lax.all_to_all(packed, ('x', 'y', 'core'), split_axis=0, concat_axis=0, t...  16.2 us
    ppermute x6, waiting for transfers between devices, plane_shift(): return lax.ppermute(block, ('x', 'y', 'core'), pairs)  14.6 us
    ppermute x6, starting transfers between devices, plane_shift(): return lax.ppermute(block, ('x', 'y', 'core'), pairs)  11.4 us
    pallas_call x1, Pallas kernels, own_vectors(): pl.pallas_call(own_kernel, in_specs=[pl.BlockSpec(memory_space=pltpu.SMEM...  9.58 us
    pallas_call x1, Pallas kernels, other_vectors(): pl.pallas_call(other_kernel, in_specs=[smem, smem, vmem, anywhere, anywhe...  8.73 us
    ppermute x1, starting transfers between devices, shards(): near = gather_plane(lax.ppermute(piece, 'aux', [(0, 1), (1, 0)]))  7.74 us
    dynamic_update_slice x8, local copies, waits for them, and re-layouts, spread(): lax.dynamic_update_slice(packed, block, (0, lax.rem(z + SIDE - step, SIDE...  7.14 us
    unnamed x25, local copies, waits for them, and re-layouts  6.49 us
  transfers between devices with their start and end apart: 16, of which 4 were waited for; matrix products, arithmetic and copies ran while one was open for 21% of the time, Pallas kernels for 9%

profile of v4, /device:TPU:1, one launch (start us, length us, event | category | flops | bytes accessed | tf_op | source)
XLA Modules:
  0.0 109.7 jit_solution(15041204680791077438)
XLA Ops:
  0.0 1.7 %constant_dynamic-slice_fusion = bf16[8,16,512]{2,1,0:T(8,128)(2,1)} fusion(bf16[8,512,512]{2,1,0:T(8,128)(2,1)} %vec_ref.1, s32[]{:T(128)S(6)} %select_n.78), kind=kLoop, calls=%fused_computation.3 | loop fusion | bytes 262148 | tf_op jit(solution)/shard_map/dynamic_slice | solution.py:184
  1.7 7.7 %collective-permute-start.6 = (bf16[8,16,512]{2,1,0:T(8,128)(2,1)}, bf16[8,16,512]{2,1,0:T(8,128)(2,1)S(1)}, u32[]{:S(2)}, u32[]{:S(2)}) collective-permute-start(bf16[8,16,512]{2,1,0:T(8,128)(2,1)} %constant_dynamic-slice_fusion), channel_id=1, source_target_pairs={{0,1},{1,0},{2,3},{3,2},{4,5},{5,4},{6,7},{7,6},{8,9},{9,8},{10,11... | collective-permute-start | bytes 393224 | tf_op jit(solution)/shard_map/ppermute | solution.py:185
  9.4 1.6 %constant_dynamic-slice_fusion.1 = (bf16[16,1,4,4,512]{4,3,2,1,0:T(4,128)(2,1)S(1)}, bf16[16,1,4,4,512]{4,3,2,1,0:T(4,128)(2,1)S(1)}, bf16[16,1,4,4,512]{4,3,2,1,0:T(4,128)(2,1)S(1)}, bf16[16,1,4,4,512]{4,3,2,1,0:T(4,128)(2,1)S(1)}) fusion(bf16[16,4,4,4,512]{4,3,2,1,0:T(4,128)(2,1)} %bitcast.35, s32[]{:T(128)S(6)} %select_n.75, s32[]{:T(128)S(6)} %select_n.72, ...), kind=kLoop, calls=%fused_computation.5 | loop fusion | bytes 2097168 | tf_op jit(solution)/shard_map/dynamic_slice | solution.py:155
  11.2 1.0 collective-permute-start.3
  14.8 3.2 %collective-permute-start.5 = (bf16[16,1,4,4,512]{4,3,2,1,0:T(4,128)(2,1)S(1)}, bf16[16,1,4,4,512]{4,3,2,1,0:T(4,128)(2,1)S(1)}, u32[]{:S(2)}, u32[]{:S(2)}) collective-permute-start(bf16[16,1,4,4,512]{4,3,2,1,0:T(4,128)(2,1)S(1)} %get-tuple-element.9), channel_id=1, source_target_pairs={{0,13},{2,15},{4,0},{6,2},{8,4},{10,6},{12,8},{14,10},{1,12},{3,14... | collective-permute-start | bytes 786440 | tf_op jit(solution)/shard_map/ppermute | solution.py:159
  18.0 1.4 %broadcast_in_dim.18 = bf16[32,4,2,4,512]{4,3,2,1,0:T(4,128)(2,1)} broadcast(bf16[]{:T(256)} %constant.99.clone.1), dimensions={} | broadcast | bytes 1048578 | tf_op jit(solution)/shard_map/broadcast_in_dim | solution.py:161
  20.2 2.8 %collective-permute-done.3 = bf16[16,1,4,4,512]{4,3,2,1,0:T(4,128)(2,1)} collective-permute-done((bf16[16,1,4,4,512]{4,3,2,1,0:T(4,128)(2,1)S(1)}, bf16[16,1,4,4,512]{4,3,2,1,0:T(4,128)(2,1)}, u32[]{:S(2)}, u32[]{:S(2)}) %collective-permute-start.3) | collective-permute-done | bytes 262176 | tf_op jit(solution)/shard_map/ppermute | solution.py:159
  23.0 2.7 %collective-permute-start.9 = (bf16[8,16,512]{2,1,0:T(8,128)(2,1)S(1)}, bf16[8,16,512]{2,1,0:T(8,128)(2,1)S(1)}, u32[]{:S(2)}, u32[]{:S(2)}) collective-permute-start(bf16[8,16,512]{2,1,0:T(8,128)(2,1)S(1)} %collective-permute-done.6), channel_id=1, source_target_pairs={{0,192},{2,50},{16,208},{18,2},{32,224},{34,18},{48,240},{50,34},{... | collective-permute-start | bytes 393224 | tf_op jit(solution)/shard_map/ppermute | solution.py:122
  25.7 1.7 %constant_dynamic-update-slice_fusion.2 = bf16[32,4,2,4,512]{4,3,2,1,0:T(4,128)(2,1)} fusion(bf16[32,4,2,4,512]{4,3,2,1,0:T(4,128)(2,1)} %constant_dynamic-update-slice_fusion.3, bf16[32,1,2,4,512]{4,3,2,1,0:T(4,128)(2,1)} %bitcast.10, s32[]{:T(128)S(6)} %select_n.71), kind=kLoop, calls=%fused_computation.8 | loop fusion | bytes 524292 | tf_op jit(solution)/shard_map/dynamic_update_slice | solution.py:163
  27.5 1.8 %collective-permute-start.8 = (bf16[8,16,512]{2,1,0:T(8,128)(2,1)S(1)}, bf16[8,16,512]{2,1,0:T(8,128)(2,1)S(1)}, u32[]{:S(2)}, u32[]{:S(2)}) collective-permute-start(bf16[8,16,512]{2,1,0:T(8,128)(2,1)S(1)} %collective-permute-done.6), channel_id=1, source_target_pairs={{0,128},{2,34},{16,144},{18,50},{32,160},{34,2},{48,176},{50,18},{... | collective-permute-start | bytes 393224 | tf_op jit(solution)/shard_map/ppermute | solution.py:122
  29.3 1.7 %constant_dynamic-update-slice_fusion.1 = bf16[32,4,2,4,512]{4,3,2,1,0:T(4,128)(2,1)} fusion(bf16[32,4,2,4,512]{4,3,2,1,0:T(4,128)(2,1)} %constant_dynamic-update-slice_fusion.2, bf16[32,1,2,4,512]{4,3,2,1,0:T(4,128)(2,1)} %bitcast.11, s32[]{:T(128)S(6)} %select_n.74), kind=kLoop, calls=%fused_computation.6 | loop fusion | bytes 524292 | tf_op jit(solution)/shard_map/dynamic_update_slice | solution.py:163
  31.0 1.3 %collective-permute-start.7 = (bf16[8,16,512]{2,1,0:T(8,128)(2,1)S(1)}, bf16[8,16,512]{2,1,0:T(8,128)(2,1)S(1)}, u32[]{:S(2)}, u32[]{:S(2)}) collective-permute-start(bf16[8,16,512]{2,1,0:T(8,128)(2,1)S(1)} %collective-permute-done.6), channel_id=1, source_target_pairs={{0,64},{2,18},{16,80},{18,34},{32,96},{34,50},{48,112},{50,2},{64,... | collective-permute-start | bytes 393224 | tf_op jit(solution)/shard_map/ppermute | solution.py:122
  33.1 11.2 %all-to-all-start = ((bf16[32,4,2,4,512]{4,3,2,1,0:T(4,128)(2,1)}), bf16[32,4,2,4,512]{4,3,2,1,0:T(4,128)(2,1)S(1)}, u32[]{:S(2)}, u32[]{:S(2)}) async-start(bf16[32,4,2,4,512]{4,3,2,1,0:T(4,128)(2,1)} %constant_dynamic-update-slice_fusion), calls=%async_computation | async-start | bytes 2097152 | tf_op jit(solution)/shard_map/all_to_all | solution.py:166
  45.6 2.9 %collective-permute-start.11 = (bf16[4,8,16,512]{3,2,1,0:T(8,128)(2,1)S(1)}, bf16[4,8,16,512]{3,2,1,0:T(8,128)(2,1)S(1)}, u32[]{:S(2)}, u32[]{:S(2)}) collective-permute-start(bf16[4,8,16,512]{3,2,1,0:T(8,128)(2,1)S(1)} %get-tuple-element.18), channel_id=1, source_target_pairs={{0,32},{2,130},{16,48},{18,146},{32,0},{34,162},{48,16},{50,178},{... | collective-permute-start | bytes 1572872 | tf_op jit(solution)/shard_map/ppermute | solution.py:122
  48.8 2.4 %collective-permute-start.12 = (bf16[4,8,16,512]{3,2,1,0:T(8,128)(2,1)S(1)}, bf16[4,8,16,512]{3,2,1,0:T(8,128)(2,1)}, u32[]{:S(2)}, u32[]{:S(2)}) collective-permute-start(bf16[4,8,16,512]{3,2,1,0:T(8,128)(2,1)S(1)} %get-tuple-element.18), channel_id=1, source_target_pairs={{0,48},{2,194},{16,0},{18,210},{32,16},{34,226},{48,32},{50,242},{... | collective-permute-start | bytes 1572872 | tf_op jit(solution)/shard_map/ppermute | solution.py:122
  52.0 1.0 constant_dynamic-update-slice_fusion.6
  53.0 1.0 constant_dynamic-update-slice_fusion.5
  53.9 2.1 %collective-permute-done.2 = bf16[16,1,4,4,256]{4,3,2,1,0:T(4,128)(2,1)S(1)} collective-permute-done((bf16[16,1,4,4,256]{4,3,2,1,0:T(4,128)(2,1)}, bf16[16,1,4,4,256]{4,3,2,1,0:T(4,128)(2,1)S(1)}, u32[]{:S(2)}, u32[]{:S(2)}) %collective-permute-start.2) | collective-permute-done | bytes 131104 | tf_op jit(solution)/shard_map/ppermute | solution.py:159
  56.1 9.3 %collective-permute-done.11 = bf16[4,8,16,512]{3,2,1,0:T(8,128)(2,1)S(1)} collective-permute-done((bf16[4,8,16,512]{3,2,1,0:T(8,128)(2,1)S(1)}, bf16[4,8,16,512]{3,2,1,0:T(8,128)(2,1)S(1)}, u32[]{:S(2)}, u32[]{:S(2)}) %collective-permute-start.11) | collective-permute-done | bytes 524320 | tf_op jit(solution)/shard_map/ppermute | solution.py:122
  65.4 5.3 %collective-permute-done.10 = bf16[4,8,16,512]{3,2,1,0:T(8,128)(2,1)S(1)} collective-permute-done((bf16[4,8,16,512]{3,2,1,0:T(8,128)(2,1)S(1)}, bf16[4,8,16,512]{3,2,1,0:T(8,128)(2,1)S(1)}, u32[]{:S(2)}, u32[]{:S(2)}) %collective-permute-start.10) | collective-permute-done | bytes 524320 | tf_op jit(solution)/shard_map/ppermute | solution.py:122
  71.5 1.8 %pad_maximum_fusion.near_ref = bf16[4,4,8,16,512]{4,3,2,1,0:T(8,128)(2,1)S(1)} fusion(bf16[1,4,8,16,512]{4,3,2,1,0:T(8,128)(2,1)} %bitcast.22, bf16[1,4,8,16,512]{4,3,2,1,0:T(8,128)(2,1)} %bitcast.41, bf16[1,4,8,16,512]{4,3,2,1,0:T(8,128)(2,1)} %bitcast.42, bf16[1,4,8,16,512]{4,3,2,1,0:T(8,128)(2,1)} %get-tuple-element.17), kind=kLoop, calls=%fused_computation.1 | loop fusion | flops 3145728 | bytes 4194304 | tf_op jit(solution)/shard_map/stack | solution.py:127
  73.8 1.5 %copy.10 = bf16[2,16,4,2,4,512]{5,4,3,2,1,0:T(4,128)(2,1)} copy(bf16[2,16,4,2,4,512]{5,4,0,2,3,1:T(4,128)(2,1)S(1)} %bitcast.37) | data formatting | bytes 2097152 | tf_op jit(solution)/shard_map/transpose | solution.py:173
  75.3 1.3 %reshape_reshape.7.amps_ref = bf16[1024,512]{1,0:T(8,128)(2,1)S(1)} reshape(bf16[2,16,4,2,4,512]{5,4,3,2,1,0:T(4,128)(2,1)} %copy.10) | data formatting | bytes 2097152 | tf_op jit(solution)/shard_map/reshape;reshape | solution.py:193
  76.7 5.0 %all-to-all-start.1 = ((bf16[32,4,2,4,256]{4,3,2,1,0:T(4,128)(2,1)}), bf16[32,4,2,4,256]{4,3,2,1,0:T(4,128)(2,1)}, u32[]{:S(2)}, u32[]{:S(2)}) async-start(bf16[32,4,2,4,256]{4,3,2,1,0:T(4,128)(2,1)} %copy-done.6), calls=%async_computation.1 | async-start | bytes 1048576 | tf_op jit(solution)/shard_map/all_to_all | solution.py:166
  81.7 2.2 %copy-done.2 = bf16[8,512,512]{2,1,0:T(8,128)(2,1)S(1)} copy-done((bf16[8,512,512]{2,1,0:T(8,128)(2,1)S(1)}, bf16[8,512,512]{2,1,0:T(8,128)(2,1)}, u32[]{:S(2)}) %copy-start.2) | copy-done | bytes 4194328
  83.8 9.6 %own_vectors.1.base_ref = f32[512,512]{1,0:T(8,128)S(1)} custom-call(s32[4]{0:T(128)S(1)} %pad_add_fusion.place_ref, bf16[1024,512]{1,0:T(8,128)(2,1)S(1)} %reshape_reshape.7.amps_ref, bf16[8,512,512]{2,1,0:T(8,128)(2,1)S(1)} %copy-done.2), custom_call_target="tpu_custom_call" | custom-call | flops 68719476736 | bytes 67108864 | tf_op jit(solution)/shard_map/own_vectors/pallas_call | solution.py:43
  93.4 1.0 copy-done.3
  94.4 2.1 %copy.11 = bf16[2,16,4,2,4,256]{5,4,3,2,1,0:T(4,128)(2,1)} copy(bf16[2,16,4,2,4,256]{5,4,0,2,3,1:T(4,128)(2,1)} %bitcast.24) | data formatting | bytes 1048576 | tf_op jit(solution)/shard_map/transpose | solution.py:173
  96.5 2.0 %reshape.78.hole_ref = bf16[2,512,256]{2,1,0:T(8,128)(2,1)} reshape(bf16[2,16,4,2,4,256]{5,4,3,2,1,0:T(4,128)(2,1)} %copy.11) | data formatting | bytes 1048576 | tf_op jit(solution)/shard_map/reshape | solution.py:173
  98.5 1.0 copy-done.1
  99.5 1.2 %copy-done.4 = f32[512,512]{1,0:T(8,128)S(1)} copy-done((f32[512,512]{1,0:T(8,128)S(1)}, f32[512,512]{1,0:T(8,128)}, u32[]{:S(2)}) %copy-start.4) | copy-done | bytes 1048600
  100.8 8.7 %other_vectors.1 = f32[2,512,256]{2,1,0:T(8,128)} custom-call(s32[4]{0:T(128)S(1)} %pad_add_fusion.place_ref, f32[2]{0:T(128)S(1)} %fusion.2.occ_ref, bf16[1024,512]{1,0:T(8,128)(2,1)S(1)} %reshape_reshape.7.amps_ref, bf16[4,4,8,16,512]{4,3,2,1,0:T(8,128)(2,1)S(1)} %pad_maximum_fusion.near_ref, bf16[4,4,8,16,512]{4,3,2,1,0:T(8,128)(2,1)} %collective-permute-done.13.far_ref, ...), custom_call_target="tpu_custom_call" | custom-call | flops 4294967296 | bytes 4194304 | tf_op jit(solution)/shard_map/other_vectors/pallas_call | solution.py:96
  (53 shorter events, 7.9 us)
Async XLA Ops:
  0.0 12.4 %copy-start = (bf16[256,256]{1,0:T(8,128)(2,1)S(1)}, bf16[256,256]{1,0:T(8,128)(2,1)}, u32[]{:S(2)}) copy-start(bf16[256,256]{1,0:T(8,128)(2,1)} %param.7) | copy-start | bytes 393220
  0.0 12.1 %copy-start.5 = (bf16[256,4,512]{2,1,0:T(4,128)(2,1)S(1)}, bf16[256,4,512]{2,1,0:T(4,128)(2,1)}, u32[]{:S(2)}) copy-start(bf16[256,4,512]{2,1,0:T(4,128)(2,1)} %param.6) | copy-start | bytes 3145732
  1.7 18.6 %collective-permute-start.6 = (bf16[8,16,512]{2,1,0:T(8,128)(2,1)}, bf16[8,16,512]{2,1,0:T(8,128)(2,1)S(1)}, u32[]{:S(2)}, u32[]{:S(2)}) collective-permute-start(bf16[8,16,512]{2,1,0:T(8,128)(2,1)} %constant_dynamic-slice_fusion), channel_id=1, source_target_pairs={{0,1},{1,0},{2,3},{3,2},{4,5},{5,4},{6,7},{7,6},{8,9},{9,8},{10,11... | collective-permute-start | bytes 393224 | tf_op jit(solution)/shard_map/ppermute | solution.py:185
  11.1 16.4 %collective-permute-start.4 = (bf16[16,1,4,4,512]{4,3,2,1,0:T(4,128)(2,1)S(1)}, bf16[16,1,4,4,512]{4,3,2,1,0:T(4,128)(2,1)}, u32[]{:S(2)}, u32[]{:S(2)}) collective-permute-start(bf16[16,1,4,4,512]{4,3,2,1,0:T(4,128)(2,1)S(1)} %get-tuple-element.10), channel_id=1, source_target_pairs={{0,8},{2,11},{4,12},{6,15},{8,1},{10,2},{12,5},{14,6},{1,9},{3,10}... | collective-permute-start | bytes 786440 | tf_op jit(solution)/shard_map/ppermute | solution.py:159
  11.2 11.8 %collective-permute-start.3 = (bf16[16,1,4,4,512]{4,3,2,1,0:T(4,128)(2,1)S(1)}, bf16[16,1,4,4,512]{4,3,2,1,0:T(4,128)(2,1)}, u32[]{:S(2)}, u32[]{:S(2)}) collective-permute-start(bf16[16,1,4,4,512]{4,3,2,1,0:T(4,128)(2,1)S(1)} %get-tuple-element.11), channel_id=1, source_target_pairs={{0,4},{2,6},{4,8},{6,10},{8,12},{10,14},{12,1},{14,3},{1,5},{3,7},... | collective-permute-start | bytes 786440 | tf_op jit(solution)/shard_map/ppermute | solution.py:159
  14.7 38.3 %collective-permute-start.1 = (bf16[16,1,4,4,256]{4,3,2,1,0:T(4,128)(2,1)}, bf16[16,1,4,4,256]{4,3,2,1,0:T(4,128)(2,1)}, u32[]{:S(2)}, u32[]{:S(2)}) collective-permute-start(bf16[16,1,4,4,256]{4,3,2,1,0:T(4,128)(2,1)} %get-tuple-element.14), channel_id=1, source_target_pairs={{0,8},{2,11},{4,12},{6,15},{8,1},{10,2},{12,5},{14,6},{1,9},{3,10}... | collective-permute-start | bytes 393224 | tf_op jit(solution)/shard_map/ppermute | solution.py:159
  14.8 16.3 %collective-permute-start.5 = (bf16[16,1,4,4,512]{4,3,2,1,0:T(4,128)(2,1)S(1)}, bf16[16,1,4,4,512]{4,3,2,1,0:T(4,128)(2,1)S(1)}, u32[]{:S(2)}, u32[]{:S(2)}) collective-permute-start(bf16[16,1,4,4,512]{4,3,2,1,0:T(4,128)(2,1)S(1)} %get-tuple-element.9), channel_id=1, source_target_pairs={{0,13},{2,15},{4,0},{6,2},{8,4},{10,6},{12,8},{14,10},{1,12},{3,14... | collective-permute-start | bytes 786440 | tf_op jit(solution)/shard_map/ppermute | solution.py:159
  19.4 24.9 %copy-start.11 = (s32[2]{0:T(128)S(1)}, s32[2]{0:T(128)}, u32[]{:S(2)}) copy-start(s32[2]{0:T(128)} %param.9) | copy-start | bytes 28
  20.2 31.4 %collective-permute-start = (bf16[16,1,4,4,256]{4,3,2,1,0:T(4,128)(2,1)}, bf16[16,1,4,4,256]{4,3,2,1,0:T(4,128)(2,1)}, u32[]{:S(2)}, u32[]{:S(2)}) collective-permute-start(bf16[16,1,4,4,256]{4,3,2,1,0:T(4,128)(2,1)} %get-tuple-element.15), channel_id=1, source_target_pairs={{0,4},{2,6},{4,8},{6,10},{8,12},{10,14},{12,1},{14,3},{1,5},{3,7},... | collective-permute-start | bytes 393224 | tf_op jit(solution)/shard_map/ppermute | solution.py:159
  23.0 21.7 %collective-permute-start.9 = (bf16[8,16,512]{2,1,0:T(8,128)(2,1)S(1)}, bf16[8,16,512]{2,1,0:T(8,128)(2,1)S(1)}, u32[]{:S(2)}, u32[]{:S(2)}) collective-permute-start(bf16[8,16,512]{2,1,0:T(8,128)(2,1)S(1)} %collective-permute-done.6), channel_id=1, source_target_pairs={{0,192},{2,50},{16,208},{18,2},{32,224},{34,18},{48,240},{50,34},{... | collective-permute-start | bytes 393224 | tf_op jit(solution)/shard_map/ppermute | solution.py:122
  27.5 17.2 %collective-permute-start.8 = (bf16[8,16,512]{2,1,0:T(8,128)(2,1)S(1)}, bf16[8,16,512]{2,1,0:T(8,128)(2,1)S(1)}, u32[]{:S(2)}, u32[]{:S(2)}) collective-permute-start(bf16[8,16,512]{2,1,0:T(8,128)(2,1)S(1)} %collective-permute-done.6), channel_id=1, source_target_pairs={{0,128},{2,34},{16,144},{18,50},{32,160},{34,2},{48,176},{50,18},{... | collective-permute-start | bytes 393224 | tf_op jit(solution)/shard_map/ppermute | solution.py:122
  31.0 13.6 %collective-permute-start.7 = (bf16[8,16,512]{2,1,0:T(8,128)(2,1)S(1)}, bf16[8,16,512]{2,1,0:T(8,128)(2,1)S(1)}, u32[]{:S(2)}, u32[]{:S(2)}) collective-permute-start(bf16[8,16,512]{2,1,0:T(8,128)(2,1)S(1)} %collective-permute-done.6), channel_id=1, source_target_pairs={{0,64},{2,18},{16,80},{18,34},{32,96},{34,50},{48,112},{50,2},{64,... | collective-permute-start | bytes 393224 | tf_op jit(solution)/shard_map/ppermute | solution.py:122
  33.1 18.1 %copy-start.10 = (f32[16]{0:T(128)S(1)}, f32[16]{0:T(128)}, u32[]{:S(2)}) copy-start(f32[16]{0:T(128)} %param.10) | copy-start | bytes 196
  33.1 18.3 %copy-start.9 = (f32[512]{0:T(512)S(1)}, f32[512]{0:T(512)}, u32[]{:S(2)}) copy-start(f32[512]{0:T(512)} %param.11) | copy-start | bytes 6148
  33.1 40.7 %all-to-all-start = ((bf16[32,4,2,4,512]{4,3,2,1,0:T(4,128)(2,1)}), bf16[32,4,2,4,512]{4,3,2,1,0:T(4,128)(2,1)S(1)}, u32[]{:S(2)}, u32[]{:S(2)}) async-start(bf16[32,4,2,4,512]{4,3,2,1,0:T(4,128)(2,1)} %constant_dynamic-update-slice_fusion), calls=%async_computation | async-start | bytes 2097152 | tf_op jit(solution)/shard_map/all_to_all | solution.py:166
  45.6 19.8 %collective-permute-start.11 = (bf16[4,8,16,512]{3,2,1,0:T(8,128)(2,1)S(1)}, bf16[4,8,16,512]{3,2,1,0:T(8,128)(2,1)S(1)}, u32[]{:S(2)}, u32[]{:S(2)}) collective-permute-start(bf16[4,8,16,512]{3,2,1,0:T(8,128)(2,1)S(1)} %get-tuple-element.18), channel_id=1, source_target_pairs={{0,32},{2,130},{16,48},{18,146},{32,0},{34,162},{48,16},{50,178},{... | collective-permute-start | bytes 1572872 | tf_op jit(solution)/shard_map/ppermute | solution.py:122
  48.5 22.3 %collective-permute-start.10 = (bf16[4,8,16,512]{3,2,1,0:T(8,128)(2,1)S(1)}, bf16[4,8,16,512]{3,2,1,0:T(8,128)(2,1)S(1)}, u32[]{:S(2)}, u32[]{:S(2)}) collective-permute-start(bf16[4,8,16,512]{3,2,1,0:T(8,128)(2,1)S(1)} %get-tuple-element.18), channel_id=1, source_target_pairs={{0,16},{2,66},{16,32},{18,82},{32,48},{34,98},{48,0},{50,114},{64,... | collective-permute-start | bytes 1572872 | tf_op jit(solution)/shard_map/ppermute | solution.py:122
  48.8 21.9 %collective-permute-start.12 = (bf16[4,8,16,512]{3,2,1,0:T(8,128)(2,1)S(1)}, bf16[4,8,16,512]{3,2,1,0:T(8,128)(2,1)}, u32[]{:S(2)}, u32[]{:S(2)}) collective-permute-start(bf16[4,8,16,512]{3,2,1,0:T(8,128)(2,1)S(1)} %get-tuple-element.18), channel_id=1, source_target_pairs={{0,48},{2,194},{16,0},{18,210},{32,16},{34,226},{48,32},{50,242},{... | collective-permute-start | bytes 1572872 | tf_op jit(solution)/shard_map/ppermute | solution.py:122
  51.7 4.4 %collective-permute-start.2 = (bf16[16,1,4,4,256]{4,3,2,1,0:T(4,128)(2,1)}, bf16[16,1,4,4,256]{4,3,2,1,0:T(4,128)(2,1)S(1)}, u32[]{:S(2)}, u32[]{:S(2)}) collective-permute-start(bf16[16,1,4,4,256]{4,3,2,1,0:T(4,128)(2,1)} %get-tuple-element.13), channel_id=1, source_target_pairs={{0,13},{2,15},{4,0},{6,2},{8,4},{10,6},{12,8},{14,10},{1,12},{3,14... | collective-permute-start | bytes 393224 | tf_op jit(solution)/shard_map/ppermute | solution.py:159
  56.1 14.6 %copy-start.6 = (bf16[32,4,2,4,256]{4,3,2,1,0:T(4,128)(2,1)}, bf16[32,4,2,4,256]{4,3,2,1,0:T(4,128)(2,1)S(1)}, u32[]{:S(2)}) copy-start(bf16[32,4,2,4,256]{4,3,2,1,0:T(4,128)(2,1)S(1)} %constant_dynamic-update-slice_fusion.4) | copy-start | bytes 1572868
  65.4 5.3 %copy-start.7 = (bf16[4,8,16,512]{3,2,1,0:T(8,128)(2,1)}, bf16[4,8,16,512]{3,2,1,0:T(8,128)(2,1)S(1)}, u32[]{:S(2)}) copy-start(bf16[4,8,16,512]{3,2,1,0:T(8,128)(2,1)S(1)} %collective-permute-done.11) | copy-start | bytes 1572868
  70.7 0.8 copy-start.8
  73.3 25.2 %collective-permute-start.13 = (bf16[4,4,8,16,512]{4,3,2,1,0:T(8,128)(2,1)S(1)}, bf16[4,4,8,16,512]{4,3,2,1,0:T(8,128)(2,1)}, u32[]{:S(2)}, u32[]{:S(2)}) collective-permute-start(bf16[4,4,8,16,512]{4,3,2,1,0:T(8,128)(2,1)S(1)} %pad_maximum_fusion.near_ref), channel_id=1, source_target_pairs={{0,2},{2,0},{1,3},{3,1},{4,6},{6,4},{5,7},{7,5},{8,10},{10,8},{9,1... | collective-permute-start | bytes 6291464 | tf_op jit(solution)/shard_map/ppermute | solution.py:186
  76.7 17.8 %all-to-all-start.1 = ((bf16[32,4,2,4,256]{4,3,2,1,0:T(4,128)(2,1)}), bf16[32,4,2,4,256]{4,3,2,1,0:T(4,128)(2,1)}, u32[]{:S(2)}, u32[]{:S(2)}) async-start(bf16[32,4,2,4,256]{4,3,2,1,0:T(4,128)(2,1)} %copy-done.6), calls=%async_computation.1 | async-start | bytes 1048576 | tf_op jit(solution)/shard_map/all_to_all | solution.py:166
  81.7 2.2 %copy-start.2 = (bf16[8,512,512]{2,1,0:T(8,128)(2,1)S(1)}, bf16[8,512,512]{2,1,0:T(8,128)(2,1)}, u32[]{:S(2)}) copy-start(bf16[8,512,512]{2,1,0:T(8,128)(2,1)} %vec_ref.1) | copy-start | bytes 12582916
  93.4 1.0 copy-start.3
  98.5 1.0 copy-start.1
  99.5 1.2 %copy-start.4 = (f32[512,512]{1,0:T(8,128)S(1)}, f32[512,512]{1,0:T(8,128)}, u32[]{:S(2)}) copy-start(f32[512,512]{1,0:T(8,128)} %copy-done.3) | copy-start | bytes 3145732

commit v5 on v4

v5 whole, which is shorter than its diff:
```python
import jax
import jax.numpy as jnp
from jax import lax
from jax.experimental import pallas as pl
from jax.experimental.pallas import tpu as pltpu
from jax.sharding import Mesh, PartitionSpec as P

NO = 16
AXES = ("x", "y", "z", "core", "aux")
PAIR = AXES[:4]
SIDE = 4
OWN_LIMIT = 56 * 1024 * 1024
VMEM_LIMIT = 20 * 1024 * 1024
NT = (((1,), (1,)), ((), ()))


def turned(amps_ref, cols):
    nv = cols.shape[1]
    return jnp.concatenate(
        [
            lax.dot_general(amps_ref[p * nv : (p + 1) * nv], cols, NT, preferred_element_type=jnp.float32).astype(jnp.bfloat16)
            for p in range(2)
        ],
        axis=1,
    )


def sum_vectors(nq, ready, vector, columns, amps_ref, right, total_ref, started):
    ready(0)
    right[0] = turned(amps_ref, columns(0))
    for q in range(nq):
        if q + 1 < nq:
            ready(q + 1)
            right[(q + 1) % 2] = turned(amps_ref, columns(q + 1))
        product = jnp.dot(vector(q), right[q % 2], preferred_element_type=jnp.float32)
        total_ref[...] = total_ref[...] + product if q or started else product


def split_pairs(first, second):
    rows = first.shape[1] // 2
    low = lax.broadcasted_iota(jnp.int32, first.shape, 1) < rows
    return (
        jnp.where(low, first, pltpu.roll(second, rows, axis=1)),
        jnp.where(low, pltpu.roll(first, rows, axis=1), second),
    )


def own_kernel(place_ref, got_ref, vec_ref, total_ref, amps_ref, vec, right, sems):
    nq, nv, _ = vec.shape
    half = nv // 2
    copies = [pltpu.make_async_copy(vec_ref.at[q], vec.at[q], sems.at[q]) for q in range(nq)]
    for copy in copies:
        copy.start()
    couples, _, both, _ = got_ref.shape
    chunk = couples // 8
    for i in range(8):
        tiles = [got_ref[pl.ds(i * chunk, chunk), side].astype(jnp.float32) for side in range(2)]
        for p, tile in enumerate(split_pairs(*tiles)):
            rows = chunk * both
            amps_ref[p * nv + i * rows : p * nv + (i + 1) * rows] = tile.reshape(rows, nv).astype(jnp.bfloat16)
    start = pl.multiple_of(place_ref[0] * half, half)
    sum_vectors(
        nq, lambda q: copies[q].wait(), lambda q: vec[q], lambda q: vec[q, pl.ds(start, half), :],
        amps_ref, right, total_ref, False,
    )


def estimate(nq, nv):
    return pl.CostEstimate(flops=4 * nq * nv**3, bytes_accessed=2 * nq * nv * nv, transcendentals=0)


def own_vectors(place, got, cholesky):
    nq, nv, _ = cholesky.shape
    return pl.pallas_call(
        own_kernel,
        in_specs=[
            pl.BlockSpec(memory_space=pltpu.SMEM),
            pl.BlockSpec(memory_space=pltpu.VMEM),
            pl.BlockSpec(memory_space=pltpu.HBM),
        ],
        out_specs=[pl.BlockSpec(memory_space=pltpu.VMEM)] * 2,
        out_shape=[
            jax.ShapeDtypeStruct((nv, nv), jnp.float32),
            jax.ShapeDtypeStruct((2 * nv, nv), jnp.bfloat16),
        ],
        scratch_shapes=[
            pltpu.VMEM((nq, nv, nv), jnp.bfloat16),
            pltpu.VMEM((2, nv, nv), jnp.bfloat16),
            pltpu.SemaphoreType.DMA((nq,)),
        ],
        compiler_params=pltpu.CompilerParams(vmem_limit_bytes=OWN_LIMIT),
        cost_estimate=estimate(16 * nq, nv),
        name="own_vectors",
    )(place, got, cholesky)


def other_kernel(
    place_ref, occ_ref, amps_ref, near_ref, far_ref, base_ref, hole_ref, rows_ref, cols_ref, out_ref, vec, total, right, sems
):
    nq, slots, strip, nv = vec.shape
    half, part = nv // 2, nq // 2
    core, x0, y0 = place_ref[1], place_ref[2], place_ref[3]

    fill = pltpu.make_async_copy(base_ref, total, sems.at[2])
    fill.start()
    for h in range(2):
        for owner, src in ((core, near_ref), (1 - core, far_ref)):
            for outer in range(SIDE):
                for inner in range(SIDE):
                    dx = inner + owner * (outer - inner)
                    dy = outer + owner * (inner - outer)
                    x, y = lax.rem(x0 + SIDE - dx, SIDE), lax.rem(y0 + SIDE - dy, SIDE)
                    pltpu.make_async_copy(
                        src.at[outer, inner, pl.ds(h * part, part)],
                        vec.at[pl.ds(h * part, part), (owner * SIDE + x) * SIDE + y],
                        sems.at[h],
                    ).start()
    def ready(q):
        if q % part == 0:
            block = vec.at[pl.ds(q, part)]
            pltpu.make_async_copy(block, block, sems.at[q // part]).wait()

    fill.wait()
    sum_vectors(
        nq, ready, lambda q: vec[q].reshape(nv, nv),
        lambda q: vec[q, pl.ds(place_ref[0] * (slots // 2), slots // 2)].reshape(half, nv),
        amps_ref, right, total, True,
    )
    level = rows_ref[...] + cols_ref[...]
    cells, _, planes, both, width = hole_ref.shape
    tiles = [
        hole_ref[:, side].astype(jnp.float32).reshape(cells * planes, both, width) for side in range(2)
    ]
    holes = split_pairs(*tiles)
    for p in range(out_ref.shape[0]):
        value = holes[p].reshape(nv, half) + total[:, p * half : (p + 1) * half]
        out_ref[p] = value / (level - occ_ref[p])


def other_vectors(place, occ_sum, amps, near, far, base, hole, rows, cols):
    nq, strip, nv = near.shape[2:]
    vmem = pl.BlockSpec(memory_space=pltpu.VMEM)
    smem = pl.BlockSpec(memory_space=pltpu.SMEM)
    anywhere = pl.BlockSpec(memory_space=pl.ANY)
    return pl.pallas_call(
        other_kernel,
        in_specs=[smem, smem, vmem, anywhere, anywhere, anywhere, vmem, vmem, vmem],
        out_specs=vmem,
        out_shape=jax.ShapeDtypeStruct((2, nv, nv // 2), jnp.float32),
        scratch_shapes=[
            pltpu.VMEM((nq, nv // strip, strip, nv), jnp.bfloat16),
            pltpu.VMEM((nv, nv), jnp.float32),
            pltpu.VMEM((2, nv, nv), jnp.bfloat16),
            pltpu.SemaphoreType.DMA((3,)),
        ],
        compiler_params=pltpu.CompilerParams(vmem_limit_bytes=VMEM_LIMIT),
        cost_estimate=estimate(nq, nv),
        name="other_vectors",
    )(place, occ_sum, amps, near, far, base, hole, rows, cols)


def plane_shift(block, shift, first_core_axis):
    pairs = []
    for x in range(SIDE):
        for y in range(SIDE):
            for core in range(2):
                if core == first_core_axis:
                    to = x * SIDE + (y + shift) % SIDE
                else:
                    to = (x + shift) % SIDE * SIDE + y
                pairs.append(((x * SIDE + y) * 2 + core, to * 2 + core))
    return lax.ppermute(block, ("x", "y", "core"), pairs)


def gather_plane(block):
    for stage in range(2):
        block = jnp.stack([block] + [plane_shift(block, d, 1 - stage) for d in (1, 2, 3)])
    return block


def ring_pairs(step):
    steps = {1: (1, 1), 3: (-1, -1), 2: (2, -2)}[step]
    pairs = []
    for z8 in range(2 * SIDE):
        for core in range(2):
            to = (z8 + steps[core]) % (2 * SIDE)
            pairs.append(((z8 % SIDE * 2 + core) * 2 + z8 // SIDE, (to % SIDE * 2 + core) * 2 + to // SIDE))
    return pairs


def ring_target(z8, core, step):
    move = {0: 0, 1: 1, 3: -1}.get(step)
    move = 2 - 4 * core if move is None else move
    return lax.rem(z8 + move + 2 * SIDE, 2 * SIDE)


def spread(hole, width, z, core, aux, after):
    n_pair, rows, full = hole.shape
    cells, each = SIDE * SIDE, n_pair // (2 * SIDE**3)
    view = hole.reshape(cells, SIDE, 2, each * rows, full)
    packed = jnp.zeros((2 * cells, SIDE, each * rows, width), hole.dtype)
    for step in range(SIDE):
        target = ring_target(aux * SIDE + z, core, step)
        column = lax.div(target, SIDE) * width
        block = lax.dynamic_slice(
            view, (0, lax.rem(target, SIDE), 0, 0, column), (cells, 1, 2, each * rows, width)
        )
        if step:
            block = lax.ppermute(block, ("z", "core", "aux"), ring_pairs(step))
        block = block.reshape(2 * cells, 1, each * rows, width)
        packed = lax.dynamic_update_slice(packed, block, (0, lax.rem(z + SIDE - step, SIDE), 0, 0))
    packed, after = lax.optimization_barrier((packed, after))
    got = lax.all_to_all(packed, ("x", "y", "core"), split_axis=0, concat_axis=0, tiled=True)
    return got.reshape(cells, 2, SIDE, each * rows, width), after


def shards(amplitudes, ladder, cholesky, pair_ids, occ_energy, vir_energy):
    n_pair, rows, n_virt = amplitudes.shape
    half_width = n_virt // lax.axis_size("aux")
    aux, core, z = lax.axis_index("aux"), lax.axis_index("core"), lax.axis_index("z")
    x, y = lax.axis_index("x"), lax.axis_index("y")
    strip = half_width // (SIDE * SIDE)

    slot = (core * SIDE + x) * SIDE + y
    piece = lax.dynamic_slice_in_dim(cholesky, slot * strip, strip, 1)
    piece = lax.ppermute(piece, "aux", [(0, 1), (1, 0)])
    hole = jnp.dot(
        ladder, amplitudes.reshape(n_pair, -1), preferred_element_type=jnp.float32
    ).astype(jnp.bfloat16).reshape(amplitudes.shape)
    packed = amplitudes.reshape(n_pair // 2, 2 * rows, n_virt)
    packed, piece, hole = lax.optimization_barrier((packed, piece, hole))
    near = gather_plane(piece)
    far = lax.ppermute(near, "core", [(0, 1), (1, 0)])

    got_amps = lax.all_to_all(packed, PAIR, split_axis=0, concat_axis=0, tiled=True)
    pair_hole, got_amps = spread(hole, half_width, z, core, aux, got_amps)
    got_amps = got_amps.reshape(n_pair // 4, 2, 2 * rows, n_virt)

    orbitals = jnp.arange(NO, dtype=jnp.int32)
    first_hot = (pair_ids[:, None] // NO == orbitals[None, :]).astype(jnp.float32)
    second_hot = (pair_ids[:, None] % NO == orbitals[None, :]).astype(jnp.float32)
    occ_sum = jnp.sum((first_hot + second_hot) * occ_energy[None, :], axis=1)
    vir_cols = lax.dynamic_slice_in_dim(vir_energy, aux * half_width, half_width, 0)
    place = jnp.stack([aux, core, x, y]).astype(jnp.int32)

    base, pair_amps = own_vectors(place, got_amps, cholesky)
    return other_vectors(
        place, occ_sum, pair_amps, near, far, base, pair_hole, vir_energy[:, None], vir_cols[None, :]
    )


def solution(mesh):
    fine = Mesh(mesh.devices.reshape(SIDE, SIDE, SIDE, 2, 2), AXES)
    in_specs = (P(None, PAIR, None), P(), P("aux", None, None), P(PAIR), P(), P())
    out_specs = P(PAIR, None, "aux")
    return jax.shard_map(shards, mesh=fine, in_specs=in_specs, out_specs=out_specs, check_vma=False)
```

time: 110 us -> 90.2 us (0.82)
  local copies, waits for them, and re-layouts: 27.5 us -> 11.8 us
  waiting for transfers between devices: 19.5 us -> 15.8 us
  starting transfers between devices: 40.5 us -> 42.2 us
  Pallas kernels: 18.3 us -> 16.6 us
    all_to_all x0 -> x1, starting transfers between devices: none -> 13.3 us  [shards(): lax.all_to_all(packed, PAIR, split_axis=0, concat_axis=0, tiled=True)]
    all_to_all x2 -> x1, starting transfers between devices: 16.2 us -> 5.67 us  [spread(): lax.all_to_all(packed, ('x', 'y', 'core'), split_axis=0, concat_axis=0, t...]
    ppermute x6, waiting for transfers between devices: 14.6 us -> 8.75 us  [plane_shift(): return lax.ppermute(block, ('x', 'y', 'core'), pairs)]
    dynamic_update_slice x8 -> x4, local copies, waits for them, and re-layouts: 7.14 us -> 2.74 us  [spread(): lax.dynamic_update_slice(packed, block, (0, lax.rem(z + SIDE - step, SIDE...]
    transpose x2 -> x0, local copies, waits for them, and re-layouts: 3.66 us -> none  [by_pair(): got.reshape(cells, 2, planes, each, rows, width).transpose(3, 0, 2, 1, 4, 5)]
    all_to_all x2 -> x1, waiting for transfers between devices: 0.01 us -> 3.05 us  [spread(): lax.all_to_all(packed, ('x', 'y', 'core'), split_axis=0, concat_axis=0, t...]
    ppermute x6, starting transfers between devices: 11.4 us -> 8.39 us  [plane_shift(): return lax.ppermute(block, ('x', 'y', 'core'), pairs)]
    dynamic_slice x2 -> x0, local copies, waits for them, and re-layouts: 2.55 us -> none  [spread(): lax.dynamic_slice(view, (0, lax.rem(target, SIDE), 0, 0, column), (cells,...]
  transfers between devices with their start and end apart: 16 -> 13, of which waited for: 4 -> 5; matrix products, arithmetic and copies ran while one was open for 21% -> 12% of each run, Pallas kernels for 9% -> 10%
where the time goes in v5:
time: 90.2 us; the launch traced here: 89.7 us
  starting transfers between devices  42.2 us (47%)
  Pallas kernels  16.6 us (18%)
  waiting for transfers between devices  15.8 us (18%)
  local copies, waits for them, and re-layouts  11.8 us (13%)
  other arithmetic  2.4 us (3%)
    all_to_all x1, starting transfers between devices, shards(): lax.all_to_all(packed, PAIR, split_axis=0, concat_axis=0, tiled=True)  13.3 us
    ppermute x6, waiting for transfers between devices, plane_shift(): return lax.ppermute(block, ('x', 'y', 'core'), pairs)  8.75 us
    pallas_call x1, Pallas kernels, own_vectors(): pl.pallas_call(own_kernel, in_specs=[pl.BlockSpec(memory_space=pltpu.SMEM...  8.55 us
    ppermute x6, starting transfers between devices, plane_shift(): return lax.ppermute(block, ('x', 'y', 'core'), pairs)  8.39 us
    pallas_call x1, Pallas kernels, other_vectors(): pl.pallas_call(other_kernel, in_specs=[smem, smem, vmem, anywhere, anywhe...  8.02 us
    ppermute x1, starting transfers between devices, shards(): piece = lax.ppermute(piece, 'aux', [(0, 1), (1, 0)])  7.83 us
    ppermute x3, starting transfers between devices, spread(): block = lax.ppermute(block, ('z', 'core', 'aux'), ring_pairs(step))  6.93 us
    all_to_all x1, starting transfers between devices, spread(): lax.all_to_all(packed, ('x', 'y', 'core'), split_axis=0, concat_axis=0, t...  5.67 us
  transfers between devices with their start and end apart: 13, of which 5 were waited for; matrix products, arithmetic and copies ran while one was open for 12% of the time, Pallas kernels for 10%

profile of v5, /device:TPU:1, one launch (start us, length us, event | category | flops | bytes accessed | tf_op | source)
XLA Modules:
  0.0 89.7 jit_solution(17118318984559119488)
XLA Ops:
  0.0 0.9 %constant_dynamic-slice_fusion.1 = bf16[8,16,512]{2,1,0:T(8,128)(2,1)S(1)} fusion(bf16[8,512,512]{2,1,0:T(8,128)(2,1)} %vec_ref.1, s32[]{:T(128)S(6)} %select_n.58), kind=kLoop, calls=%fused_computation.11 | loop fusion | bytes 262148 | tf_op jit(solution)/shard_map/dynamic_slice | solution.py:225
  1.0 7.8 %collective-permute-start = (bf16[8,16,512]{2,1,0:T(8,128)(2,1)S(1)}, bf16[8,16,512]{2,1,0:T(8,128)(2,1)S(1)}, u32[]{:S(2)}, u32[]{:S(2)}) collective-permute-start(bf16[8,16,512]{2,1,0:T(8,128)(2,1)S(1)} %constant_dynamic-slice_fusion.1), channel_id=1, source_target_pairs={{0,1},{1,0},{2,3},{3,2},{4,5},{5,4},{6,7},{7,6},{8,9},{9,8},{10,11... | collective-permute-start | bytes 393224 | tf_op jit(solution)/shard_map/ppermute | solution.py:226
  8.8 1.6 %copy.25 = bf16[32,8,4,512]{3,1,2,0:T(8,128)(2,1)S(1)} copy(bf16[32,8,4,512]{3,2,1,0:T(4,128)(2,1)} %bitcast.35) | data formatting | bytes 2097152
  10.8 1.1 %reshape.57 = bf16[128,8,512]{2,1,0:T(8,128)(2,1)} reshape(bf16[256,4,512]{2,1,0:T(4,128)(2,1)S(1)} %copy-done.4) | data formatting | bytes 2097152 | tf_op jit(solution)/shard_map/reshape | solution.py:230
  12.0 0.8 reshape.59
  12.8 13.3 %all-to-all-start = ((bf16[128,8,512]{2,1,0:T(8,128)(2,1)}), bf16[128,8,512]{2,1,0:T(8,128)(2,1)}, u32[]{:S(2)}, u32[]{:S(2)}) async-start(bf16[128,8,512]{2,1,0:T(8,128)(2,1)} %reshape.57), calls=%async_computation | async-start | bytes 2097152 | tf_op jit(solution)/shard_map/all_to_all | solution.py:235
  26.1 2.7 %collective-permute-start.6 = (bf16[8,16,512]{2,1,0:T(8,128)(2,1)S(1)}, bf16[8,16,512]{2,1,0:T(8,128)(2,1)S(1)}, u32[]{:S(2)}, u32[]{:S(2)}) collective-permute-start(bf16[8,16,512]{2,1,0:T(8,128)(2,1)S(1)} %collective-permute-done), channel_id=1, source_target_pairs={{0,192},{2,50},{16,208},{18,2},{32,224},{34,18},{48,240},{50,34},{... | collective-permute-start | bytes 393224 | tf_op jit(solution)/shard_map/ppermute | solution.py:172
  28.8 0.5 collective-permute-start.5
  29.4 0.6 collective-permute-start.4
  30.5 0.8 dynamic-slice_bitcast_fusion
  31.3 1.2 %collective-permute-start.1 = (bf16[16,1,2,8,256]{4,3,2,0,1:T(8,128)(2,1)}, bf16[16,1,2,8,256]{4,3,2,0,1:T(8,128)(2,1)S(1)}, u32[]{:S(2)}, u32[]{:S(2)}) collective-permute-start(bf16[16,1,2,8,256]{4,3,2,0,1:T(8,128)(2,1)} %get-tuple-element.21), channel_id=1, source_target_pairs={{0,4},{2,6},{4,8},{6,10},{8,12},{10,14},{12,1},{14,3},{1,5},{3,7},... | collective-permute-start | bytes 393224 | tf_op jit(solution)/shard_map/ppermute | solution.py:209
  32.5 4.3 %collective-permute-done.6 = bf16[8,16,512]{2,1,0:T(8,128)(2,1)S(1)} collective-permute-done((bf16[8,16,512]{2,1,0:T(8,128)(2,1)S(1)}, bf16[8,16,512]{2,1,0:T(8,128)(2,1)S(1)}, u32[]{:S(2)}, u32[]{:S(2)}) %collective-permute-start.6) | collective-permute-done | bytes 131104 | tf_op jit(solution)/shard_map/ppermute | solution.py:172
  36.8 1.5 %collective-permute-done.5 = bf16[8,16,512]{2,1,0:T(8,128)(2,1)S(1)} collective-permute-done((bf16[8,16,512]{2,1,0:T(8,128)(2,1)S(1)}, bf16[8,16,512]{2,1,0:T(8,128)(2,1)S(1)}, u32[]{:S(2)}, u32[]{:S(2)}) %collective-permute-start.5) | collective-permute-done | bytes 131104 | tf_op jit(solution)/shard_map/ppermute | solution.py:172
  38.4 2.9 %collective-permute-done.4 = bf16[8,16,512]{2,1,0:T(8,128)(2,1)S(1)} collective-permute-done((bf16[8,16,512]{2,1,0:T(8,128)(2,1)S(1)}, bf16[8,16,512]{2,1,0:T(8,128)(2,1)S(1)}, u32[]{:S(2)}, u32[]{:S(2)}) %collective-permute-start.4) | collective-permute-done | bytes 131104 | tf_op jit(solution)/shard_map/ppermute | solution.py:172
  41.3 1.9 %collective-permute-start.8 = (bf16[4,8,16,512]{3,2,1,0:T(8,128)(2,1)S(1)}, bf16[4,8,16,512]{3,2,1,0:T(8,128)(2,1)S(1)}, u32[]{:S(2)}, u32[]{:S(2)}) collective-permute-start(bf16[4,8,16,512]{3,2,1,0:T(8,128)(2,1)S(1)} %get-tuple-element.24), channel_id=1, source_target_pairs={{0,32},{2,130},{16,48},{18,146},{32,0},{34,162},{48,16},{50,178},{... | collective-permute-start | bytes 1572872 | tf_op jit(solution)/shard_map/ppermute | solution.py:172
  43.6 2.2 %collective-permute-start.9 = (bf16[4,8,16,512]{3,2,1,0:T(8,128)(2,1)S(1)}, bf16[4,8,16,512]{3,2,1,0:T(8,128)(2,1)}, u32[]{:S(2)}, u32[]{:S(2)}) collective-permute-start(bf16[4,8,16,512]{3,2,1,0:T(8,128)(2,1)S(1)} %get-tuple-element.24), channel_id=1, source_target_pairs={{0,48},{2,194},{16,0},{18,210},{32,16},{34,226},{48,32},{50,242},{... | collective-permute-start | bytes 1572872 | tf_op jit(solution)/shard_map/ppermute | solution.py:172
  45.9 0.7 pad_add_fusion.place_ref
  46.8 4.3 %collective-permute-start.2 = (bf16[16,1,2,8,256]{4,3,2,0,1:T(8,128)(2,1)}, bf16[16,1,2,8,256]{4,3,2,0,1:T(8,128)(2,1)S(1)}, u32[]{:S(2)}, u32[]{:S(2)}) collective-permute-start(bf16[16,1,2,8,256]{4,3,2,0,1:T(8,128)(2,1)} %get-tuple-element.20), channel_id=1, source_target_pairs={{0,8},{2,11},{4,12},{6,15},{8,1},{10,2},{12,5},{14,6},{1,9},{3,10}... | collective-permute-start | bytes 393224 | tf_op jit(solution)/shard_map/ppermute | solution.py:209
  51.1 0.9 broadcast_in_dim.6
  51.9 0.7 constant_dynamic-update-slice_fusion.3
  52.6 1.5 %collective-permute-start.3 = (bf16[16,1,2,8,256]{4,3,2,0,1:T(8,128)(2,1)S(1)}, bf16[16,1,2,8,256]{4,3,2,0,1:T(8,128)(2,1)S(1)}, u32[]{:S(2)}, u32[]{:S(2)}) collective-permute-start(bf16[16,1,2,8,256]{4,3,2,0,1:T(8,128)(2,1)S(1)} %get-tuple-element.19), channel_id=1, source_target_pairs={{0,13},{2,15},{4,0},{6,2},{8,4},{10,6},{12,8},{14,10},{1,12},{3,14... | collective-permute-start | bytes 393224 | tf_op jit(solution)/shard_map/ppermute | solution.py:209
  54.1 0.7 constant_dynamic-update-slice_fusion.2
  54.8 0.7 constant_dynamic-update-slice_fusion.1
  55.5 4.0 %collective-permute-done.3 = bf16[16,1,2,8,256]{4,3,2,0,1:T(8,128)(2,1)S(1)} collective-permute-done((bf16[16,1,2,8,256]{4,3,2,0,1:T(8,128)(2,1)S(1)}, bf16[16,1,2,8,256]{4,3,2,0,1:T(8,128)(2,1)S(1)}, u32[]{:S(2)}, u32[]{:S(2)}) %collective-permute-start.3) | collective-permute-done | bytes 131104 | tf_op jit(solution)/shard_map/ppermute | solution.py:209
  59.5 0.7 constant_dynamic-update-slice_fusion
  60.2 1.5 %pad_maximum_fusion.near_ref = bf16[4,4,8,16,512]{4,3,2,1,0:T(8,128)(2,1)S(1)} fusion(bf16[1,4,8,16,512]{4,3,2,1,0:T(8,128)(2,1)} %bitcast.16, bf16[1,4,8,16,512]{4,3,2,1,0:T(8,128)(2,1)S(1)} %bitcast.38, bf16[1,4,8,16,512]{4,3,2,1,0:T(8,128)(2,1)} %bitcast.14, bf16[1,4,8,16,512]{4,3,2,1,0:T(8,128)(2,1)S(1)} %get-tuple-element.23), kind=kLoop, calls=%fused_computation.1 | loop fusion | flops 3145728 | bytes 4194304 | tf_op jit(solution)/shard_map/stack | solution.py:177
  61.8 5.7 %all-to-all-start.1 = ((bf16[32,4,8,256]{3,2,1,0:T(8,128)(2,1)}), bf16[32,4,8,256]{3,2,1,0:T(8,128)(2,1)S(1)}, u32[]{:S(2)}, u32[]{:S(2)}) async-start(bf16[32,4,8,256]{3,2,1,0:T(8,128)(2,1)} %constant_dynamic-update-slice_fusion), calls=%async_computation.1 | async-start | bytes 1048576 | tf_op jit(solution)/shard_map/all_to_all | solution.py:213
  67.4 8.6 %own_vectors.1 = (f32[512,512]{1,0:T(8,128)}, bf16[1024,512]{1,0:T(8,128)(2,1)}) custom-call(s32[4]{0:T(128)} %pad_add_fusion.place_ref, bf16[64,2,8,512]{3,2,1,0:T(8,128)(2,1)} %bitcast.8.got_ref, bf16[8,512,512]{2,1,0:T(8,128)(2,1)} %vec_ref.1), custom_call_target="tpu_custom_call" | custom-call | flops 68719476736 | bytes 67108864 | tf_op jit(solution)/shard_map/own_vectors/pallas_call | solution.py:74
  76.0 3.1 %all-to-all-done.1 = bf16[32,4,8,256]{3,2,1,0:T(8,128)(2,1)S(1)} async-done(((bf16[32,4,8,256]{3,2,1,0:T(8,128)(2,1)}), bf16[32,4,8,256]{3,2,1,0:T(8,128)(2,1)S(1)}, u32[]{:S(2)}, u32[]{:S(2)}) %all-to-all-start.1) | async-done | bytes 524320 | tf_op jit(solution)/shard_map/all_to_all | solution.py:213
  79.1 1.2 %copy-done.2 = f32[512,512]{1,0:T(8,128)S(1)} copy-done((f32[512,512]{1,0:T(8,128)S(1)}, f32[512,512]{1,0:T(8,128)}, u32[]{:S(2)}) %copy-start.2) | copy-done | bytes 1048600
  80.3 1.2 %copy-done.3 = bf16[1024,512]{1,0:T(8,128)(2,1)S(1)} copy-done((bf16[1024,512]{1,0:T(8,128)(2,1)S(1)}, bf16[1024,512]{1,0:T(8,128)(2,1)}, u32[]{:S(2)}) %copy-start.3) | copy-done | bytes 1048600
  81.5 8.0 %other_vectors.1 = f32[2,512,256]{2,1,0:T(8,128)} custom-call(s32[4]{0:T(128)S(1)} %copy-done.1, f32[2]{0:T(128)S(1)} %fusion.2.occ_ref, bf16[1024,512]{1,0:T(8,128)(2,1)S(1)} %copy-done.3, bf16[4,4,8,16,512]{4,3,2,1,0:T(8,128)(2,1)S(1)} %pad_maximum_fusion.near_ref, bf16[4,4,8,16,512]{4,3,2,1,0:T(8,128)(2,1)} %collective-permute-done.10.far_ref, ...), custom_call_target="tpu_custom_call" | custom-call | flops 4294967296 | bytes 4194304 | tf_op jit(solution)/shard_map/other_vectors/pallas_call | solution.py:145
  (31 shorter events, 1.8 us)
Async XLA Ops:
  0.0 10.4 %copy-start = (bf16[256,256]{1,0:T(8,128)(2,1)S(1)}, bf16[256,256]{1,0:T(8,128)(2,1)}, u32[]{:S(2)}) copy-start(bf16[256,256]{1,0:T(8,128)(2,1)} %param.7) | copy-start | bytes 393220
  1.0 11.8 %collective-permute-start = (bf16[8,16,512]{2,1,0:T(8,128)(2,1)S(1)}, bf16[8,16,512]{2,1,0:T(8,128)(2,1)S(1)}, u32[]{:S(2)}, u32[]{:S(2)}) collective-permute-start(bf16[8,16,512]{2,1,0:T(8,128)(2,1)S(1)} %constant_dynamic-slice_fusion.1), channel_id=1, source_target_pairs={{0,1},{1,0},{2,3},{3,2},{4,5},{5,4},{6,7},{7,6},{8,9},{9,8},{10,11... | collective-permute-start | bytes 393224 | tf_op jit(solution)/shard_map/ppermute | solution.py:226
  8.8 2.0 %copy-start.4 = (bf16[256,4,512]{2,1,0:T(4,128)(2,1)S(1)}, bf16[256,4,512]{2,1,0:T(4,128)(2,1)}, u32[]{:S(2)}) copy-start(bf16[256,4,512]{2,1,0:T(4,128)(2,1)} %param.6) | copy-start | bytes 3145732
  11.9 14.1 %copy-start.7 = (s32[2]{0:T(128)S(1)}, s32[2]{0:T(128)}, u32[]{:S(2)}) copy-start(s32[2]{0:T(128)} %param.9) | copy-start | bytes 28
  11.9 18.0 %copy-start.6 = (f32[16]{0:T(128)S(1)}, f32[16]{0:T(128)}, u32[]{:S(2)}) copy-start(f32[16]{0:T(128)} %param.10) | copy-start | bytes 196
  12.8 49.0 %all-to-all-start = ((bf16[128,8,512]{2,1,0:T(8,128)(2,1)}), bf16[128,8,512]{2,1,0:T(8,128)(2,1)}, u32[]{:S(2)}, u32[]{:S(2)}) async-start(bf16[128,8,512]{2,1,0:T(8,128)(2,1)} %reshape.57), calls=%async_computation | async-start | bytes 2097152 | tf_op jit(solution)/shard_map/all_to_all | solution.py:235
  26.1 10.7 %collective-permute-start.6 = (bf16[8,16,512]{2,1,0:T(8,128)(2,1)S(1)}, bf16[8,16,512]{2,1,0:T(8,128)(2,1)S(1)}, u32[]{:S(2)}, u32[]{:S(2)}) collective-permute-start(bf16[8,16,512]{2,1,0:T(8,128)(2,1)S(1)} %collective-permute-done), channel_id=1, source_target_pairs={{0,192},{2,50},{16,208},{18,2},{32,224},{34,18},{48,240},{50,34},{... | collective-permute-start | bytes 393224 | tf_op jit(solution)/shard_map/ppermute | solution.py:172
  28.8 9.5 %collective-permute-start.5 = (bf16[8,16,512]{2,1,0:T(8,128)(2,1)S(1)}, bf16[8,16,512]{2,1,0:T(8,128)(2,1)S(1)}, u32[]{:S(2)}, u32[]{:S(2)}) collective-permute-start(bf16[8,16,512]{2,1,0:T(8,128)(2,1)S(1)} %collective-permute-done), channel_id=1, source_target_pairs={{0,128},{2,34},{16,144},{18,50},{32,160},{34,2},{48,176},{50,18},{... | collective-permute-start | bytes 393224 | tf_op jit(solution)/shard_map/ppermute | solution.py:172
  29.4 11.9 %collective-permute-start.4 = (bf16[8,16,512]{2,1,0:T(8,128)(2,1)S(1)}, bf16[8,16,512]{2,1,0:T(8,128)(2,1)S(1)}, u32[]{:S(2)}, u32[]{:S(2)}) collective-permute-start(bf16[8,16,512]{2,1,0:T(8,128)(2,1)S(1)} %collective-permute-done), channel_id=1, source_target_pairs={{0,64},{2,18},{16,80},{18,34},{32,96},{34,50},{48,112},{50,2},{64,... | collective-permute-start | bytes 393224 | tf_op jit(solution)/shard_map/ppermute | solution.py:172
  30.2 16.3 %copy-start.5 = (f32[512]{0:T(512)S(1)}, f32[512]{0:T(512)}, u32[]{:S(2)}) copy-start(f32[512]{0:T(512)} %param.11) | copy-start | bytes 6148
  31.3 21.3 %collective-permute-start.1 = (bf16[16,1,2,8,256]{4,3,2,0,1:T(8,128)(2,1)}, bf16[16,1,2,8,256]{4,3,2,0,1:T(8,128)(2,1)S(1)}, u32[]{:S(2)}, u32[]{:S(2)}) collective-permute-start(bf16[16,1,2,8,256]{4,3,2,0,1:T(8,128)(2,1)} %get-tuple-element.21), channel_id=1, source_target_pairs={{0,4},{2,6},{4,8},{6,10},{8,12},{10,14},{12,1},{14,3},{1,5},{3,7},... | collective-permute-start | bytes 393224 | tf_op jit(solution)/shard_map/ppermute | solution.py:209
  41.3 18.8 %collective-permute-start.8 = (bf16[4,8,16,512]{3,2,1,0:T(8,128)(2,1)S(1)}, bf16[4,8,16,512]{3,2,1,0:T(8,128)(2,1)S(1)}, u32[]{:S(2)}, u32[]{:S(2)}) collective-permute-start(bf16[4,8,16,512]{3,2,1,0:T(8,128)(2,1)S(1)} %get-tuple-element.24), channel_id=1, source_target_pairs={{0,32},{2,130},{16,48},{18,146},{32,0},{34,162},{48,16},{50,178},{... | collective-permute-start | bytes 1572872 | tf_op jit(solution)/shard_map/ppermute | solution.py:172
  43.2 17.0 %collective-permute-start.7 = (bf16[4,8,16,512]{3,2,1,0:T(8,128)(2,1)S(1)}, bf16[4,8,16,512]{3,2,1,0:T(8,128)(2,1)}, u32[]{:S(2)}, u32[]{:S(2)}) collective-permute-start(bf16[4,8,16,512]{3,2,1,0:T(8,128)(2,1)S(1)} %get-tuple-element.24), channel_id=1, source_target_pairs={{0,16},{2,66},{16,32},{18,82},{32,48},{34,98},{48,0},{50,114},{64,... | collective-permute-start | bytes 1572872 | tf_op jit(solution)/shard_map/ppermute | solution.py:172
  43.6 16.5 %collective-permute-start.9 = (bf16[4,8,16,512]{3,2,1,0:T(8,128)(2,1)S(1)}, bf16[4,8,16,512]{3,2,1,0:T(8,128)(2,1)}, u32[]{:S(2)}, u32[]{:S(2)}) collective-permute-start(bf16[4,8,16,512]{3,2,1,0:T(8,128)(2,1)S(1)} %get-tuple-element.24), channel_id=1, source_target_pairs={{0,48},{2,194},{16,0},{18,210},{32,16},{34,226},{48,32},{50,242},{... | collective-permute-start | bytes 1572872 | tf_op jit(solution)/shard_map/ppermute | solution.py:172
  46.8 8.0 %collective-permute-start.2 = (bf16[16,1,2,8,256]{4,3,2,0,1:T(8,128)(2,1)}, bf16[16,1,2,8,256]{4,3,2,0,1:T(8,128)(2,1)S(1)}, u32[]{:S(2)}, u32[]{:S(2)}) collective-permute-start(bf16[16,1,2,8,256]{4,3,2,0,1:T(8,128)(2,1)} %get-tuple-element.20), channel_id=1, source_target_pairs={{0,8},{2,11},{4,12},{6,15},{8,1},{10,2},{12,5},{14,6},{1,9},{3,10}... | collective-permute-start | bytes 393224 | tf_op jit(solution)/shard_map/ppermute | solution.py:209
  52.6 6.8 %collective-permute-start.3 = (bf16[16,1,2,8,256]{4,3,2,0,1:T(8,128)(2,1)S(1)}, bf16[16,1,2,8,256]{4,3,2,0,1:T(8,128)(2,1)S(1)}, u32[]{:S(2)}, u32[]{:S(2)}) collective-permute-start(bf16[16,1,2,8,256]{4,3,2,0,1:T(8,128)(2,1)S(1)} %get-tuple-element.19), channel_id=1, source_target_pairs={{0,13},{2,15},{4,0},{6,2},{8,4},{10,6},{12,8},{14,10},{1,12},{3,14... | collective-permute-start | bytes 393224 | tf_op jit(solution)/shard_map/ppermute | solution.py:209
  61.6 17.4 %collective-permute-start.10 = (bf16[4,4,8,16,512]{4,3,2,1,0:T(8,128)(2,1)S(1)}, bf16[4,4,8,16,512]{4,3,2,1,0:T(8,128)(2,1)}, u32[]{:S(2)}, u32[]{:S(2)}) collective-permute-start(bf16[4,4,8,16,512]{4,3,2,1,0:T(8,128)(2,1)S(1)} %pad_maximum_fusion.near_ref), channel_id=1, source_target_pairs={{0,2},{2,0},{1,3},{3,1},{4,6},{6,4},{5,7},{7,5},{8,10},{10,8},{9,1... | collective-permute-start | bytes 6291464 | tf_op jit(solution)/shard_map/ppermute | solution.py:233
  61.8 17.3 %all-to-all-start.1 = ((bf16[32,4,8,256]{3,2,1,0:T(8,128)(2,1)}), bf16[32,4,8,256]{3,2,1,0:T(8,128)(2,1)S(1)}, u32[]{:S(2)}, u32[]{:S(2)}) async-start(bf16[32,4,8,256]{3,2,1,0:T(8,128)(2,1)} %constant_dynamic-update-slice_fusion), calls=%async_computation.1 | async-start | bytes 1048576 | tf_op jit(solution)/shard_map/all_to_all | solution.py:213
  67.4 11.6 %copy-start.1 = (s32[4]{0:T(128)S(1)}, s32[4]{0:T(128)}, u32[]{:S(2)}) copy-start(s32[4]{0:T(128)} %pad_add_fusion.place_ref) | copy-start | bytes 52
  79.1 1.2 %copy-start.2 = (f32[512,512]{1,0:T(8,128)S(1)}, f32[512,512]{1,0:T(8,128)}, u32[]{:S(2)}) copy-start(f32[512,512]{1,0:T(8,128)} %get-tuple-element.17.base_ref) | copy-start | bytes 3145732
  80.3 1.2 %copy-start.3 = (bf16[1024,512]{1,0:T(8,128)(2,1)S(1)}, bf16[1024,512]{1,0:T(8,128)(2,1)}, u32[]{:S(2)}) copy-start(bf16[1024,512]{1,0:T(8,128)(2,1)} %get-tuple-element.15.amps_ref) | copy-start | bytes 3145732

commit v6 on v0

v6 whole, which is shorter than its diff:
```python
import jax
import jax.numpy as jnp
from jax import lax
from jax.experimental import pallas as pl
from jax.experimental.pallas import tpu as pltpu
from jax.sharding import Mesh, PartitionSpec as P

NO = 16
AXES = ("x", "y", "z", "core", "aux")
PAIR = AXES[:4]
SIDE = 4
VMEM_LIMIT = 56 * 1024 * 1024
NT = (((1,), (1,)), ((), ()))


def turned(amps_ref, cols):
    nv = cols.shape[1]
    return jnp.concatenate(
        [
            lax.dot_general(amps_ref[p * nv : (p + 1) * nv], cols, NT, preferred_element_type=jnp.float32).astype(jnp.bfloat16)
            for p in range(2)
        ],
        axis=1,
    )


def split_pairs(first, second):
    rows = first.shape[1] // 2
    low = lax.broadcasted_iota(jnp.int32, first.shape, 1) < rows
    return (
        jnp.where(low, first, pltpu.roll(second, rows, axis=1)),
        jnp.where(low, pltpu.roll(first, rows, axis=1), second),
    )


def particle_kernel(
    place_ref, occ_ref, got_hbm, own_hbm, near_hbm, far_hbm, rows_ref, cols_ref, out_hbm,
    got_ref, amps_ref, own, other, right, total, out_ref, sems,
):
    nq, nv, _ = own.shape
    half, part = nv // 2, nq // 2
    slots = other.shape[1]
    aux, core, x0, y0 = (place_ref[i] for i in range(4))

    fetch = pltpu.make_async_copy(got_hbm, got_ref, sems.at[nq])
    fetch.start()
    own_copies = [pltpu.make_async_copy(own_hbm.at[q], own.at[q], sems.at[q]) for q in range(nq)]
    for copy in own_copies:
        copy.start()
    for h in range(2):
        for owner, src in ((core, near_hbm), (1 - core, far_hbm)):
            for outer in range(SIDE):
                for inner in range(SIDE):
                    dx = inner + owner * (outer - inner)
                    dy = outer + owner * (inner - outer)
                    x, y = lax.rem(x0 + SIDE - dx, SIDE), lax.rem(y0 + SIDE - dy, SIDE)
                    pltpu.make_async_copy(
                        src.at[outer, inner, pl.ds(h * part, part)],
                        other.at[pl.ds(h * part, part), (owner * SIDE + x) * SIDE + y],
                        sems.at[nq + 1 + h],
                    ).start()
    fetch.wait()

    couples, _, both, _ = got_ref.shape
    chunk = couples // 8
    for i in range(8):
        tiles = [got_ref[pl.ds(i * chunk, chunk), side, :, :nv].astype(jnp.float32) for side in range(2)]
        for p, tile in enumerate(split_pairs(*tiles)):
            rows = chunk * both
            amps_ref[p * nv + i * rows : p * nv + (i + 1) * rows] = tile.reshape(rows, nv).astype(jnp.bfloat16)

    def ready(q):
        if q < nq:
            own_copies[q].wait()
        elif (q - nq) % part == 0:
            block = other.at[pl.ds(q - nq, part)]
            pltpu.make_async_copy(block, block, sems.at[nq + 1 + (q - nq) // part]).wait()

    def columns(q):
        if q < nq:
            return own[q, pl.ds(pl.multiple_of(aux * half, half), half), :]
        return other[q - nq, pl.ds(aux * (slots // 2), slots // 2)].reshape(half, nv)

    def vector(q):
        return own[q] if q < nq else other[q - nq].reshape(nv, nv)

    ready(0)
    right[0] = turned(amps_ref, columns(0))
    for q in range(2 * nq):
        if q + 1 < 2 * nq:
            ready(q + 1)
            right[(q + 1) % 2] = turned(amps_ref, columns(q + 1))
        product = jnp.dot(vector(q), right[q % 2], preferred_element_type=jnp.float32)
        total[...] = total[...] + product if q else product

    level = rows_ref[...] + cols_ref[...]
    tiles = [got_ref[:, side, :, nv:].astype(jnp.float32) for side in range(2)]
    stores = []
    for p, hole in enumerate(split_pairs(*tiles)):
        value = hole.reshape(nv, half) + total[:, p * half : (p + 1) * half]
        out_ref[p] = value / (level - occ_ref[p])
        stores.append(pltpu.make_async_copy(out_ref.at[p], out_hbm.at[p], sems.at[p]))
        stores[p].start()
    for store in stores:
        store.wait()


def particle(place, occ_sum, got, own, near, far, rows, cols):
    nq, nv, _ = own.shape
    slots = nv // near.shape[3]
    vmem = pl.BlockSpec(memory_space=pltpu.VMEM)
    smem = pl.BlockSpec(memory_space=pltpu.SMEM)
    anywhere = pl.BlockSpec(memory_space=pl.ANY)
    return pl.pallas_call(
        particle_kernel,
        in_specs=[smem, smem, anywhere, anywhere, anywhere, anywhere, vmem, vmem],
        out_specs=anywhere,
        out_shape=jax.ShapeDtypeStruct((2, nv, nv // 2), jnp.float32),
        scratch_shapes=[
            pltpu.VMEM(got.shape, jnp.bfloat16),
            pltpu.VMEM((2 * nv, nv), jnp.bfloat16),
            pltpu.VMEM((nq, nv, nv), jnp.bfloat16),
            pltpu.VMEM((nq, slots, nv // slots, nv), jnp.bfloat16),
            pltpu.VMEM((2, nv, nv), jnp.bfloat16),
            pltpu.VMEM((nv, nv), jnp.float32),
            pltpu.VMEM((2, nv, nv // 2), jnp.float32),
            pltpu.SemaphoreType.DMA((nq + 3,)),
        ],
        compiler_params=pltpu.CompilerParams(vmem_limit_bytes=VMEM_LIMIT),
        cost_estimate=pl.CostEstimate(
            flops=8 * nq * nv**3, bytes_accessed=4 * nq * nv * nv, transcendentals=0
        ),
        name="particle",
    )(place, occ_sum, got, own, near, far, rows, cols)


def plane_shift(block, shift, first_core_axis):
    pairs = []
    for x in range(SIDE):
        for y in range(SIDE):
            for core in range(2):
                if core == first_core_axis:
                    to = x * SIDE + (y + shift) % SIDE
                else:
                    to = (x + shift) % SIDE * SIDE + y
                pairs.append(((x * SIDE + y) * 2 + core, to * 2 + core))
    return lax.ppermute(block, ("x", "y", "core"), pairs)


def gather_plane(block):
    for stage in range(2):
        block = jnp.stack([block] + [plane_shift(block, d, 1 - stage) for d in (1, 2, 3)])
    return block


def shards(amplitudes, ladder, cholesky, pair_ids, occ_energy, vir_energy):
    n_pair, rows, n_virt = amplitudes.shape
    half_width = n_virt // lax.axis_size("aux")
    aux, core = lax.axis_index("aux"), lax.axis_index("core")
    x, y = lax.axis_index("x"), lax.axis_index("y")
    strip = half_width // (SIDE * SIDE)

    slot = (core * SIDE + x) * SIDE + y
    piece = lax.dynamic_slice_in_dim(cholesky, slot * strip, strip, 1)
    piece = lax.ppermute(piece, "aux", [(0, 1), (1, 0)])

    mine = lax.dynamic_slice_in_dim(amplitudes, aux * half_width, half_width, 2)
    hole = jnp.dot(
        ladder, mine.reshape(n_pair, -1), preferred_element_type=jnp.float32
    ).astype(jnp.bfloat16)
    packed = jnp.concatenate(
        [amplitudes.reshape(-1, 2 * rows, n_virt), hole.reshape(-1, 2 * rows, half_width)], axis=2
    )
    packed, piece = lax.optimization_barrier((packed, piece))
    got = lax.all_to_all(packed, PAIR, split_axis=0, concat_axis=0, tiled=True)
    got = got.reshape(-1, 2, *got.shape[1:])
    near = gather_plane(piece)
    far = lax.ppermute(near, "core", [(0, 1), (1, 0)])

    orbitals = jnp.arange(NO, dtype=jnp.int32)
    first_hot = (pair_ids[:, None] // NO == orbitals[None, :]).astype(jnp.float32)
    second_hot = (pair_ids[:, None] % NO == orbitals[None, :]).astype(jnp.float32)
    occ_sum = jnp.sum((first_hot + second_hot) * occ_energy[None, :], axis=1)
    vir_cols = lax.dynamic_slice_in_dim(vir_energy, aux * half_width, half_width, 0)
    place = jnp.stack([aux, core, x, y]).astype(jnp.int32)

    return particle(place, occ_sum, got, cholesky, near, far, vir_energy[:, None], vir_cols[None, :])


def solution(mesh):
    fine = Mesh(mesh.devices.reshape(SIDE, SIDE, SIDE, 2, 2), AXES)
    in_specs = (P(None, PAIR, None), P(), P("aux", None, None), P(PAIR), P(), P())
    out_specs = P(PAIR, None, "aux")
    return jax.shard_map(shards, mesh=fine, in_specs=in_specs, out_specs=out_specs, check_vma=False)
```

time: 159 us -> 81.9 us (0.52)
  waiting for transfers between devices: 74.3 us -> 28.2 us
  blocking collectives: 43.5 us -> 0 us
  starting transfers between devices: 6.57 us -> 31.6 us
  matrix products: 14.2 us -> 0.35 us
  Pallas kernels: 0 us -> 13.5 us
  between operations: 13.5 us -> 0.28 us
    all_to_all x1, waiting for transfers between devices: 74.3 us -> 0.01 us  [shards(): got = lax.all_to_all(packed, PAIR, split_axis=0, concat_axis=0, tiled=True)]
    all_to_all x1 -> x0, blocking collectives: 43.5 us -> none  [shards(): lax.all_to_all(amplitudes, 'pair', split_axis=0, concat_axis=1, tiled=True)]
    ppermute x0 -> x8, waiting for transfers between devices: none -> 28.2 us  [the longest x6 27 us: plane_shift(): return lax.ppermute(block, ('x', 'y', 'core'), pairs)]
    ppermute x0 -> x8, starting transfers between devices: none -> 18.2 us  [the longest x6 10 us: plane_shift(): return lax.ppermute(block, ('x', 'y', 'core'), pairs)]
    dot_general x2 -> x1, matrix products: 14.2 us -> 0.35 us  [shards(): jnp.dot(ladder, mine.reshape(n_pair, -1), preferred_element_type=jnp.floa...]
    pallas_call x0 -> x1, Pallas kernels: none -> 13.5 us  [particle(): pl.pallas_call(particle_kernel, in_specs=[smem, smem, anywhere, anywhere,...]
    all_to_all x1, starting transfers between devices: 6.57 us -> 13.4 us  [shards(): got = lax.all_to_all(packed, PAIR, split_axis=0, concat_axis=0, tiled=True)]
    div x1 -> x0, other arithmetic: 2.46 us -> none  [shards(): return (pair_hole.astype(jnp.float32) + summed) / denominator]
  transfers between devices with their start and end apart: 2 -> 9, of which waited for: 1 -> 6; matrix products, arithmetic and copies ran while one was open for 2% -> 9% of each run, Pallas kernels for 0% -> 0%
where the time goes in v6:
time: 81.9 us; the launch traced here: 81.7 us
  starting transfers between devices  31.6 us (39%)
  waiting for transfers between devices  28.2 us (34%)
  Pallas kernels  13.5 us (16%)
  local copies, waits for them, and re-layouts  4.83 us (6%)
  other arithmetic  2.91 us (4%)
    ppermute x6, waiting for transfers between devices, plane_shift(): return lax.ppermute(block, ('x', 'y', 'core'), pairs)  27 us
    pallas_call x1, Pallas kernels, particle(): pl.pallas_call(particle_kernel, in_specs=[smem, smem, anywhere, anywhere,...  13.5 us
    all_to_all x1, starting transfers between devices, shards(): got = lax.all_to_all(packed, PAIR, split_axis=0, concat_axis=0, tiled=True)  13.4 us
    ppermute x6, starting transfers between devices, plane_shift(): return lax.ppermute(block, ('x', 'y', 'core'), pairs)  10 us
    ppermute x1, starting transfers between devices, shards(): piece = lax.ppermute(piece, 'aux', [(0, 1), (1, 0)])  7.83 us
  transfers between devices with their start and end apart: 9, of which 6 were waited for; matrix products, arithmetic and copies ran while one was open for 9% of the time, Pallas kernels for 0%

profile of v6, /device:TPU:1, one launch (start us, length us, event | category | flops | bytes accessed | tf_op | source)
XLA Modules:
  0.0 81.7 jit_solution(8309737346615642544)
XLA Ops:
  0.0 1.0 %constant_dynamic-slice_fusion = bf16[8,16,512]{2,1,0:T(8,128)(2,1)S(1)} fusion(bf16[8,512,512]{2,1,0:T(8,128)(2,1)} %own_hbm.1, s32[]{:T(128)S(6)} %select_n.24), kind=kLoop, calls=%fused_computation.16 | loop fusion | bytes 262148 | tf_op jit(solution)/shard_map/dynamic_slice | solution.py:164
  1.0 7.8 %collective-permute-start = (bf16[8,16,512]{2,1,0:T(8,128)(2,1)S(1)}, bf16[8,16,512]{2,1,0:T(8,128)(2,1)S(1)}, u32[]{:S(2)}, u32[]{:S(2)}) collective-permute-start(bf16[8,16,512]{2,1,0:T(8,128)(2,1)S(1)} %constant_dynamic-slice_fusion), channel_id=1, source_target_pairs={{0,1},{1,0},{2,3},{3,2},{4,5},{5,4},{6,7},{7,6},{8,9},{9,8},{10,11... | collective-permute-start | bytes 393224 | tf_op jit(solution)/shard_map/ppermute | solution.py:165
  8.8 1.3 %reshape.39 = bf16[128,8,512]{2,1,0:T(8,128)(2,1)S(1)} reshape(bf16[256,4,512]{2,1,0:T(4,128)(2,1)} %param.6) | data formatting | bytes 2097152 | tf_op jit(solution)/shard_map/reshape | solution.py:172
  10.2 0.2 constant_dynamic-slice_fusion.1
  10.4 0.1 copy.11
  10.5 0.4 fusion
  10.9 0.2 copy.9
  11.1 0.3 reshape.41
  11.4 1.3 %pad_maximum_fusion.1 = bf16[128,8,768]{2,1,0:T(8,128)(2,1)} fusion(bf16[128,8,256]{2,1,0:T(8,128)(2,1)S(1)} %reshape.41, bf16[128,8,512]{2,1,0:T(8,128)(2,1)S(1)} %reshape.39), kind=kLoop, calls=%fused_computation.1 | loop fusion | flops 3145728 | bytes 3145728 | tf_op jit(solution)/shard_map/concatenate | solution.py:171
  12.7 0.0 collective-permute-done
  12.7 13.4 %all-to-all-start = ((bf16[128,8,768]{2,1,0:T(8,128)(2,1)}), bf16[128,8,768]{2,1,0:T(8,128)(2,1)}, u32[]{:S(2)}, u32[]{:S(2)}) async-start(bf16[128,8,768]{2,1,0:T(8,128)(2,1)} %pad_maximum_fusion.1), calls=%async_computation | async-start | bytes 3145728 | tf_op jit(solution)/shard_map/all_to_all | solution.py:175
  26.1 2.7 %collective-permute-start.3 = (bf16[8,16,512]{2,1,0:T(8,128)(2,1)S(1)}, bf16[8,16,512]{2,1,0:T(8,128)(2,1)S(1)}, u32[]{:S(2)}, u32[]{:S(2)}) collective-permute-start(bf16[8,16,512]{2,1,0:T(8,128)(2,1)S(1)} %collective-permute-done), channel_id=1, source_target_pairs={{0,192},{2,50},{16,208},{18,2},{32,224},{34,18},{48,240},{50,34},{... | collective-permute-start | bytes 393224 | tf_op jit(solution)/shard_map/ppermute | solution.py:147
  28.8 0.5 collective-permute-start.2
  29.4 0.6 collective-permute-start.1
  29.9 7.7 %collective-permute-done.3 = bf16[8,16,512]{2,1,0:T(8,128)(2,1)S(1)} collective-permute-done((bf16[8,16,512]{2,1,0:T(8,128)(2,1)S(1)}, bf16[8,16,512]{2,1,0:T(8,128)(2,1)S(1)}, u32[]{:S(2)}, u32[]{:S(2)}) %collective-permute-start.3) | collective-permute-done | bytes 131104 | tf_op jit(solution)/shard_map/ppermute | solution.py:147
  37.6 3.2 %collective-permute-done.2 = bf16[8,16,512]{2,1,0:T(8,128)(2,1)S(1)} collective-permute-done((bf16[8,16,512]{2,1,0:T(8,128)(2,1)S(1)}, bf16[8,16,512]{2,1,0:T(8,128)(2,1)S(1)}, u32[]{:S(2)}, u32[]{:S(2)}) %collective-permute-start.2) | collective-permute-done | bytes 131104 | tf_op jit(solution)/shard_map/ppermute | solution.py:147
  40.8 2.3 %collective-permute-done.1 = bf16[8,16,512]{2,1,0:T(8,128)(2,1)S(1)} collective-permute-done((bf16[8,16,512]{2,1,0:T(8,128)(2,1)S(1)}, bf16[8,16,512]{2,1,0:T(8,128)(2,1)S(1)}, u32[]{:S(2)}, u32[]{:S(2)}) %collective-permute-start.1) | collective-permute-done | bytes 131104 | tf_op jit(solution)/shard_map/ppermute | solution.py:147
  43.2 0.1 fusion.4
  43.2 3.5 %collective-permute-start.5 = (bf16[4,8,16,512]{3,2,1,0:T(8,128)(2,1)S(1)}, bf16[4,8,16,512]{3,2,1,0:T(8,128)(2,1)S(1)}, u32[]{:S(2)}, u32[]{:S(2)}) collective-permute-start(bf16[4,8,16,512]{3,2,1,0:T(8,128)(2,1)S(1)} %get-tuple-element.10), channel_id=1, source_target_pairs={{0,32},{2,130},{16,48},{18,146},{32,0},{34,162},{48,16},{50,178},{... | collective-permute-start | bytes 1572872 | tf_op jit(solution)/shard_map/ppermute | solution.py:147
  46.7 0.0 collective-permute-start.4
  46.7 2.7 %collective-permute-start.6 = (bf16[4,8,16,512]{3,2,1,0:T(8,128)(2,1)S(1)}, bf16[4,8,16,512]{3,2,1,0:T(8,128)(2,1)S(1)}, u32[]{:S(2)}, u32[]{:S(2)}) collective-permute-start(bf16[4,8,16,512]{3,2,1,0:T(8,128)(2,1)S(1)} %get-tuple-element.10), channel_id=1, source_target_pairs={{0,48},{2,194},{16,0},{18,210},{32,16},{34,226},{48,32},{50,242},{... | collective-permute-start | bytes 1572872 | tf_op jit(solution)/shard_map/ppermute | solution.py:147
  49.4 6.2 %collective-permute-done.5 = bf16[4,8,16,512]{3,2,1,0:T(8,128)(2,1)S(1)} collective-permute-done((bf16[4,8,16,512]{3,2,1,0:T(8,128)(2,1)S(1)}, bf16[4,8,16,512]{3,2,1,0:T(8,128)(2,1)S(1)}, u32[]{:S(2)}, u32[]{:S(2)}) %collective-permute-start.5) | collective-permute-done | bytes 524320 | tf_op jit(solution)/shard_map/ppermute | solution.py:147
  55.6 7.6 %collective-permute-done.4 = bf16[4,8,16,512]{3,2,1,0:T(8,128)(2,1)S(1)} collective-permute-done((bf16[4,8,16,512]{3,2,1,0:T(8,128)(2,1)S(1)}, bf16[4,8,16,512]{3,2,1,0:T(8,128)(2,1)S(1)}, u32[]{:S(2)}, u32[]{:S(2)}) %collective-permute-start.4) | collective-permute-done | bytes 524320 | tf_op jit(solution)/shard_map/ppermute | solution.py:147
  63.2 0.0 collective-permute-done.6
  63.2 0.3 pad_maximum_fusion.near_hbm
  63.5 0.4 collective-permute-start.7
  63.9 0.8 dynamic_slice.11
  64.7 0.8 %copy.10.rows_ref = f32[512,1]{1,0:T(8,128)} copy(f32[512,1]{0,1:T(1,128)S(1)} %bitcast.31) | data formatting | bytes 4096 | tf_op jit(solution)/shard_map/broadcast_in_dim | solution.py:187
  65.5 0.6 pad_add_fusion.place_ref
  66.2 0.7 fusion.3.occ_ref
  66.8 1.2 %collective-permute-done.7.far_hbm = bf16[4,4,8,16,512]{4,3,2,1,0:T(8,128)(2,1)} collective-permute-done((bf16[4,4,8,16,512]{4,3,2,1,0:T(8,128)(2,1)S(1)}, bf16[4,4,8,16,512]{4,3,2,1,0:T(8,128)(2,1)}, u32[]{:S(2)}, u32[]{:S(2)}) %collective-permute-start.7) | collective-permute-done | bytes 2097184 | tf_op jit(solution)/shard_map/ppermute | solution.py:178
  68.0 13.5 %particle.1 = f32[2,512,256]{2,1,0:T(8,128)} custom-call(s32[4]{0:T(128)} %pad_add_fusion.place_ref, f32[2]{0:T(128)} %fusion.3.occ_ref, bf16[64,2,8,768]{3,2,1,0:T(8,128)(2,1)} %bitcast.5.got_hbm, bf16[8,512,512]{2,1,0:T(8,128)(2,1)} %own_hbm.1, bf16[4,4,8,16,512]{4,3,2,1,0:T(8,128)(2,1)} %copy-done.2, ...), custom_call_target="tpu_custom_call" | custom-call | flops 8589934592 | bytes 8388608 | tf_op jit(solution)/shard_map/particle/pallas_call | solution.py:114
  (14 shorter events, 0.0 us)
Async XLA Ops:
  0.0 10.5 %copy-start = (bf16[256,256]{1,0:T(8,128)(2,1)S(1)}, bf16[256,256]{1,0:T(8,128)(2,1)}, u32[]{:S(2)}) copy-start(bf16[256,256]{1,0:T(8,128)(2,1)} %param.7) | copy-start | bytes 393220
  0.0 10.2 %copy-start.1 = (bf16[256,4,512]{2,1,0:T(4,128)(2,1)S(1)}, bf16[256,4,512]{2,1,0:T(4,128)(2,1)}, u32[]{:S(2)}) copy-start(bf16[256,4,512]{2,1,0:T(4,128)(2,1)} %param.6) | copy-start | bytes 3145732
  1.0 11.7 %collective-permute-start = (bf16[8,16,512]{2,1,0:T(8,128)(2,1)S(1)}, bf16[8,16,512]{2,1,0:T(8,128)(2,1)S(1)}, u32[]{:S(2)}, u32[]{:S(2)}) collective-permute-start(bf16[8,16,512]{2,1,0:T(8,128)(2,1)S(1)} %constant_dynamic-slice_fusion), channel_id=1, source_target_pairs={{0,1},{1,0},{2,3},{3,2},{4,5},{5,4},{6,7},{7,6},{8,9},{9,8},{10,11... | collective-permute-start | bytes 393224 | tf_op jit(solution)/shard_map/ppermute | solution.py:165
  12.7 55.4 %all-to-all-start = ((bf16[128,8,768]{2,1,0:T(8,128)(2,1)}), bf16[128,8,768]{2,1,0:T(8,128)(2,1)}, u32[]{:S(2)}, u32[]{:S(2)}) async-start(bf16[128,8,768]{2,1,0:T(8,128)(2,1)} %pad_maximum_fusion.1), calls=%async_computation | async-start | bytes 3145728 | tf_op jit(solution)/shard_map/all_to_all | solution.py:175
  26.1 11.5 %collective-permute-start.3 = (bf16[8,16,512]{2,1,0:T(8,128)(2,1)S(1)}, bf16[8,16,512]{2,1,0:T(8,128)(2,1)S(1)}, u32[]{:S(2)}, u32[]{:S(2)}) collective-permute-start(bf16[8,16,512]{2,1,0:T(8,128)(2,1)S(1)} %collective-permute-done), channel_id=1, source_target_pairs={{0,192},{2,50},{16,208},{18,2},{32,224},{34,18},{48,240},{50,34},{... | collective-permute-start | bytes 393224 | tf_op jit(solution)/shard_map/ppermute | solution.py:147
  28.8 12.0 %collective-permute-start.2 = (bf16[8,16,512]{2,1,0:T(8,128)(2,1)S(1)}, bf16[8,16,512]{2,1,0:T(8,128)(2,1)S(1)}, u32[]{:S(2)}, u32[]{:S(2)}) collective-permute-start(bf16[8,16,512]{2,1,0:T(8,128)(2,1)S(1)} %collective-permute-done), channel_id=1, source_target_pairs={{0,128},{2,34},{16,144},{18,50},{32,160},{34,2},{48,176},{50,18},{... | collective-permute-start | bytes 393224 | tf_op jit(solution)/shard_map/ppermute | solution.py:147
  29.4 13.8 %collective-permute-start.1 = (bf16[8,16,512]{2,1,0:T(8,128)(2,1)S(1)}, bf16[8,16,512]{2,1,0:T(8,128)(2,1)S(1)}, u32[]{:S(2)}, u32[]{:S(2)}) collective-permute-start(bf16[8,16,512]{2,1,0:T(8,128)(2,1)S(1)} %collective-permute-done), channel_id=1, source_target_pairs={{0,64},{2,18},{16,80},{18,34},{32,96},{34,50},{48,112},{50,2},{64,... | collective-permute-start | bytes 393224 | tf_op jit(solution)/shard_map/ppermute | solution.py:147
  43.2 12.3 %collective-permute-start.5 = (bf16[4,8,16,512]{3,2,1,0:T(8,128)(2,1)S(1)}, bf16[4,8,16,512]{3,2,1,0:T(8,128)(2,1)S(1)}, u32[]{:S(2)}, u32[]{:S(2)}) collective-permute-start(bf16[4,8,16,512]{3,2,1,0:T(8,128)(2,1)S(1)} %get-tuple-element.10), channel_id=1, source_target_pairs={{0,32},{2,130},{16,48},{18,146},{32,0},{34,162},{48,16},{50,178},{... | collective-permute-start | bytes 1572872 | tf_op jit(solution)/shard_map/ppermute | solution.py:147
  46.7 16.4 %collective-permute-start.4 = (bf16[4,8,16,512]{3,2,1,0:T(8,128)(2,1)S(1)}, bf16[4,8,16,512]{3,2,1,0:T(8,128)(2,1)S(1)}, u32[]{:S(2)}, u32[]{:S(2)}) collective-permute-start(bf16[4,8,16,512]{3,2,1,0:T(8,128)(2,1)S(1)} %get-tuple-element.10), channel_id=1, source_target_pairs={{0,16},{2,66},{16,32},{18,82},{32,48},{34,98},{48,0},{50,114},{64,... | collective-permute-start | bytes 1572872 | tf_op jit(solution)/shard_map/ppermute | solution.py:147
  46.7 16.4 %collective-permute-start.6 = (bf16[4,8,16,512]{3,2,1,0:T(8,128)(2,1)S(1)}, bf16[4,8,16,512]{3,2,1,0:T(8,128)(2,1)S(1)}, u32[]{:S(2)}, u32[]{:S(2)}) collective-permute-start(bf16[4,8,16,512]{3,2,1,0:T(8,128)(2,1)S(1)} %get-tuple-element.10), channel_id=1, source_target_pairs={{0,48},{2,194},{16,0},{18,210},{32,16},{34,226},{48,32},{50,242},{... | collective-permute-start | bytes 1572872 | tf_op jit(solution)/shard_map/ppermute | solution.py:147
  63.2 0.7 copy-start.3
  63.2 3.0 %copy-start.5 = (s32[2]{0:T(128)S(1)}, s32[2]{0:T(128)}, u32[]{:S(2)}) copy-start(s32[2]{0:T(128)} %param.9) | copy-start | bytes 28
  63.2 3.0 %copy-start.4 = (f32[16]{0:T(128)S(1)}, f32[16]{0:T(128)}, u32[]{:S(2)}) copy-start(f32[16]{0:T(128)} %param.10) | copy-start | bytes 196
  63.5 4.6 %copy-start.2 = (bf16[4,4,8,16,512]{4,3,2,1,0:T(8,128)(2,1)}, bf16[4,4,8,16,512]{4,3,2,1,0:T(8,128)(2,1)S(1)}, u32[]{:S(2)}) copy-start(bf16[4,4,8,16,512]{4,3,2,1,0:T(8,128)(2,1)S(1)} %pad_maximum_fusion.near_hbm) | copy-start | bytes 6291460
  63.5 4.6 %collective-permute-start.7 = (bf16[4,4,8,16,512]{4,3,2,1,0:T(8,128)(2,1)S(1)}, bf16[4,4,8,16,512]{4,3,2,1,0:T(8,128)(2,1)}, u32[]{:S(2)}, u32[]{:S(2)}) collective-permute-start(bf16[4,4,8,16,512]{4,3,2,1,0:T(8,128)(2,1)S(1)} %pad_maximum_fusion.near_hbm), channel_id=1, source_target_pairs={{0,2},{2,0},{1,3},{3,1},{4,6},{6,4},{5,7},{7,5},{8,10},{10,8},{9,1... | collective-permute-start | bytes 6291464 | tf_op jit(solution)/shard_map/ppermute | solution.py:178

commit v7 on v6

--- a/solution.py
+++ b/solution.py
@@ -10,6 +10,7 @@
 PAIR = AXES[:4]
 SIDE = 4
 VMEM_LIMIT = 56 * 1024 * 1024
+WEIGHT = 20 * 10**9
 NT = (((1,), (1,)), ((), ()))
 
 
@@ -34,16 +35,18 @@
 
 
 def particle_kernel(
-    place_ref, occ_ref, got_hbm, own_hbm, near_hbm, far_hbm, rows_ref, cols_ref, out_hbm,
+    place_ref, occ_ref, got_hbm, one_hbm, two_hbm, three_hbm, own_hbm, near_hbm, far_hbm, rows_ref, cols_ref, out_hbm,
     got_ref, amps_ref, own, other, right, total, out_ref, sems,
 ):
     nq, nv, _ = own.shape
     half, part = nv // 2, nq // 2
     slots = other.shape[1]
-    aux, core, x0, y0 = (place_ref[i] for i in range(4))
-
-    fetch = pltpu.make_async_copy(got_hbm, got_ref, sems.at[nq])
-    fetch.start()
+    aux, core, x0, y0, z = (place_ref[i] for i in range(5))
+
+    fetches = []
+    for step, src in enumerate((got_hbm.at[:, :, z], one_hbm, two_hbm, three_hbm)):
+        fetches.append(pltpu.make_async_copy(src, got_ref.at[:, lax.rem(z + SIDE - step, SIDE)], sems.at[nq + 3 + step]))
+        fetches[step].start()
     own_copies = [pltpu.make_async_copy(own_hbm.at[q], own.at[q], sems.at[q]) for q in range(nq)]
     for copy in own_copies:
         copy.start()
@@ -59,12 +62,20 @@
                         other.at[pl.ds(h * part, part), (owner * SIDE + x) * SIDE + y],
                         sems.at[nq + 1 + h],
                     ).start()
-    fetch.wait()
-
-    couples, _, both, _ = got_ref.shape
-    chunk = couples // 8
+    for fetch in fetches:
+        fetch.wait()
+
+    cells, planes, _, both, _ = got_ref.shape
+    chunk = cells * planes // 8
+
+    def tiles_of(begin, count, lanes):
+        return [
+            got_ref[begin : begin + count, :, side, :, lanes].astype(jnp.float32).reshape(count * planes, both, -1)
+            for side in range(2)
+        ]
+
     for i in range(8):
-        tiles = [got_ref[pl.ds(i * chunk, chunk), side, :, :nv].astype(jnp.float32) for side in range(2)]
+        tiles = tiles_of(i * (cells // 8), cells // 8, slice(0, nv))
         for p, tile in enumerate(split_pairs(*tiles)):
             rows = chunk * both
             amps_ref[p * nv + i * rows : p * nv + (i + 1) * rows] = tile.reshape(rows, nv).astype(jnp.bfloat16)
@@ -94,7 +105,7 @@
         total[...] = total[...] + product if q else product
 
     level = rows_ref[...] + cols_ref[...]
-    tiles = [got_ref[:, side, :, nv:].astype(jnp.float32) for side in range(2)]
+    tiles = tiles_of(0, cells, slice(nv, nv + half))
     stores = []
     for p, hole in enumerate(split_pairs(*tiles)):
         value = hole.reshape(nv, half) + total[:, p * half : (p + 1) * half]
@@ -105,7 +116,7 @@
         store.wait()
 
 
-def particle(place, occ_sum, got, own, near, far, rows, cols):
+def particle(place, occ_sum, got, ring, own, near, far, rows, cols):
     nq, nv, _ = own.shape
     slots = nv // near.shape[3]
     vmem = pl.BlockSpec(memory_space=pltpu.VMEM)
@@ -113,25 +124,42 @@
     anywhere = pl.BlockSpec(memory_space=pl.ANY)
     return pl.pallas_call(
         particle_kernel,
-        in_specs=[smem, smem, anywhere, anywhere, anywhere, anywhere, vmem, vmem],
+        in_specs=[smem, smem, *[anywhere] * 7, vmem, vmem],
         out_specs=anywhere,
         out_shape=jax.ShapeDtypeStruct((2, nv, nv // 2), jnp.float32),
         scratch_shapes=[
-            pltpu.VMEM(got.shape, jnp.bfloat16),
+            pltpu.VMEM((got.shape[0], SIDE, 2, *got.shape[3:]), jnp.bfloat16),
             pltpu.VMEM((2 * nv, nv), jnp.bfloat16),
             pltpu.VMEM((nq, nv, nv), jnp.bfloat16),
             pltpu.VMEM((nq, slots, nv // slots, nv), jnp.bfloat16),
             pltpu.VMEM((2, nv, nv), jnp.bfloat16),
             pltpu.VMEM((nv, nv), jnp.float32),
             pltpu.VMEM((2, nv, nv // 2), jnp.float32),
-            pltpu.SemaphoreType.DMA((nq + 3,)),
+            pltpu.SemaphoreType.DMA((nq + 3 + SIDE,)),
         ],
         compiler_params=pltpu.CompilerParams(vmem_limit_bytes=VMEM_LIMIT),
         cost_estimate=pl.CostEstimate(
             flops=8 * nq * nv**3, bytes_accessed=4 * nq * nv * nv, transcendentals=0
         ),
         name="particle",
-    )(place, occ_sum, got, own, near, far, rows, cols)
+    )(place, occ_sum, got, *ring, own, near, far, rows, cols)
+
+
+def arrived_kernel(place_ref, *refs):
+    for i in range(place_ref.shape[0]):
+        refs[-1][i] = place_ref[i]
+
+
+def arrived(place, ring):
+    smem = pl.BlockSpec(memory_space=pltpu.SMEM)
+    return pl.pallas_call(
+        arrived_kernel,
+        in_specs=[smem, *[pl.BlockSpec(memory_space=pl.ANY)] * len(ring)],
+        out_specs=smem,
+        out_shape=jax.ShapeDtypeStruct(place.shape, place.dtype),
+        cost_estimate=pl.CostEstimate(flops=WEIGHT, bytes_accessed=0, transcendentals=0),
+        name="arrived",
+    )(place, *ring)
 
 
 def plane_shift(block, shift, first_core_axis):
@@ -153,27 +181,46 @@
     return block
 
 
+def ring_pairs(step):
+    steps = {1: (1, 1), 3: (-1, -1), 2: (2, -2)}[step]
+    pairs = []
+    for z8 in range(2 * SIDE):
+        for core in range(2):
+            to = (z8 + steps[core]) % (2 * SIDE)
+            pairs.append(((z8 % SIDE * 2 + core) * 2 + z8 // SIDE, (to % SIDE * 2 + core) * 2 + to // SIDE))
+    return pairs
+
+
 def shards(amplitudes, ladder, cholesky, pair_ids, occ_energy, vir_energy):
     n_pair, rows, n_virt = amplitudes.shape
     half_width = n_virt // lax.axis_size("aux")
     aux, core = lax.axis_index("aux"), lax.axis_index("core")
-    x, y = lax.axis_index("x"), lax.axis_index("y")
+    x, y, z = lax.axis_index("x"), lax.axis_index("y"), lax.axis_index("z")
     strip = half_width // (SIDE * SIDE)
 
     slot = (core * SIDE + x) * SIDE + y
     piece = lax.dynamic_slice_in_dim(cholesky, slot * strip, strip, 1)
     piece = lax.ppermute(piece, "aux", [(0, 1), (1, 0)])
 
-    mine = lax.dynamic_slice_in_dim(amplitudes, aux * half_width, half_width, 2)
     hole = jnp.dot(
-        ladder, mine.reshape(n_pair, -1), preferred_element_type=jnp.float32
+        ladder, amplitudes.reshape(n_pair, -1), preferred_element_type=jnp.float32
     ).astype(jnp.bfloat16)
-    packed = jnp.concatenate(
-        [amplitudes.reshape(-1, 2 * rows, n_virt), hole.reshape(-1, 2 * rows, half_width)], axis=2
-    )
+    blocks = (SIDE * SIDE, SIDE, 2, 2 * rows)
+    hole = hole.reshape(*blocks, n_virt)
+    step = lax.rem(jnp.arange(SIDE) - z + SIDE, SIDE)[:, None]
+    move = jnp.where(step == 3, -1, jnp.where(step == 2, 2 - 4 * jnp.arange(2)[None, :], step))
+    upper = lax.rem(aux * SIDE + z + move + 2 * SIDE, 2 * SIDE) >= SIDE
+    hole = jnp.where(upper[None, :, :, None, None], hole[..., half_width:], hole[..., :half_width])
+    packed = jnp.concatenate([amplitudes.reshape(*blocks, n_virt), hole], axis=4)
+    packed = packed.transpose(0, 2, 1, 3, 4).reshape(2 * SIDE * SIDE, SIDE, 2 * rows, -1)
     packed, piece = lax.optimization_barrier((packed, piece))
-    got = lax.all_to_all(packed, PAIR, split_axis=0, concat_axis=0, tiled=True)
-    got = got.reshape(-1, 2, *got.shape[1:])
+    got = lax.all_to_all(packed, ("x", "y", "core"), split_axis=0, concat_axis=0, tiled=True)
+    ring = []
+    for d in range(1, SIDE):
+        block = lax.dynamic_slice_in_dim(got, lax.rem(z + d, SIDE), 1, 1)
+        block = lax.ppermute(block, ("z", "core", "aux"), ring_pairs(d))
+        ring.append(block.reshape(SIDE * SIDE, 2, 2 * rows, -1))
+    got = got.reshape(SIDE * SIDE, 2, SIDE, 2 * rows, -1)
     near = gather_plane(piece)
     far = lax.ppermute(near, "core", [(0, 1), (1, 0)])
 
@@ -182,9 +229,9 @@
     second_hot = (pair_ids[:, None] % NO == orbitals[None, :]).astype(jnp.float32)
     occ_sum = jnp.sum((first_hot + second_hot) * occ_energy[None, :], axis=1)
     vir_cols = lax.dynamic_slice_in_dim(vir_energy, aux * half_width, half_width, 0)
-    place = jnp.stack([aux, core, x, y]).astype(jnp.int32)
-
-    return particle(place, occ_sum, got, cholesky, near, far, vir_energy[:, None], vir_cols[None, :])
+    place = jnp.stack([aux, core, x, y, z]).astype(jnp.int32)
+
+    return particle(arrived(place, ring), occ_sum, got, ring, cholesky, near, far, vir_energy[:, None], vir_cols[None, :])
 
 
 def solution(mesh):

time: 81.9 us -> 91.4 us (1.12); the launches traced: 81.7 us -> 90.2 us
  local copies, waits for them, and re-layouts: 4.83 us -> 7.92 us
  starting transfers between devices: 31.6 us -> 33.9 us
  Pallas kernels: 13.5 us -> 14.7 us
  other arithmetic: 2.91 us -> 4.06 us
    ppermute x0 -> x3, starting transfers between devices: none -> 7.64 us  [shards(): block = lax.ppermute(block, ('z', 'core', 'aux'), ring_pairs(d))]
    ppermute x0 -> x3, waiting for transfers between devices: none -> 7.43 us  [shards(): block = lax.ppermute(block, ('z', 'core', 'aux'), ring_pairs(d))]
    ppermute x6, waiting for transfers between devices: 27 us -> 21.5 us  [plane_shift(): return lax.ppermute(block, ('x', 'y', 'core'), pairs)]
    all_to_all x1, starting transfers between devices: 13.4 us -> 8.04 us  [shards(): lax.all_to_all(packed, ('x', 'y', 'core'), split_axis=0, concat_axis=0, t...]
    another operation x2, other arithmetic: 0.35 us -> 2.92 us  [gather_plane(): jnp.stack([block] + [plane_shift(block, d, 1 - stage) for d in (1, 2, 3)])]
    concatenate x0 -> x1, local copies, waits for them, and re-layouts: none -> 1.37 us  [shards(): jnp.concatenate([amplitudes.reshape(*blocks, n_virt), hole], axis=4)]
    pallas_call x1 -> x2, Pallas kernels: 13.5 us -> 14.7 us  [the longest x1 13.5 us: particle(): pl.pallas_call(particle_kernel, in_specs=[smem, smem, *[anywhere] * 7, vm...]
    ppermute x1, waiting for transfers between devices: 1.2 us -> 0.01 us  [shards(): far = lax.ppermute(near, 'core', [(0, 1), (1, 0)])]
  transfers between devices with their start and end apart: 9 -> 12, of which waited for: 6 -> 6; matrix products, arithmetic and copies ran while one was open for 9% -> 13% of each run, Pallas kernels for 0% -> 1%
where the time goes in v7:
time: 91.4 us; the launch traced here: 90.2 us
  starting transfers between devices  33.9 us (37%)
  waiting for transfers between devices  28.9 us (32%)
  Pallas kernels  14.7 us (16%)
  local copies, waits for them, and re-layouts  7.92 us (9%)
  other arithmetic  4.06 us (4%)
    ppermute x6, waiting for transfers between devices, plane_shift(): return lax.ppermute(block, ('x', 'y', 'core'), pairs)  21.5 us
    pallas_call x1, Pallas kernels, particle(): pl.pallas_call(particle_kernel, in_specs=[smem, smem, *[anywhere] * 7, vm...  13.5 us
    ppermute x6, starting transfers between devices, plane_shift(): return lax.ppermute(block, ('x', 'y', 'core'), pairs)  9.01 us
    all_to_all x1, starting transfers between devices, shards(): lax.all_to_all(packed, ('x', 'y', 'core'), split_axis=0, concat_axis=0, t...  8.04 us
    ppermute x1, starting transfers between devices, shards(): piece = lax.ppermute(piece, 'aux', [(0, 1), (1, 0)])  7.83 us
    ppermute x3, starting transfers between devices, shards(): block = lax.ppermute(block, ('z', 'core', 'aux'), ring_pairs(d))  7.64 us
    ppermute x3, waiting for transfers between devices, shards(): block = lax.ppermute(block, ('z', 'core', 'aux'), ring_pairs(d))  7.43 us
    another operation x2, other arithmetic, gather_plane(): jnp.stack([block] + [plane_shift(block, d, 1 - stage) for d in (1, 2, 3)])  2.92 us
  transfers between devices with their start and end apart: 12, of which 6 were waited for; matrix products, arithmetic and copies ran while one was open for 13% of the time, Pallas kernels for 1%

profile of v7, /device:TPU:1, one launch (start us, length us, event | category | flops | bytes accessed | tf_op | source)
XLA Modules:
  0.0 90.2 jit_solution(13040206271104298286)
XLA Ops:
  0.0 1.0 %constant_dynamic-slice_fusion.3 = bf16[8,16,512]{2,1,0:T(8,128)(2,1)S(1)} fusion(bf16[8,512,512]{2,1,0:T(8,128)(2,1)} %own_hbm.1, s32[]{:T(128)S(6)} %select_n.52), kind=kLoop, calls=%fused_computation.24 | loop fusion | bytes 262148 | tf_op jit(solution)/shard_map/dynamic_slice | solution.py:202
  1.0 7.8 %collective-permute-start = (bf16[8,16,512]{2,1,0:T(8,128)(2,1)S(1)}, bf16[8,16,512]{2,1,0:T(8,128)(2,1)S(1)}, u32[]{:S(2)}, u32[]{:S(2)}) collective-permute-start(bf16[8,16,512]{2,1,0:T(8,128)(2,1)S(1)} %constant_dynamic-slice_fusion.3), channel_id=1, source_target_pairs={{0,1},{1,0},{2,3},{3,2},{4,5},{5,4},{6,7},{7,6},{8,9},{9,8},{10,11... | collective-permute-start | bytes 393224 | tf_op jit(solution)/shard_map/ppermute | solution.py:203
  8.9 1.3 %reshape.148 = bf16[16,4,2,8,512]{4,3,2,1,0:T(8,128)(2,1)S(1)} reshape(bf16[256,4,512]{2,1,0:T(4,128)(2,1)} %param.6) | data formatting | bytes 2097152 | tf_op jit(solution)/shard_map/reshape | solution.py:214
  10.2 0.3 copy.19
  10.5 0.4 convolution_convert_fusion
  11.0 0.7 reshape.150
  12.0 1.4 %copy.18 = bf16[16,4,2,8,768]{4,3,1,2,0:T(8,128)(2,1)} copy(bf16[16,4,2,8,768]{4,3,2,1,0:T(8,128)(2,1)S(1)} %pad_maximum_fusion.1) | data formatting | bytes 3145728 | tf_op jit(solution)/shard_map/concatenate | solution.py:214
  13.4 8.0 %all-to-all-start = ((bf16[32,4,8,768]{3,2,1,0:T(8,128)(2,1)}), bf16[32,4,8,768]{3,2,1,0:T(8,128)(2,1)S(1)}, u32[]{:S(2)}, u32[]{:S(2)}) async-start(bf16[32,4,8,768]{3,2,1,0:T(8,128)(2,1)} %bitcast.6), calls=%async_computation | async-start | bytes 3145728 | tf_op jit(solution)/shard_map/all_to_all | solution.py:217
  21.4 2.7 %collective-permute-start.6 = (bf16[8,16,512]{2,1,0:T(8,128)(2,1)S(1)}, bf16[8,16,512]{2,1,0:T(8,128)(2,1)S(1)}, u32[]{:S(2)}, u32[]{:S(2)}) collective-permute-start(bf16[8,16,512]{2,1,0:T(8,128)(2,1)S(1)} %collective-permute-done), channel_id=1, source_target_pairs={{0,192},{2,50},{16,208},{18,2},{32,224},{34,18},{48,240},{50,34},{... | collective-permute-start | bytes 393224 | tf_op jit(solution)/shard_map/ppermute | solution.py:175
  24.1 0.6 collective-permute-start.5
  24.7 0.6 collective-permute-start.4
  25.3 16.7 %collective-permute-done.6 = bf16[8,16,512]{2,1,0:T(8,128)(2,1)S(1)} collective-permute-done((bf16[8,16,512]{2,1,0:T(8,128)(2,1)S(1)}, bf16[8,16,512]{2,1,0:T(8,128)(2,1)S(1)}, u32[]{:S(2)}, u32[]{:S(2)}) %collective-permute-start.6) | collective-permute-done | bytes 131104 | tf_op jit(solution)/shard_map/ppermute | solution.py:175
  42.0 2.2 %collective-permute-done.5 = bf16[8,16,512]{2,1,0:T(8,128)(2,1)S(1)} collective-permute-done((bf16[8,16,512]{2,1,0:T(8,128)(2,1)S(1)}, bf16[8,16,512]{2,1,0:T(8,128)(2,1)S(1)}, u32[]{:S(2)}, u32[]{:S(2)}) %collective-permute-start.5) | collective-permute-done | bytes 131104 | tf_op jit(solution)/shard_map/ppermute | solution.py:175
  44.2 0.8 collective-permute-done.4
  45.1 2.5 %collective-permute-start.8 = (bf16[4,8,16,512]{3,2,1,0:T(8,128)(2,1)S(1)}, bf16[4,8,16,512]{3,2,1,0:T(8,128)(2,1)S(1)}, u32[]{:S(2)}, u32[]{:S(2)}) collective-permute-start(bf16[4,8,16,512]{3,2,1,0:T(8,128)(2,1)S(1)} %get-tuple-element.13), channel_id=1, source_target_pairs={{0,32},{2,130},{16,48},{18,146},{32,0},{34,162},{48,16},{50,178},{... | collective-permute-start | bytes 1572872 | tf_op jit(solution)/shard_map/ppermute | solution.py:175
  47.6 0.3 collective-permute-start.7
  48.0 2.3 %collective-permute-start.9 = (bf16[4,8,16,512]{3,2,1,0:T(8,128)(2,1)S(1)}, bf16[4,8,16,512]{3,2,1,0:T(8,128)(2,1)}, u32[]{:S(2)}, u32[]{:S(2)}) collective-permute-start(bf16[4,8,16,512]{3,2,1,0:T(8,128)(2,1)S(1)} %get-tuple-element.13), channel_id=1, source_target_pairs={{0,48},{2,194},{16,0},{18,210},{32,16},{34,226},{48,32},{50,242},{... | collective-permute-start | bytes 1572872 | tf_op jit(solution)/shard_map/ppermute | solution.py:175
  50.3 1.1 %constant_dynamic-slice_fusion = (bf16[32,1,8,768]{3,2,1,0:T(8,128)(2,1)}, bf16[32,1,8,768]{3,2,1,0:T(8,128)(2,1)}, bf16[32,1,8,768]{3,2,1,0:T(8,128)(2,1)}) fusion(bf16[32,4,8,768]{3,2,1,0:T(8,128)(2,1)S(1)} %all-to-all-done, s32[]{:T(128)S(6)} %select_n.55, s32[]{:T(128)S(6)} %select_n.54, s32[]{:T(128)S(6)} %select_n.53), kind=kLoop, calls=%fused_computation.21 | loop fusion | bytes 2359308 | tf_op jit(solution)/shard_map/dynamic_slice | solution.py:220
  51.4 4.1 %collective-permute-start.3 = (bf16[32,1,8,768]{3,2,1,0:T(8,128)(2,1)}, bf16[32,1,8,768]{3,2,1,0:T(8,128)(2,1)}, u32[]{:S(2)}, u32[]{:S(2)}) collective-permute-start(bf16[32,1,8,768]{3,2,1,0:T(8,128)(2,1)} %get-tuple-element.9), channel_id=1, source_target_pairs={{0,13},{2,15},{4,0},{6,2},{8,4},{10,6},{12,8},{14,10},{1,12},{3,14... | collective-permute-start | bytes 1179656 | tf_op jit(solution)/shard_map/ppermute | solution.py:221
  55.5 2.9 %collective-permute-start.2 = (bf16[32,1,8,768]{3,2,1,0:T(8,128)(2,1)}, bf16[32,1,8,768]{3,2,1,0:T(8,128)(2,1)}, u32[]{:S(2)}, u32[]{:S(2)}) collective-permute-start(bf16[32,1,8,768]{3,2,1,0:T(8,128)(2,1)} %get-tuple-element.10), channel_id=1, source_target_pairs={{0,8},{2,11},{4,12},{6,15},{8,1},{10,2},{12,5},{14,6},{1,9},{3,10}... | collective-permute-start | bytes 1179656 | tf_op jit(solution)/shard_map/ppermute | solution.py:221
  58.4 0.7 collective-permute-start.1
  59.1 1.7 %collective-permute-done.7 = bf16[4,8,16,512]{3,2,1,0:T(8,128)(2,1)} collective-permute-done((bf16[4,8,16,512]{3,2,1,0:T(8,128)(2,1)S(1)}, bf16[4,8,16,512]{3,2,1,0:T(8,128)(2,1)}, u32[]{:S(2)}, u32[]{:S(2)}) %collective-permute-start.7) | collective-permute-done | bytes 524320 | tf_op jit(solution)/shard_map/ppermute | solution.py:175
  60.8 2.8 %pad_maximum_fusion.near_hbm = bf16[4,4,8,16,512]{4,3,2,1,0:T(8,128)(2,1)} fusion(bf16[1,4,8,16,512]{4,3,2,1,0:T(8,128)(2,1)} %bitcast.18, bf16[1,4,8,16,512]{4,3,2,1,0:T(8,128)(2,1)S(1)} %bitcast.30, bf16[1,4,8,16,512]{4,3,2,1,0:T(8,128)(2,1)} %bitcast.16, bf16[1,4,8,16,512]{4,3,2,1,0:T(8,128)(2,1)S(1)} %get-tuple-element.12), kind=kLoop, calls=%fused_computation.1 | loop fusion | flops 3145728 | bytes 4194304 | tf_op jit(solution)/shard_map/stack | solution.py:180
  63.6 1.4 %collective-permute-start.10 = (bf16[4,4,8,16,512]{4,3,2,1,0:T(8,128)(2,1)}, bf16[4,4,8,16,512]{4,3,2,1,0:T(8,128)(2,1)}, u32[]{:S(2)}, u32[]{:S(2)}) collective-permute-start(bf16[4,4,8,16,512]{4,3,2,1,0:T(8,128)(2,1)} %pad_maximum_fusion.near_hbm), channel_id=1, source_target_pairs={{0,2},{2,0},{1,3},{3,1},{4,6},{6,4},{5,7},{7,5},{8,10},{10,8},{9,1... | collective-permute-start | bytes 6291464 | tf_op jit(solution)/shard_map/ppermute | solution.py:225
  65.0 0.6 dynamic_slice.19
  65.6 0.9 copy.17.rows_ref
  66.5 0.6 stack.53.place_ref
  67.1 0.8 fusion.4.occ_ref
  67.9 5.7 %collective-permute-done.2 = bf16[32,1,8,768]{3,2,1,0:T(8,128)(2,1)} collective-permute-done((bf16[32,1,8,768]{3,2,1,0:T(8,128)(2,1)}, bf16[32,1,8,768]{3,2,1,0:T(8,128)(2,1)}, u32[]{:S(2)}, u32[]{:S(2)}) %collective-permute-start.2) | collective-permute-done | bytes 393248 | tf_op jit(solution)/shard_map/ppermute | solution.py:221
  73.6 1.7 %collective-permute-done.1 = bf16[32,1,8,768]{3,2,1,0:T(8,128)(2,1)} collective-permute-done((bf16[32,1,8,768]{3,2,1,0:T(8,128)(2,1)}, bf16[32,1,8,768]{3,2,1,0:T(8,128)(2,1)}, u32[]{:S(2)}, u32[]{:S(2)}) %collective-permute-start.1) | collective-permute-done | bytes 393248 | tf_op jit(solution)/shard_map/ppermute | solution.py:221
  75.3 1.2 %arrived.1.place_ref = s32[5]{0:T(128)} custom-call(s32[5]{0:T(128)} %stack.53.place_ref, bf16[16,2,8,768]{3,2,1,0:T(8,128)(2,1)} %bitcast.7.refs_0_.one_hbm, bf16[16,2,8,768]{3,2,1,0:T(8,128)(2,1)} %bitcast.8.refs_1_.two_hbm, bf16[16,2,8,768]{3,2,1,0:T(8,128)(2,1)} %bitcast.9.refs_2_.three_hbm), custom_call_target="tpu_custom_call" | custom-call | flops 20000000000 | tf_op jit(solution)/shard_map/arrived/pallas_call | solution.py:155
  76.5 13.5 %particle.1 = f32[2,512,256]{2,1,0:T(8,128)} custom-call(s32[5]{0:T(128)} %arrived.1.place_ref, f32[2]{0:T(128)} %fusion.4.occ_ref, bf16[16,2,4,8,768]{4,3,2,1,0:T(8,128)(2,1)} %bitcast.27, bf16[16,2,8,768]{3,2,1,0:T(8,128)(2,1)} %bitcast.7.refs_0_.one_hbm, bf16[16,2,8,768]{3,2,1,0:T(8,128)(2,1)} %bitcast.8.refs_1_.two_hbm, ...), custom_call_target="tpu_custom_call" | custom-call | flops 8589934592 | bytes 8388608 | tf_op jit(solution)/shard_map/particle/pallas_call | solution.py:125
  (26 shorter events, 0.5 us)
Async XLA Ops:
  0.0 10.5 %copy-start = (bf16[256,256]{1,0:T(8,128)(2,1)S(1)}, bf16[256,256]{1,0:T(8,128)(2,1)}, u32[]{:S(2)}) copy-start(bf16[256,256]{1,0:T(8,128)(2,1)} %param.7) | copy-start | bytes 393220
  0.0 10.2 %copy-start.2 = (bf16[256,4,512]{2,1,0:T(4,128)(2,1)S(1)}, bf16[256,4,512]{2,1,0:T(4,128)(2,1)}, u32[]{:S(2)}) copy-start(bf16[256,4,512]{2,1,0:T(4,128)(2,1)} %param.6) | copy-start | bytes 3145732
  1.0 12.4 %collective-permute-start = (bf16[8,16,512]{2,1,0:T(8,128)(2,1)S(1)}, bf16[8,16,512]{2,1,0:T(8,128)(2,1)S(1)}, u32[]{:S(2)}, u32[]{:S(2)}) collective-permute-start(bf16[8,16,512]{2,1,0:T(8,128)(2,1)S(1)} %constant_dynamic-slice_fusion.3), channel_id=1, source_target_pairs={{0,1},{1,0},{2,3},{3,2},{4,5},{5,4},{6,7},{7,6},{8,9},{9,8},{10,11... | collective-permute-start | bytes 393224 | tf_op jit(solution)/shard_map/ppermute | solution.py:203
  13.4 36.9 %all-to-all-start = ((bf16[32,4,8,768]{3,2,1,0:T(8,128)(2,1)}), bf16[32,4,8,768]{3,2,1,0:T(8,128)(2,1)S(1)}, u32[]{:S(2)}, u32[]{:S(2)}) async-start(bf16[32,4,8,768]{3,2,1,0:T(8,128)(2,1)} %bitcast.6), calls=%async_computation | async-start | bytes 3145728 | tf_op jit(solution)/shard_map/all_to_all | solution.py:217
  21.4 20.5 %collective-permute-start.6 = (bf16[8,16,512]{2,1,0:T(8,128)(2,1)S(1)}, bf16[8,16,512]{2,1,0:T(8,128)(2,1)S(1)}, u32[]{:S(2)}, u32[]{:S(2)}) collective-permute-start(bf16[8,16,512]{2,1,0:T(8,128)(2,1)S(1)} %collective-permute-done), channel_id=1, source_target_pairs={{0,192},{2,50},{16,208},{18,2},{32,224},{34,18},{48,240},{50,34},{... | collective-permute-start | bytes 393224 | tf_op jit(solution)/shard_map/ppermute | solution.py:175
  24.1 20.1 %collective-permute-start.5 = (bf16[8,16,512]{2,1,0:T(8,128)(2,1)S(1)}, bf16[8,16,512]{2,1,0:T(8,128)(2,1)S(1)}, u32[]{:S(2)}, u32[]{:S(2)}) collective-permute-start(bf16[8,16,512]{2,1,0:T(8,128)(2,1)S(1)} %collective-permute-done), channel_id=1, source_target_pairs={{0,128},{2,34},{16,144},{18,50},{32,160},{34,2},{48,176},{50,18},{... | collective-permute-start | bytes 393224 | tf_op jit(solution)/shard_map/ppermute | solution.py:175
  24.7 20.4 %collective-permute-start.4 = (bf16[8,16,512]{2,1,0:T(8,128)(2,1)S(1)}, bf16[8,16,512]{2,1,0:T(8,128)(2,1)S(1)}, u32[]{:S(2)}, u32[]{:S(2)}) collective-permute-start(bf16[8,16,512]{2,1,0:T(8,128)(2,1)S(1)} %collective-permute-done), channel_id=1, source_target_pairs={{0,64},{2,18},{16,80},{18,34},{32,96},{34,50},{48,112},{50,2},{64,... | collective-permute-start | bytes 393224 | tf_op jit(solution)/shard_map/ppermute | solution.py:175
  45.1 13.3 %collective-permute-start.8 = (bf16[4,8,16,512]{3,2,1,0:T(8,128)(2,1)S(1)}, bf16[4,8,16,512]{3,2,1,0:T(8,128)(2,1)S(1)}, u32[]{:S(2)}, u32[]{:S(2)}) collective-permute-start(bf16[4,8,16,512]{3,2,1,0:T(8,128)(2,1)S(1)} %get-tuple-element.13), channel_id=1, source_target_pairs={{0,32},{2,130},{16,48},{18,146},{32,0},{34,162},{48,16},{50,178},{... | collective-permute-start | bytes 1572872 | tf_op jit(solution)/shard_map/ppermute | solution.py:175
  47.6 13.1 %collective-permute-start.7 = (bf16[4,8,16,512]{3,2,1,0:T(8,128)(2,1)S(1)}, bf16[4,8,16,512]{3,2,1,0:T(8,128)(2,1)}, u32[]{:S(2)}, u32[]{:S(2)}) collective-permute-start(bf16[4,8,16,512]{3,2,1,0:T(8,128)(2,1)S(1)} %get-tuple-element.13), channel_id=1, source_target_pairs={{0,16},{2,66},{16,32},{18,82},{32,48},{34,98},{48,0},{50,114},{64,... | collective-permute-start | bytes 1572872 | tf_op jit(solution)/shard_map/ppermute | solution.py:175
  48.0 12.8 %collective-permute-start.9 = (bf16[4,8,16,512]{3,2,1,0:T(8,128)(2,1)S(1)}, bf16[4,8,16,512]{3,2,1,0:T(8,128)(2,1)}, u32[]{:S(2)}, u32[]{:S(2)}) collective-permute-start(bf16[4,8,16,512]{3,2,1,0:T(8,128)(2,1)S(1)} %get-tuple-element.13), channel_id=1, source_target_pairs={{0,48},{2,194},{16,0},{18,210},{32,16},{34,226},{48,32},{50,242},{... | collective-permute-start | bytes 1572872 | tf_op jit(solution)/shard_map/ppermute | solution.py:175
  50.3 13.3 %copy-start.1 = (bf16[32,4,8,768]{3,2,1,0:T(8,128)(2,1)}, bf16[32,4,8,768]{3,2,1,0:T(8,128)(2,1)S(1)}, u32[]{:S(2)}) copy-start(bf16[32,4,8,768]{3,2,1,0:T(8,128)(2,1)S(1)} %all-to-all-done) | copy-start | bytes 4718596
  51.4 16.4 %collective-permute-start.3 = (bf16[32,1,8,768]{3,2,1,0:T(8,128)(2,1)}, bf16[32,1,8,768]{3,2,1,0:T(8,128)(2,1)}, u32[]{:S(2)}, u32[]{:S(2)}) collective-permute-start(bf16[32,1,8,768]{3,2,1,0:T(8,128)(2,1)} %get-tuple-element.9), channel_id=1, source_target_pairs={{0,13},{2,15},{4,0},{6,2},{8,4},{10,6},{12,8},{14,10},{1,12},{3,14... | collective-permute-start | bytes 1179656 | tf_op jit(solution)/shard_map/ppermute | solution.py:221
  55.5 18.1 %collective-permute-start.2 = (bf16[32,1,8,768]{3,2,1,0:T(8,128)(2,1)}, bf16[32,1,8,768]{3,2,1,0:T(8,128)(2,1)}, u32[]{:S(2)}, u32[]{:S(2)}) collective-permute-start(bf16[32,1,8,768]{3,2,1,0:T(8,128)(2,1)} %get-tuple-element.10), channel_id=1, source_target_pairs={{0,8},{2,11},{4,12},{6,15},{8,1},{10,2},{12,5},{14,6},{1,9},{3,10}... | collective-permute-start | bytes 1179656 | tf_op jit(solution)/shard_map/ppermute | solution.py:221
  58.4 16.9 %collective-permute-start.1 = (bf16[32,1,8,768]{3,2,1,0:T(8,128)(2,1)}, bf16[32,1,8,768]{3,2,1,0:T(8,128)(2,1)}, u32[]{:S(2)}, u32[]{:S(2)}) collective-permute-start(bf16[32,1,8,768]{3,2,1,0:T(8,128)(2,1)} %get-tuple-element.11), channel_id=1, source_target_pairs={{0,4},{2,6},{4,8},{6,10},{8,12},{10,14},{12,1},{14,3},{1,5},{3,7},... | collective-permute-start | bytes 1179656 | tf_op jit(solution)/shard_map/ppermute | solution.py:221
  60.8 4.2 %copy-start.5 = (s32[2]{0:T(128)S(1)}, s32[2]{0:T(128)}, u32[]{:S(2)}) copy-start(s32[2]{0:T(128)} %param.9) | copy-start | bytes 28
  60.8 4.2 %copy-start.3 = (f32[512]{0:T(512)S(1)}, f32[512]{0:T(512)}, u32[]{:S(2)}) copy-start(f32[512]{0:T(512)} %param.11) | copy-start | bytes 6148
  60.8 6.3 %copy-start.4 = (f32[16]{0:T(128)S(1)}, f32[16]{0:T(128)}, u32[]{:S(2)}) copy-start(f32[16]{0:T(128)} %param.10) | copy-start | bytes 196
  63.6 12.9 %collective-permute-start.10 = (bf16[4,4,8,16,512]{4,3,2,1,0:T(8,128)(2,1)}, bf16[4,4,8,16,512]{4,3,2,1,0:T(8,128)(2,1)}, u32[]{:S(2)}, u32[]{:S(2)}) collective-permute-start(bf16[4,4,8,16,512]{4,3,2,1,0:T(8,128)(2,1)} %pad_maximum_fusion.near_hbm), channel_id=1, source_target_pairs={{0,2},{2,0},{1,3},{3,1},{4,6},{6,4},{5,7},{7,5},{8,10},{10,8},{9,1... | collective-permute-start | bytes 6291464 | tf_op jit(solution)/shard_map/ppermute | solution.py:225

commit v8 on v6

v8 whole, which is shorter than its diff:
```python
import jax
import jax.numpy as jnp
from jax import lax
from jax.experimental import pallas as pl
from jax.experimental.pallas import tpu as pltpu
from jax.sharding import Mesh, PartitionSpec as P

NO = 16
AXES = ("x", "y", "z", "core", "aux")
PAIR = AXES[:4]
SIDE = 4
OWN_LIMIT = 48 * 1024 * 1024
OTHER_LIMIT = 48 * 1024 * 1024
WEIGHT = 4
NT = (((1,), (1,)), ((), ()))


def turned(amps_ref, cols):
    nv = cols.shape[1]
    return jnp.concatenate(
        [
            lax.dot_general(amps_ref[p * nv : (p + 1) * nv], cols, NT, preferred_element_type=jnp.float32).astype(jnp.bfloat16)
            for p in range(2)
        ],
        axis=1,
    )


def split_pairs(first, second):
    rows = first.shape[1] // 2
    low = lax.broadcasted_iota(jnp.int32, first.shape, 1) < rows
    return (
        jnp.where(low, first, pltpu.roll(second, rows, axis=1)),
        jnp.where(low, pltpu.roll(first, rows, axis=1), second),
    )


def add_vectors(nq, ready, vector, columns, amps_ref, right, total, started):
    ready(0)
    right[0] = turned(amps_ref, columns(0))
    for q in range(nq):
        if q + 1 < nq:
            ready(q + 1)
            right[(q + 1) % 2] = turned(amps_ref, columns(q + 1))
        product = jnp.dot(vector(q), right[q % 2], preferred_element_type=jnp.float32)
        total[...] = total[...] + product if q or started else product


def own_kernel(place_ref, got_hbm, own_hbm, total, amps_ref, got_ref, own, right, sems):
    nq, nv, _ = own.shape
    half = nv // 2
    fetch = pltpu.make_async_copy(got_hbm.at[:, :, :, pl.ds(0, nv)], got_ref, sems.at[nq])
    fetch.start()
    copies = [pltpu.make_async_copy(own_hbm.at[q], own.at[q], sems.at[q]) for q in range(nq)]
    for copy in copies:
        copy.start()
    fetch.wait()
    couples, _, both, _ = got_ref.shape
    chunk = couples // 8
    for i in range(8):
        tiles = [got_ref[pl.ds(i * chunk, chunk), side].astype(jnp.float32) for side in range(2)]
        for p, tile in enumerate(split_pairs(*tiles)):
            rows = chunk * both
            amps_ref[p * nv + i * rows : p * nv + (i + 1) * rows] = tile.reshape(rows, nv).astype(jnp.bfloat16)
    start = pl.multiple_of(place_ref[0] * half, half)
    add_vectors(
        nq, lambda q: copies[q].wait(), lambda q: own[q], lambda q: own[q, pl.ds(start, half), :],
        amps_ref, right, total, False,
    )


def other_kernel(*refs):
    place_ref, occ_ref, got_hbm, base_hbm, amps_hbm = refs[:5]
    sources, (rows_ref, cols_ref, out_hbm) = refs[5 : 5 + 2 * SIDE], refs[5 + 2 * SIDE : 8 + 2 * SIDE]
    got_ref, amps_ref, other, right, total, out_ref, sems = refs[8 + 2 * SIDE :]
    nq, slots, _, nv = other.shape
    half, part = nv // 2, nq // 2
    aux, core, x0, y0 = (place_ref[i] for i in range(4))
    load = pltpu.make_async_copy(amps_hbm, amps_ref, sems.at[6])
    load.start()
    for h in range(2):
        for owner, blocks in ((core, sources[:SIDE]), (1 - core, sources[SIDE:])):
            for outer, src in enumerate(blocks):
                for inner in range(SIDE):
                    dx = inner + owner * (outer - inner)
                    dy = outer + owner * (inner - outer)
                    x, y = lax.rem(x0 + SIDE - dx, SIDE), lax.rem(y0 + SIDE - dy, SIDE)
                    pltpu.make_async_copy(
                        src.at[inner, pl.ds(h * part, part)],
                        other.at[pl.ds(h * part, part), (owner * SIDE + x) * SIDE + y],
                        sems.at[h],
                    ).start()
    fill = pltpu.make_async_copy(base_hbm, total, sems.at[2])
    fill.start()
    fetch = pltpu.make_async_copy(got_hbm.at[:, :, :, pl.ds(nv, half)], got_ref, sems.at[3])
    fetch.start()

    def ready(q):
        if q % part == 0:
            block = other.at[pl.ds(q, part)]
            pltpu.make_async_copy(block, block, sems.at[q // part]).wait()

    fill.wait()
    load.wait()
    add_vectors(
        nq, ready, lambda q: other[q].reshape(nv, nv),
        lambda q: other[q, pl.ds(aux * (slots // 2), slots // 2)].reshape(half, nv),
        amps_ref, right, total, True,
    )
    fetch.wait()
    level = rows_ref[...] + cols_ref[...]
    tiles = [got_ref[:, side].astype(jnp.float32) for side in range(2)]
    stores = []
    for p, hole in enumerate(split_pairs(*tiles)):
        value = hole.reshape(nv, half) + total[:, p * half : (p + 1) * half]
        out_ref[p] = value / (level - occ_ref[p])
        stores.append(pltpu.make_async_copy(out_ref.at[p], out_hbm.at[p], sems.at[4 + p]))
        stores[p].start()
    for store in stores:
        store.wait()


def estimate(nq, nv):
    return pl.CostEstimate(flops=4 * nq * nv**3, bytes_accessed=2 * nq * nv * nv, transcendentals=0)


VMEM = pl.BlockSpec(memory_space=pltpu.VMEM)
SMEM = pl.BlockSpec(memory_space=pltpu.SMEM)
ANYWHERE = pl.BlockSpec(memory_space=pl.ANY)


def own_vectors(place, got, own):
    nq, nv, _ = own.shape
    return pl.pallas_call(
        own_kernel,
        in_specs=[SMEM, ANYWHERE, ANYWHERE],
        out_specs=[VMEM, VMEM],
        out_shape=[
            jax.ShapeDtypeStruct((nv, nv), jnp.float32),
            jax.ShapeDtypeStruct((2 * nv, nv), jnp.bfloat16),
        ],
        scratch_shapes=[
            pltpu.VMEM((*got.shape[:3], nv), jnp.bfloat16),
            pltpu.VMEM((nq, nv, nv), jnp.bfloat16),
            pltpu.VMEM((2, nv, nv), jnp.bfloat16),
            pltpu.SemaphoreType.DMA((nq + 1,)),
        ],
        compiler_params=pltpu.CompilerParams(vmem_limit_bytes=OWN_LIMIT),
        cost_estimate=estimate(WEIGHT * nq, nv),
        name="own_vectors",
    )(place, got, own)


def other_vectors(place, occ_sum, got, base, amps, near, far, rows, cols):
    nq, strip, nv = near[0].shape[1:]
    return pl.pallas_call(
        other_kernel,
        in_specs=[SMEM, SMEM, *[ANYWHERE] * (3 + 2 * SIDE), VMEM, VMEM],
        out_specs=ANYWHERE,
        out_shape=jax.ShapeDtypeStruct((2, nv, nv // 2), jnp.float32),
        scratch_shapes=[
            pltpu.VMEM((*got.shape[:3], nv // 2), jnp.bfloat16),
            pltpu.VMEM(amps.shape, jnp.bfloat16),
            pltpu.VMEM((nq, nv // strip, strip, nv), jnp.bfloat16),
            pltpu.VMEM((2, nv, nv), jnp.bfloat16),
            pltpu.VMEM((nv, nv), jnp.float32),
            pltpu.VMEM((2, nv, nv // 2), jnp.float32),
            pltpu.SemaphoreType.DMA((7,)),
        ],
        compiler_params=pltpu.CompilerParams(vmem_limit_bytes=OTHER_LIMIT),
        cost_estimate=estimate(nq, nv),
        name="other_vectors",
    )(place, occ_sum, got, base, amps, *near, *far, rows, cols)


def plane_shift(block, shift, first_core_axis):
    pairs = []
    for x in range(SIDE):
        for y in range(SIDE):
            for core in range(2):
                if core == first_core_axis:
                    to = x * SIDE + (y + shift) % SIDE
                else:
                    to = (x + shift) % SIDE * SIDE + y
                pairs.append(((x * SIDE + y) * 2 + core, to * 2 + core))
    return lax.ppermute(block, ("x", "y", "core"), pairs)


def gather_plane(block):
    shifts = range(1, SIDE)
    block = jnp.stack([block] + [plane_shift(block, d, 1) for d in shifts])
    return [block] + [plane_shift(block, d, 0) for d in shifts]


def other_core(block):
    return lax.ppermute(block, "core", [(0, 1), (1, 0)])


def shards(amplitudes, ladder, cholesky, pair_ids, occ_energy, vir_energy):
    n_pair, rows, n_virt = amplitudes.shape
    half_width = n_virt // lax.axis_size("aux")
    aux, core = lax.axis_index("aux"), lax.axis_index("core")
    x, y = lax.axis_index("x"), lax.axis_index("y")
    strip = half_width // (SIDE * SIDE)

    slot = (core * SIDE + x) * SIDE + y
    piece = lax.dynamic_slice_in_dim(cholesky, slot * strip, strip, 1)
    piece = lax.ppermute(piece, "aux", [(0, 1), (1, 0)])

    mine = lax.dynamic_slice_in_dim(amplitudes, aux * half_width, half_width, 2)
    hole = jnp.dot(
        ladder, mine.reshape(n_pair, -1), preferred_element_type=jnp.float32
    ).astype(jnp.bfloat16)
    packed = jnp.concatenate(
        [amplitudes.reshape(-1, 2 * rows, n_virt), hole.reshape(-1, 2 * rows, half_width)], axis=2
    )
    packed, piece = lax.optimization_barrier((packed, piece))
    got = lax.all_to_all(packed, PAIR, split_axis=0, concat_axis=0, tiled=True)
    got = got.reshape(-1, 2, *got.shape[1:])
    near = gather_plane(piece)

    orbitals = jnp.arange(NO, dtype=jnp.int32)
    first_hot = (pair_ids[:, None] // NO == orbitals[None, :]).astype(jnp.float32)
    second_hot = (pair_ids[:, None] % NO == orbitals[None, :]).astype(jnp.float32)
    occ_sum = jnp.sum((first_hot + second_hot) * occ_energy[None, :], axis=1)
    vir_cols = lax.dynamic_slice_in_dim(vir_energy, aux * half_width, half_width, 0)
    place = jnp.stack([aux, core, x, y]).astype(jnp.int32)

    base, pair_amps = own_vectors(place, got, cholesky)
    *late, base = lax.optimization_barrier((*near[1:], base))
    near = [near[0], *late]
    far = [other_core(block) for block in near]
    return other_vectors(
        place, occ_sum, got, base, pair_amps, near, far, vir_energy[:, None], vir_cols[None, :]
    )


def solution(mesh):
    fine = Mesh(mesh.devices.reshape(SIDE, SIDE, SIDE, 2, 2), AXES)
    in_specs = (P(None, PAIR, None), P(), P("aux", None, None), P(PAIR), P(), P())
    out_specs = P(PAIR, None, "aux")
    return jax.shard_map(shards, mesh=fine, in_specs=in_specs, out_specs=out_specs, check_vma=False)
```

time: 81.9 us -> 89.9 us (1.098)
  waiting for transfers between devices: 28.2 us -> 35.2 us
  local copies, waits for them, and re-layouts: 4.83 us -> 7.54 us
  starting transfers between devices: 31.6 us -> 29.4 us
  Pallas kernels: 13.5 us -> 15.1 us
  other arithmetic: 2.91 us -> 1.62 us
    all_to_all x1, waiting for transfers between devices: 0.01 us -> 19.5 us  [shards(): got = lax.all_to_all(packed, PAIR, split_axis=0, concat_axis=0, tiled=True)]
    ppermute x6, waiting for transfers between devices: 27 us -> 13.4 us  [plane_shift(): return lax.ppermute(block, ('x', 'y', 'core'), pairs)]
    unnamed x13 -> x17, local copies, waits for them, and re-layouts: 0.12 us -> 3.29 us
    ppermute x6, starting transfers between devices: 10 us -> 7.6 us  [plane_shift(): return lax.ppermute(block, ('x', 'y', 'core'), pairs)]
    pallas_call x1 -> x2, Pallas kernels: 13.5 us -> 15.1 us  [the longest x1 8.15 us: other_vectors(): pl.pallas_call(other_kernel, in_specs=[SMEM, SMEM, *[ANYWHERE] * (3 + 2 *...]
    ppermute x1 -> x4, starting transfers between devices: 0.4 us -> 2.02 us  [other_core(): return lax.ppermute(block, 'core', [(0, 1), (1, 0)])]
    all_to_all x1, starting transfers between devices: 13.4 us -> 12 us  [shards(): got = lax.all_to_all(packed, PAIR, split_axis=0, concat_axis=0, tiled=True)]
    ppermute x1 -> x4, waiting for transfers between devices: 1.2 us -> 2.28 us  [other_core(): return lax.ppermute(block, 'core', [(0, 1), (1, 0)])]
  transfers between devices with their start and end apart: 9 -> 12, of which waited for: 6 -> 6; matrix products, arithmetic and copies ran while one was open for 9% -> 6% of each run, Pallas kernels for 0% -> 8%
where the time goes in v8:
time: 89.9 us; the launch traced here: 89.6 us
  waiting for transfers between devices  35.2 us (39%)
  starting transfers between devices  29.4 us (33%)
  Pallas kernels  15.1 us (17%)
  local copies, waits for them, and re-layouts  7.54 us (8%)
  other arithmetic  1.62 us (2%)
    all_to_all x1, waiting for transfers between devices, shards(): got = lax.all_to_all(packed, PAIR, split_axis=0, concat_axis=0, tiled=True)  19.5 us
    ppermute x6, waiting for transfers between devices, plane_shift(): return lax.ppermute(block, ('x', 'y', 'core'), pairs)  13.4 us
    all_to_all x1, starting transfers between devices, shards(): got = lax.all_to_all(packed, PAIR, split_axis=0, concat_axis=0, tiled=True)  12 us
    pallas_call x1, Pallas kernels, other_vectors(): pl.pallas_call(other_kernel, in_specs=[SMEM, SMEM, *[ANYWHERE] * (3 + 2 *...  8.15 us
    ppermute x1, starting transfers between devices, shards(): piece = lax.ppermute(piece, 'aux', [(0, 1), (1, 0)])  7.83 us
    ppermute x6, starting transfers between devices, plane_shift(): return lax.ppermute(block, ('x', 'y', 'core'), pairs)  7.6 us
    pallas_call x1, Pallas kernels, own_vectors(): pl.pallas_call(own_kernel, in_specs=[SMEM, ANYWHERE, ANYWHERE], out_specs...  7 us
    unnamed x17, local copies, waits for them, and re-layouts  3.29 us
  transfers between devices with their start and end apart: 12, of which 6 were waited for; matrix products, arithmetic and copies ran while one was open for 6% of the time, Pallas kernels for 8%

profile of v8, /device:TPU:1, one launch (start us, length us, event | category | flops | bytes accessed | tf_op | source)
XLA Modules:
  0.0 89.6 jit_solution(15077852061491900873)
XLA Ops:
  0.0 0.9 %constant_dynamic-slice_fusion = bf16[8,16,512]{2,1,0:T(8,128)(2,1)S(1)} fusion(bf16[8,512,512]{2,1,0:T(8,128)(2,1)} %own_hbm.1, s32[]{:T(128)S(6)} %select_n.24), kind=kLoop, calls=%fused_computation.15 | loop fusion | bytes 262148 | tf_op jit(solution)/shard_map/dynamic_slice | solution.py:207
  1.0 7.8 %collective-permute-start = (bf16[8,16,512]{2,1,0:T(8,128)(2,1)S(1)}, bf16[8,16,512]{2,1,0:T(8,128)(2,1)S(1)}, u32[]{:S(2)}, u32[]{:S(2)}) collective-permute-start(bf16[8,16,512]{2,1,0:T(8,128)(2,1)S(1)} %constant_dynamic-slice_fusion), channel_id=1, source_target_pairs={{0,1},{1,0},{2,3},{3,2},{4,5},{5,4},{6,7},{7,6},{8,9},{9,8},{10,11... | collective-permute-start | bytes 393224 | tf_op jit(solution)/shard_map/ppermute | solution.py:208
  8.8 1.3 %reshape.39 = bf16[128,8,512]{2,1,0:T(8,128)(2,1)S(1)} reshape(bf16[256,4,512]{2,1,0:T(4,128)(2,1)} %param.6) | data formatting | bytes 2097152 | tf_op jit(solution)/shard_map/reshape | solution.py:215
  10.1 1.2 %constant_dynamic-slice_fusion.1 = bf16[256,4,256]{2,1,0:T(4,128)(2,1)S(1)} fusion(bf16[256,4,512]{2,1,0:T(4,128)(2,1)} %param.6, s32[]{:T(128)S(6)} %select_n.23), kind=kLoop, calls=%fused_computation.16 | loop fusion | bytes 1048580 | tf_op jit(solution)/shard_map/dynamic_slice | solution.py:210
  11.4 0.1 copy.11
  11.5 0.4 fusion
  11.8 0.2 copy.9
  12.0 0.3 reshape.41
  12.4 1.3 %pad_maximum_fusion = bf16[128,8,768]{2,1,0:T(8,128)(2,1)} fusion(bf16[128,8,256]{2,1,0:T(8,128)(2,1)S(1)} %reshape.41, bf16[128,8,512]{2,1,0:T(8,128)(2,1)S(1)} %reshape.39), kind=kLoop, calls=%fused_computation | loop fusion | flops 3145728 | bytes 3145728 | tf_op jit(solution)/shard_map/concatenate | solution.py:214
  13.7 12.0 %all-to-all-start = ((bf16[128,8,768]{2,1,0:T(8,128)(2,1)}), bf16[128,8,768]{2,1,0:T(8,128)(2,1)S(1)}, u32[]{:S(2)}, u32[]{:S(2)}) async-start(bf16[128,8,768]{2,1,0:T(8,128)(2,1)} %pad_maximum_fusion), calls=%async_computation | async-start | bytes 3145728 | tf_op jit(solution)/shard_map/all_to_all | solution.py:218
  25.6 2.7 %collective-permute-start.3 = (bf16[8,16,512]{2,1,0:T(8,128)(2,1)S(1)}, bf16[8,16,512]{2,1,0:T(8,128)(2,1)S(1)}, u32[]{:S(2)}, u32[]{:S(2)}) collective-permute-start(bf16[8,16,512]{2,1,0:T(8,128)(2,1)S(1)} %collective-permute-done), channel_id=1, source_target_pairs={{0,192},{2,50},{16,208},{18,2},{32,224},{34,18},{48,240},{50,34},{... | collective-permute-start | bytes 393224 | tf_op jit(solution)/shard_map/ppermute | solution.py:186
  28.4 0.5 collective-permute-start.2
  28.9 0.6 collective-permute-start.1
  29.5 7.4 %collective-permute-done.3 = bf16[8,16,512]{2,1,0:T(8,128)(2,1)S(1)} collective-permute-done((bf16[8,16,512]{2,1,0:T(8,128)(2,1)S(1)}, bf16[8,16,512]{2,1,0:T(8,128)(2,1)S(1)}, u32[]{:S(2)}, u32[]{:S(2)}) %collective-permute-start.3) | collective-permute-done | bytes 131104 | tf_op jit(solution)/shard_map/ppermute | solution.py:186
  36.9 3.7 %collective-permute-done.2 = bf16[8,16,512]{2,1,0:T(8,128)(2,1)S(1)} collective-permute-done((bf16[8,16,512]{2,1,0:T(8,128)(2,1)S(1)}, bf16[8,16,512]{2,1,0:T(8,128)(2,1)S(1)}, u32[]{:S(2)}, u32[]{:S(2)}) %collective-permute-start.2) | collective-permute-done | bytes 131104 | tf_op jit(solution)/shard_map/ppermute | solution.py:186
  40.6 2.3 %collective-permute-done.1 = bf16[8,16,512]{2,1,0:T(8,128)(2,1)S(1)} collective-permute-done((bf16[8,16,512]{2,1,0:T(8,128)(2,1)S(1)}, bf16[8,16,512]{2,1,0:T(8,128)(2,1)S(1)}, u32[]{:S(2)}, u32[]{:S(2)}) %collective-permute-start.1) | collective-permute-done | bytes 131104 | tf_op jit(solution)/shard_map/ppermute | solution.py:186
  43.2 2.6 %collective-permute-start.6 = (bf16[4,8,16,512]{3,2,1,0:T(8,128)(2,1)S(1)}, bf16[4,8,16,512]{3,2,1,0:T(8,128)(2,1)S(1)}, u32[]{:S(2)}, u32[]{:S(2)}) collective-permute-start(bf16[4,8,16,512]{3,2,1,0:T(8,128)(2,1)S(1)} %pad_maximum_fusion.1.refs_5_), channel_id=1, source_target_pairs={{0,48},{2,194},{16,0},{18,210},{32,16},{34,226},{48,32},{50,242},{... | collective-permute-start | bytes 1572872 | tf_op jit(solution)/shard_map/ppermute | solution.py:186
  45.8 0.4 collective-permute-start.5
  46.2 0.8 collective-permute-start.4
  46.9 19.5 %all-to-all-done = bf16[128,8,768]{2,1,0:T(8,128)(2,1)S(1)} async-done(((bf16[128,8,768]{2,1,0:T(8,128)(2,1)}), bf16[128,8,768]{2,1,0:T(8,128)(2,1)S(1)}, u32[]{:S(2)}, u32[]{:S(2)}) %all-to-all-start) | async-done | bytes 1572896 | tf_op jit(solution)/shard_map/all_to_all | solution.py:218
  66.4 7.0 %own_vectors.1 = (f32[512,512]{1,0:T(8,128)S(1)}, bf16[1024,512]{1,0:T(8,128)(2,1)S(1)}) custom-call(s32[4]{0:T(128)S(1)} %pad_add_fusion.place_ref.refs_0_, bf16[64,2,8,768]{3,2,1,0:T(8,128)(2,1)S(1)} %bitcast.17, bf16[8,512,512]{2,1,0:T(8,128)(2,1)} %own_hbm.1), custom_call_target="tpu_custom_call" | custom-call | flops 17179869184 | bytes 16777216 | tf_op jit(solution)/shard_map/own_vectors/pallas_call | solution.py:134
  73.4 1.0 %copy-done.2 = f32[512,512]{1,0:T(8,128)} copy-done((f32[512,512]{1,0:T(8,128)}, f32[512,512]{1,0:T(8,128)S(1)}, u32[]{:S(2)}) %copy-start.2) | copy-done | bytes 1048600
  74.4 1.0 %copy-done.4 = bf16[1024,512]{1,0:T(8,128)(2,1)} copy-done((bf16[1024,512]{1,0:T(8,128)(2,1)}, bf16[1024,512]{1,0:T(8,128)(2,1)S(1)}, u32[]{:S(2)}) %copy-start.4) | copy-done | bytes 1048600
  75.4 1.4 %collective-permute-start.8 = (bf16[4,8,16,512]{3,2,1,0:T(8,128)(2,1)}, bf16[4,8,16,512]{3,2,1,0:T(8,128)(2,1)S(1)}, u32[]{:S(2)}, u32[]{:S(2)}) collective-permute-start(bf16[4,8,16,512]{3,2,1,0:T(8,128)(2,1)} %collective-permute-done.4.refs_6_), channel_id=1, source_target_pairs={{0,2},{2,0},{1,3},{3,1},{4,6},{6,4},{5,7},{7,5},{8,10},{10,8},{9,1... | collective-permute-start | bytes 1572872 | tf_op jit(solution)/shard_map/ppermute | solution.py:196
  76.8 0.1 collective-permute-start.9
  76.9 0.4 collective-permute-start.10
  77.4 0.1 copy.10.refs_13_
  77.6 0.2 fusion.3.refs_1_
  77.8 0.8 collective-permute-done.8.refs_10_
  78.5 1.5 %collective-permute-done.9.refs_11_ = bf16[4,8,16,512]{3,2,1,0:T(8,128)(2,1)S(1)} collective-permute-done((bf16[4,8,16,512]{3,2,1,0:T(8,128)(2,1)}, bf16[4,8,16,512]{3,2,1,0:T(8,128)(2,1)S(1)}, u32[]{:S(2)}, u32[]{:S(2)}) %collective-permute-start.9) | collective-permute-done | bytes 524320 | tf_op jit(solution)/shard_map/ppermute | solution.py:196
  80.0 1.2 %copy-done.3 = f32[512,512]{1,0:T(8,128)S(1)} copy-done((f32[512,512]{1,0:T(8,128)S(1)}, f32[512,512]{1,0:T(8,128)}, u32[]{:S(2)}) %copy-start.3) | copy-done | bytes 1048600
  81.3 8.2 %other_vectors.1 = f32[2,512,256]{2,1,0:T(8,128)} custom-call(s32[4]{0:T(128)S(1)} %pad_add_fusion.place_ref.refs_0_, f32[2]{0:T(128)S(1)} %fusion.3.refs_1_, bf16[64,2,8,768]{3,2,1,0:T(8,128)(2,1)} %bitcast.18, f32[512,512]{1,0:T(8,128)S(1)} %copy-done.3, bf16[1024,512]{1,0:T(8,128)(2,1)} %copy-done.4, ...), custom_call_target="tpu_custom_call" | custom-call | flops 4294967296 | bytes 4194304 | tf_op jit(solution)/shard_map/other_vectors/pallas_call | solution.py:156
  (24 shorter events, 0.4 us)
Async XLA Ops:
  0.0 11.5 %copy-start = (bf16[256,256]{1,0:T(8,128)(2,1)S(1)}, bf16[256,256]{1,0:T(8,128)(2,1)}, u32[]{:S(2)}) copy-start(bf16[256,256]{1,0:T(8,128)(2,1)} %param.7) | copy-start | bytes 393220
  1.0 12.7 %collective-permute-start = (bf16[8,16,512]{2,1,0:T(8,128)(2,1)S(1)}, bf16[8,16,512]{2,1,0:T(8,128)(2,1)S(1)}, u32[]{:S(2)}, u32[]{:S(2)}) collective-permute-start(bf16[8,16,512]{2,1,0:T(8,128)(2,1)S(1)} %constant_dynamic-slice_fusion), channel_id=1, source_target_pairs={{0,1},{1,0},{2,3},{3,2},{4,5},{5,4},{6,7},{7,6},{8,9},{9,8},{10,11... | collective-permute-start | bytes 393224 | tf_op jit(solution)/shard_map/ppermute | solution.py:208
  13.7 52.7 %all-to-all-start = ((bf16[128,8,768]{2,1,0:T(8,128)(2,1)}), bf16[128,8,768]{2,1,0:T(8,128)(2,1)S(1)}, u32[]{:S(2)}, u32[]{:S(2)}) async-start(bf16[128,8,768]{2,1,0:T(8,128)(2,1)} %pad_maximum_fusion), calls=%async_computation | async-start | bytes 3145728 | tf_op jit(solution)/shard_map/all_to_all | solution.py:218
  25.6 11.3 %collective-permute-start.3 = (bf16[8,16,512]{2,1,0:T(8,128)(2,1)S(1)}, bf16[8,16,512]{2,1,0:T(8,128)(2,1)S(1)}, u32[]{:S(2)}, u32[]{:S(2)}) collective-permute-start(bf16[8,16,512]{2,1,0:T(8,128)(2,1)S(1)} %collective-permute-done), channel_id=1, source_target_pairs={{0,192},{2,50},{16,208},{18,2},{32,224},{34,18},{48,240},{50,34},{... | collective-permute-start | bytes 393224 | tf_op jit(solution)/shard_map/ppermute | solution.py:186
  28.4 12.3 %collective-permute-start.2 = (bf16[8,16,512]{2,1,0:T(8,128)(2,1)S(1)}, bf16[8,16,512]{2,1,0:T(8,128)(2,1)S(1)}, u32[]{:S(2)}, u32[]{:S(2)}) collective-permute-start(bf16[8,16,512]{2,1,0:T(8,128)(2,1)S(1)} %collective-permute-done), channel_id=1, source_target_pairs={{0,128},{2,34},{16,144},{18,50},{32,160},{34,2},{48,176},{50,18},{... | collective-permute-start | bytes 393224 | tf_op jit(solution)/shard_map/ppermute | solution.py:186
  28.9 14.1 %collective-permute-start.1 = (bf16[8,16,512]{2,1,0:T(8,128)(2,1)S(1)}, bf16[8,16,512]{2,1,0:T(8,128)(2,1)S(1)}, u32[]{:S(2)}, u32[]{:S(2)}) collective-permute-start(bf16[8,16,512]{2,1,0:T(8,128)(2,1)S(1)} %collective-permute-done), channel_id=1, source_target_pairs={{0,64},{2,18},{16,80},{18,34},{32,96},{34,50},{48,112},{50,2},{64,... | collective-permute-start | bytes 393224 | tf_op jit(solution)/shard_map/ppermute | solution.py:186
  43.1 34.7 %collective-permute-start.7 = (bf16[4,8,16,512]{3,2,1,0:T(8,128)(2,1)S(1)}, bf16[4,8,16,512]{3,2,1,0:T(8,128)(2,1)S(1)}, u32[]{:S(2)}, u32[]{:S(2)}) collective-permute-start(bf16[4,8,16,512]{3,2,1,0:T(8,128)(2,1)S(1)} %pad_maximum_fusion.1.refs_5_), channel_id=1, source_target_pairs={{0,2},{2,0},{1,3},{3,1},{4,6},{6,4},{5,7},{7,5},{8,10},{10,8},{9,1... | collective-permute-start | bytes 1572872 | tf_op jit(solution)/shard_map/ppermute | solution.py:196
  43.2 32.2 %collective-permute-start.6 = (bf16[4,8,16,512]{3,2,1,0:T(8,128)(2,1)S(1)}, bf16[4,8,16,512]{3,2,1,0:T(8,128)(2,1)S(1)}, u32[]{:S(2)}, u32[]{:S(2)}) collective-permute-start(bf16[4,8,16,512]{3,2,1,0:T(8,128)(2,1)S(1)} %pad_maximum_fusion.1.refs_5_), channel_id=1, source_target_pairs={{0,48},{2,194},{16,0},{18,210},{32,16},{34,226},{48,32},{50,242},{... | collective-permute-start | bytes 1572872 | tf_op jit(solution)/shard_map/ppermute | solution.py:186
  45.8 29.6 %collective-permute-start.5 = (bf16[4,8,16,512]{3,2,1,0:T(8,128)(2,1)S(1)}, bf16[4,8,16,512]{3,2,1,0:T(8,128)(2,1)}, u32[]{:S(2)}, u32[]{:S(2)}) collective-permute-start(bf16[4,8,16,512]{3,2,1,0:T(8,128)(2,1)S(1)} %pad_maximum_fusion.1.refs_5_), channel_id=1, source_target_pairs={{0,32},{2,130},{16,48},{18,146},{32,0},{34,162},{48,16},{50,178},{... | collective-permute-start | bytes 1572872 | tf_op jit(solution)/shard_map/ppermute | solution.py:186
  46.2 29.2 %collective-permute-start.4 = (bf16[4,8,16,512]{3,2,1,0:T(8,128)(2,1)S(1)}, bf16[4,8,16,512]{3,2,1,0:T(8,128)(2,1)}, u32[]{:S(2)}, u32[]{:S(2)}) collective-permute-start(bf16[4,8,16,512]{3,2,1,0:T(8,128)(2,1)S(1)} %pad_maximum_fusion.1.refs_5_), channel_id=1, source_target_pairs={{0,16},{2,66},{16,32},{18,82},{32,48},{34,98},{48,0},{50,114},{64,... | collective-permute-start | bytes 1572872 | tf_op jit(solution)/shard_map/ppermute | solution.py:186
  66.4 7.0 %copy-start.1 = (bf16[128,8,768]{2,1,0:T(8,128)(2,1)}, bf16[128,8,768]{2,1,0:T(8,128)(2,1)S(1)}, u32[]{:S(2)}) copy-start(bf16[128,8,768]{2,1,0:T(8,128)(2,1)S(1)} %all-to-all-done) | copy-start | bytes 4718596
  66.4 10.9 %copy-start.5 = (f32[512]{0:T(512)S(1)}, f32[512]{0:T(512)}, u32[]{:S(2)}) copy-start(f32[512]{0:T(512)} %param.11) | copy-start | bytes 6148
  66.4 11.1 %copy-start.7 = (s32[2]{0:T(128)S(1)}, s32[2]{0:T(128)}, u32[]{:S(2)}) copy-start(s32[2]{0:T(128)} %param.9) | copy-start | bytes 28
  66.4 11.2 %copy-start.6 = (f32[16]{0:T(128)S(1)}, f32[16]{0:T(128)}, u32[]{:S(2)}) copy-start(f32[16]{0:T(128)} %param.10) | copy-start | bytes 196
  73.4 1.0 %copy-start.2 = (f32[512,512]{1,0:T(8,128)}, f32[512,512]{1,0:T(8,128)S(1)}, u32[]{:S(2)}) copy-start(f32[512,512]{1,0:T(8,128)S(1)} %get-tuple-element.16.refs_3_) | copy-start | bytes 3145732
  74.4 1.0 %copy-start.4 = (bf16[1024,512]{1,0:T(8,128)(2,1)}, bf16[1024,512]{1,0:T(8,128)(2,1)S(1)}, u32[]{:S(2)}) copy-start(bf16[1024,512]{1,0:T(8,128)(2,1)S(1)} %get-tuple-element.17.refs_4_) | copy-start | bytes 3145732
  75.4 3.2 %collective-permute-start.8 = (bf16[4,8,16,512]{3,2,1,0:T(8,128)(2,1)}, bf16[4,8,16,512]{3,2,1,0:T(8,128)(2,1)S(1)}, u32[]{:S(2)}, u32[]{:S(2)}) collective-permute-start(bf16[4,8,16,512]{3,2,1,0:T(8,128)(2,1)} %collective-permute-done.4.refs_6_), channel_id=1, source_target_pairs={{0,2},{2,0},{1,3},{3,1},{4,6},{6,4},{5,7},{7,5},{8,10},{10,8},{9,1... | collective-permute-start | bytes 1572872 | tf_op jit(solution)/shard_map/ppermute | solution.py:196
  76.8 3.2 %collective-permute-start.9 = (bf16[4,8,16,512]{3,2,1,0:T(8,128)(2,1)}, bf16[4,8,16,512]{3,2,1,0:T(8,128)(2,1)S(1)}, u32[]{:S(2)}, u32[]{:S(2)}) collective-permute-start(bf16[4,8,16,512]{3,2,1,0:T(8,128)(2,1)} %collective-permute-done.5.refs_7_), channel_id=1, source_target_pairs={{0,2},{2,0},{1,3},{3,1},{4,6},{6,4},{5,7},{7,5},{8,10},{10,8},{9,1... | collective-permute-start | bytes 1572872 | tf_op jit(solution)/shard_map/ppermute | solution.py:196
  76.9 3.2 %collective-permute-start.10 = (bf16[4,8,16,512]{3,2,1,0:T(8,128)(2,1)S(1)}, bf16[4,8,16,512]{3,2,1,0:T(8,128)(2,1)}, u32[]{:S(2)}, u32[]{:S(2)}) collective-permute-start(bf16[4,8,16,512]{3,2,1,0:T(8,128)(2,1)S(1)} %collective-permute-done.6.refs_8_), channel_id=1, source_target_pairs={{0,2},{2,0},{1,3},{3,1},{4,6},{6,4},{5,7},{7,5},{8,10},{10,8},{9,1... | collective-permute-start | bytes 1572872 | tf_op jit(solution)/shard_map/ppermute | solution.py:196
  80.0 1.2 %copy-start.3 = (f32[512,512]{1,0:T(8,128)S(1)}, f32[512,512]{1,0:T(8,128)}, u32[]{:S(2)}) copy-start(f32[512,512]{1,0:T(8,128)} %copy-done.2) | copy-start | bytes 3145732

commit v9 on v6

--- a/solution.py
+++ b/solution.py
@@ -171,7 +171,6 @@
     packed = jnp.concatenate(
         [amplitudes.reshape(-1, 2 * rows, n_virt), hole.reshape(-1, 2 * rows, half_width)], axis=2
     )
-    packed, piece = lax.optimization_barrier((packed, piece))
     got = lax.all_to_all(packed, PAIR, split_axis=0, concat_axis=0, tiled=True)
     got = got.reshape(-1, 2, *got.shape[1:])
     near = gather_plane(piece)

time: 81.9 us -> 79.5 us (0.971)
  starting transfers between devices: 31.6 us -> 29.2 us
    all_to_all x1, starting transfers between devices: 13.4 us -> 11 us  [shards(): got = lax.all_to_all(packed, PAIR, split_axis=0, concat_axis=0, tiled=True)]
where the time goes in v9:
time: 79.5 us; the launch traced here: 79.3 us
  starting transfers between devices  29.2 us (37%)
  waiting for transfers between devices  28.2 us (35%)
  Pallas kernels  13.5 us (17%)
  local copies, waits for them, and re-layouts  4.83 us (6%)
  other arithmetic  2.91 us (4%)
    ppermute x6, waiting for transfers between devices, plane_shift(): return lax.ppermute(block, ('x', 'y', 'core'), pairs)  27 us
    pallas_call x1, Pallas kernels, particle(): pl.pallas_call(particle_kernel, in_specs=[smem, smem, anywhere, anywhere,...  13.5 us
    all_to_all x1, starting transfers between devices, shards(): got = lax.all_to_all(packed, PAIR, split_axis=0, concat_axis=0, tiled=True)  11 us
    ppermute x6, starting transfers between devices, plane_shift(): return lax.ppermute(block, ('x', 'y', 'core'), pairs)  10 us
    ppermute x1, starting transfers between devices, shards(): piece = lax.ppermute(piece, 'aux', [(0, 1), (1, 0)])  7.83 us
  transfers between devices with their start and end apart: 9, of which 6 were waited for; matrix products, arithmetic and copies ran while one was open for 9% of the time, Pallas kernels for 0%

profile of v9, /device:TPU:1, one launch (start us, length us, event | category | flops | bytes accessed | tf_op | source)
XLA Modules:
  0.0 79.3 jit_solution(13278551137271365061)
XLA Ops:
  0.0 1.0 %constant_dynamic-slice_fusion = bf16[8,16,512]{2,1,0:T(8,128)(2,1)S(1)} fusion(bf16[8,512,512]{2,1,0:T(8,128)(2,1)} %own_hbm.1, s32[]{:T(128)S(6)} %select_n.24), kind=kLoop, calls=%fused_computation.16 | loop fusion | bytes 262148 | tf_op jit(solution)/shard_map/dynamic_slice | solution.py:164
  1.0 7.8 %collective-permute-start = (bf16[8,16,512]{2,1,0:T(8,128)(2,1)S(1)}, bf16[8,16,512]{2,1,0:T(8,128)(2,1)S(1)}, u32[]{:S(2)}, u32[]{:S(2)}) collective-permute-start(bf16[8,16,512]{2,1,0:T(8,128)(2,1)S(1)} %constant_dynamic-slice_fusion), channel_id=1, source_target_pairs={{0,1},{1,0},{2,3},{3,2},{4,5},{5,4},{6,7},{7,6},{8,9},{9,8},{10,11... | collective-permute-start | bytes 393224 | tf_op jit(solution)/shard_map/ppermute | solution.py:165
  8.8 1.3 %reshape.39 = bf16[128,8,512]{2,1,0:T(8,128)(2,1)S(1)} reshape(bf16[256,4,512]{2,1,0:T(4,128)(2,1)} %param.6) | data formatting | bytes 2097152 | tf_op jit(solution)/shard_map/reshape | solution.py:172
  10.2 0.2 constant_dynamic-slice_fusion.1
  10.4 0.1 copy.11
  10.5 0.4 fusion
  10.9 0.2 copy.9
  11.1 0.3 reshape.41
  11.4 1.3 %pad_maximum_fusion.1 = bf16[128,8,768]{2,1,0:T(8,128)(2,1)} fusion(bf16[128,8,256]{2,1,0:T(8,128)(2,1)S(1)} %reshape.41, bf16[128,8,512]{2,1,0:T(8,128)(2,1)S(1)} %reshape.39), kind=kLoop, calls=%fused_computation.1 | loop fusion | flops 3145728 | bytes 3145728 | tf_op jit(solution)/shard_map/concatenate | solution.py:171
  12.7 11.0 %all-to-all-start = ((bf16[128,8,768]{2,1,0:T(8,128)(2,1)}), bf16[128,8,768]{2,1,0:T(8,128)(2,1)}, u32[]{:S(2)}, u32[]{:S(2)}) async-start(bf16[128,8,768]{2,1,0:T(8,128)(2,1)} %pad_maximum_fusion.1), calls=%async_computation | async-start | bytes 3145728 | tf_op jit(solution)/shard_map/all_to_all | solution.py:174
  23.7 2.7 %collective-permute-start.3 = (bf16[8,16,512]{2,1,0:T(8,128)(2,1)S(1)}, bf16[8,16,512]{2,1,0:T(8,128)(2,1)S(1)}, u32[]{:S(2)}, u32[]{:S(2)}) collective-permute-start(bf16[8,16,512]{2,1,0:T(8,128)(2,1)S(1)} %collective-permute-done), channel_id=1, source_target_pairs={{0,192},{2,50},{16,208},{18,2},{32,224},{34,18},{48,240},{50,34},{... | collective-permute-start | bytes 393224 | tf_op jit(solution)/shard_map/ppermute | solution.py:147
  26.4 0.5 collective-permute-start.2
  26.9 0.6 collective-permute-start.1
  27.5 7.7 %collective-permute-done.3 = bf16[8,16,512]{2,1,0:T(8,128)(2,1)S(1)} collective-permute-done((bf16[8,16,512]{2,1,0:T(8,128)(2,1)S(1)}, bf16[8,16,512]{2,1,0:T(8,128)(2,1)S(1)}, u32[]{:S(2)}, u32[]{:S(2)}) %collective-permute-start.3) | collective-permute-done | bytes 131104 | tf_op jit(solution)/shard_map/ppermute | solution.py:147
  35.2 3.2 %collective-permute-done.2 = bf16[8,16,512]{2,1,0:T(8,128)(2,1)S(1)} collective-permute-done((bf16[8,16,512]{2,1,0:T(8,128)(2,1)S(1)}, bf16[8,16,512]{2,1,0:T(8,128)(2,1)S(1)}, u32[]{:S(2)}, u32[]{:S(2)}) %collective-permute-start.2) | collective-permute-done | bytes 131104 | tf_op jit(solution)/shard_map/ppermute | solution.py:147
  38.4 2.3 %collective-permute-done.1 = bf16[8,16,512]{2,1,0:T(8,128)(2,1)S(1)} collective-permute-done((bf16[8,16,512]{2,1,0:T(8,128)(2,1)S(1)}, bf16[8,16,512]{2,1,0:T(8,128)(2,1)S(1)}, u32[]{:S(2)}, u32[]{:S(2)}) %collective-permute-start.1) | collective-permute-done | bytes 131104 | tf_op jit(solution)/shard_map/ppermute | solution.py:147
  40.7 0.1 fusion.4
  40.8 3.5 %collective-permute-start.5 = (bf16[4,8,16,512]{3,2,1,0:T(8,128)(2,1)S(1)}, bf16[4,8,16,512]{3,2,1,0:T(8,128)(2,1)S(1)}, u32[]{:S(2)}, u32[]{:S(2)}) collective-permute-start(bf16[4,8,16,512]{3,2,1,0:T(8,128)(2,1)S(1)} %get-tuple-element.6), channel_id=1, source_target_pairs={{0,32},{2,130},{16,48},{18,146},{32,0},{34,162},{48,16},{50,178},{... | collective-permute-start | bytes 1572872 | tf_op jit(solution)/shard_map/ppermute | solution.py:147
  44.3 0.0 collective-permute-start.4
  44.3 2.7 %collective-permute-start.6 = (bf16[4,8,16,512]{3,2,1,0:T(8,128)(2,1)S(1)}, bf16[4,8,16,512]{3,2,1,0:T(8,128)(2,1)S(1)}, u32[]{:S(2)}, u32[]{:S(2)}) collective-permute-start(bf16[4,8,16,512]{3,2,1,0:T(8,128)(2,1)S(1)} %get-tuple-element.6), channel_id=1, source_target_pairs={{0,48},{2,194},{16,0},{18,210},{32,16},{34,226},{48,32},{50,242},{... | collective-permute-start | bytes 1572872 | tf_op jit(solution)/shard_map/ppermute | solution.py:147
  47.0 6.2 %collective-permute-done.5 = bf16[4,8,16,512]{3,2,1,0:T(8,128)(2,1)S(1)} collective-permute-done((bf16[4,8,16,512]{3,2,1,0:T(8,128)(2,1)S(1)}, bf16[4,8,16,512]{3,2,1,0:T(8,128)(2,1)S(1)}, u32[]{:S(2)}, u32[]{:S(2)}) %collective-permute-start.5) | collective-permute-done | bytes 524320 | tf_op jit(solution)/shard_map/ppermute | solution.py:147
  53.2 7.6 %collective-permute-done.4 = bf16[4,8,16,512]{3,2,1,0:T(8,128)(2,1)S(1)} collective-permute-done((bf16[4,8,16,512]{3,2,1,0:T(8,128)(2,1)S(1)}, bf16[4,8,16,512]{3,2,1,0:T(8,128)(2,1)S(1)}, u32[]{:S(2)}, u32[]{:S(2)}) %collective-permute-start.4) | collective-permute-done | bytes 524320 | tf_op jit(solution)/shard_map/ppermute | solution.py:147
  60.8 0.0 collective-permute-done.6
  60.8 0.3 pad_maximum_fusion.near_hbm
  61.1 0.4 collective-permute-start.7
  61.5 0.8 %dynamic_slice.11 = f32[256]{0:T(256)} dynamic-slice(f32[512]{0:T(512)S(1)} %copy-done.3, s32[]{:T(128)S(6)} %select_n.23), dynamic_slice_sizes={256} | dynamic-slice | bytes 2052 | tf_op jit(solution)/shard_map/dynamic_slice | solution.py:183
  62.3 0.8 %copy.10.rows_ref = f32[512,1]{1,0:T(8,128)} copy(f32[512,1]{0,1:T(1,128)S(1)} %bitcast.31) | data formatting | bytes 4096 | tf_op jit(solution)/shard_map/broadcast_in_dim | solution.py:186
  63.1 0.6 pad_add_fusion.place_ref
  63.8 0.7 fusion.3.occ_ref
  64.4 1.2 %collective-permute-done.7.far_hbm = bf16[4,4,8,16,512]{4,3,2,1,0:T(8,128)(2,1)} collective-permute-done((bf16[4,4,8,16,512]{4,3,2,1,0:T(8,128)(2,1)S(1)}, bf16[4,4,8,16,512]{4,3,2,1,0:T(8,128)(2,1)}, u32[]{:S(2)}, u32[]{:S(2)}) %collective-permute-start.7) | collective-permute-done | bytes 2097184 | tf_op jit(solution)/shard_map/ppermute | solution.py:177
  65.6 0.0 all-to-all-done
  65.6 13.5 %particle.1 = f32[2,512,256]{2,1,0:T(8,128)} custom-call(s32[4]{0:T(128)} %pad_add_fusion.place_ref, f32[2]{0:T(128)} %fusion.3.occ_ref, bf16[64,2,8,768]{3,2,1,0:T(8,128)(2,1)} %bitcast.5.got_hbm, bf16[8,512,512]{2,1,0:T(8,128)(2,1)} %own_hbm.1, bf16[4,4,8,16,512]{4,3,2,1,0:T(8,128)(2,1)} %copy-done.2, ...), custom_call_target="tpu_custom_call" | custom-call | flops 8589934592 | bytes 8388608 | tf_op jit(solution)/shard_map/particle/pallas_call | solution.py:114
  (14 shorter events, 0.0 us)
Async XLA Ops:
  0.0 10.5 %copy-start = (bf16[256,256]{1,0:T(8,128)(2,1)S(1)}, bf16[256,256]{1,0:T(8,128)(2,1)}, u32[]{:S(2)}) copy-start(bf16[256,256]{1,0:T(8,128)(2,1)} %param.7) | copy-start | bytes 393220
  0.0 10.2 %copy-start.1 = (bf16[256,4,512]{2,1,0:T(4,128)(2,1)S(1)}, bf16[256,4,512]{2,1,0:T(4,128)(2,1)}, u32[]{:S(2)}) copy-start(bf16[256,4,512]{2,1,0:T(4,128)(2,1)} %param.6) | copy-start | bytes 3145732
  1.0 22.7 %collective-permute-start = (bf16[8,16,512]{2,1,0:T(8,128)(2,1)S(1)}, bf16[8,16,512]{2,1,0:T(8,128)(2,1)S(1)}, u32[]{:S(2)}, u32[]{:S(2)}) collective-permute-start(bf16[8,16,512]{2,1,0:T(8,128)(2,1)S(1)} %constant_dynamic-slice_fusion), channel_id=1, source_target_pairs={{0,1},{1,0},{2,3},{3,2},{4,5},{5,4},{6,7},{7,6},{8,9},{9,8},{10,11... | collective-permute-start | bytes 393224 | tf_op jit(solution)/shard_map/ppermute | solution.py:165
  12.7 52.9 %all-to-all-start = ((bf16[128,8,768]{2,1,0:T(8,128)(2,1)}), bf16[128,8,768]{2,1,0:T(8,128)(2,1)}, u32[]{:S(2)}, u32[]{:S(2)}) async-start(bf16[128,8,768]{2,1,0:T(8,128)(2,1)} %pad_maximum_fusion.1), calls=%async_computation | async-start | bytes 3145728 | tf_op jit(solution)/shard_map/all_to_all | solution.py:174
  23.7 11.5 %collective-permute-start.3 = (bf16[8,16,512]{2,1,0:T(8,128)(2,1)S(1)}, bf16[8,16,512]{2,1,0:T(8,128)(2,1)S(1)}, u32[]{:S(2)}, u32[]{:S(2)}) collective-permute-start(bf16[8,16,512]{2,1,0:T(8,128)(2,1)S(1)} %collective-permute-done), channel_id=1, source_target_pairs={{0,192},{2,50},{16,208},{18,2},{32,224},{34,18},{48,240},{50,34},{... | collective-permute-start | bytes 393224 | tf_op jit(solution)/shard_map/ppermute | solution.py:147
  26.4 12.0 %collective-permute-start.2 = (bf16[8,16,512]{2,1,0:T(8,128)(2,1)S(1)}, bf16[8,16,512]{2,1,0:T(8,128)(2,1)S(1)}, u32[]{:S(2)}, u32[]{:S(2)}) collective-permute-start(bf16[8,16,512]{2,1,0:T(8,128)(2,1)S(1)} %collective-permute-done), channel_id=1, source_target_pairs={{0,128},{2,34},{16,144},{18,50},{32,160},{34,2},{48,176},{50,18},{... | collective-permute-start | bytes 393224 | tf_op jit(solution)/shard_map/ppermute | solution.py:147
  26.9 13.8 %collective-permute-start.1 = (bf16[8,16,512]{2,1,0:T(8,128)(2,1)S(1)}, bf16[8,16,512]{2,1,0:T(8,128)(2,1)S(1)}, u32[]{:S(2)}, u32[]{:S(2)}) collective-permute-start(bf16[8,16,512]{2,1,0:T(8,128)(2,1)S(1)} %collective-permute-done), channel_id=1, source_target_pairs={{0,64},{2,18},{16,80},{18,34},{32,96},{34,50},{48,112},{50,2},{64,... | collective-permute-start | bytes 393224 | tf_op jit(solution)/shard_map/ppermute | solution.py:147
  40.8 12.3 %collective-permute-start.5 = (bf16[4,8,16,512]{3,2,1,0:T(8,128)(2,1)S(1)}, bf16[4,8,16,512]{3,2,1,0:T(8,128)(2,1)S(1)}, u32[]{:S(2)}, u32[]{:S(2)}) collective-permute-start(bf16[4,8,16,512]{3,2,1,0:T(8,128)(2,1)S(1)} %get-tuple-element.6), channel_id=1, source_target_pairs={{0,32},{2,130},{16,48},{18,146},{32,0},{34,162},{48,16},{50,178},{... | collective-permute-start | bytes 1572872 | tf_op jit(solution)/shard_map/ppermute | solution.py:147
  44.3 16.4 %collective-permute-start.4 = (bf16[4,8,16,512]{3,2,1,0:T(8,128)(2,1)S(1)}, bf16[4,8,16,512]{3,2,1,0:T(8,128)(2,1)S(1)}, u32[]{:S(2)}, u32[]{:S(2)}) collective-permute-start(bf16[4,8,16,512]{3,2,1,0:T(8,128)(2,1)S(1)} %get-tuple-element.6), channel_id=1, source_target_pairs={{0,16},{2,66},{16,32},{18,82},{32,48},{34,98},{48,0},{50,114},{64,... | collective-permute-start | bytes 1572872 | tf_op jit(solution)/shard_map/ppermute | solution.py:147
  44.3 16.4 %collective-permute-start.6 = (bf16[4,8,16,512]{3,2,1,0:T(8,128)(2,1)S(1)}, bf16[4,8,16,512]{3,2,1,0:T(8,128)(2,1)S(1)}, u32[]{:S(2)}, u32[]{:S(2)}) collective-permute-start(bf16[4,8,16,512]{3,2,1,0:T(8,128)(2,1)S(1)} %get-tuple-element.6), channel_id=1, source_target_pairs={{0,48},{2,194},{16,0},{18,210},{32,16},{34,226},{48,32},{50,242},{... | collective-permute-start | bytes 1572872 | tf_op jit(solution)/shard_map/ppermute | solution.py:147
  60.8 0.7 copy-start.3
  60.8 3.0 %copy-start.5 = (s32[2]{0:T(128)S(1)}, s32[2]{0:T(128)}, u32[]{:S(2)}) copy-start(s32[2]{0:T(128)} %param.9) | copy-start | bytes 28
  60.8 3.0 %copy-start.4 = (f32[16]{0:T(128)S(1)}, f32[16]{0:T(128)}, u32[]{:S(2)}) copy-start(f32[16]{0:T(128)} %param.10) | copy-start | bytes 196
  61.1 4.6 %copy-start.2 = (bf16[4,4,8,16,512]{4,3,2,1,0:T(8,128)(2,1)}, bf16[4,4,8,16,512]{4,3,2,1,0:T(8,128)(2,1)S(1)}, u32[]{:S(2)}) copy-start(bf16[4,4,8,16,512]{4,3,2,1,0:T(8,128)(2,1)S(1)} %pad_maximum_fusion.near_hbm) | copy-start | bytes 6291460
  61.1 4.6 %collective-permute-start.7 = (bf16[4,4,8,16,512]{4,3,2,1,0:T(8,128)(2,1)S(1)}, bf16[4,4,8,16,512]{4,3,2,1,0:T(8,128)(2,1)}, u32[]{:S(2)}, u32[]{:S(2)}) collective-permute-start(bf16[4,4,8,16,512]{4,3,2,1,0:T(8,128)(2,1)S(1)} %pad_maximum_fusion.near_hbm), channel_id=1, source_target_pairs={{0,2},{2,0},{1,3},{3,1},{4,6},{6,4},{5,7},{7,5},{8,10},{10,8},{9,1... | collective-permute-start | bytes 6291464 | tf_op jit(solution)/shard_map/ppermute | solution.py:177

commit v10 on v9

--- a/solution.py
+++ b/solution.py
@@ -42,8 +42,12 @@
     slots = other.shape[1]
     aux, core, x0, y0 = (place_ref[i] for i in range(4))
 
-    fetch = pltpu.make_async_copy(got_hbm, got_ref, sems.at[nq])
-    fetch.start()
+    fetches = [
+        pltpu.make_async_copy(got_hbm.at[:, side], got_ref.at[:, which], sems.at[index])
+        for side, which, index in ((0, core, nq), (1, 1 - core, nq + 3))
+    ]
+    for fetch in fetches:
+        fetch.start()
     own_copies = [pltpu.make_async_copy(own_hbm.at[q], own.at[q], sems.at[q]) for q in range(nq)]
     for copy in own_copies:
         copy.start()
@@ -59,7 +63,8 @@
                         other.at[pl.ds(h * part, part), (owner * SIDE + x) * SIDE + y],
                         sems.at[nq + 1 + h],
                     ).start()
-    fetch.wait()
+    for fetch in fetches:
+        fetch.wait()
 
     couples, _, both, _ = got_ref.shape
     chunk = couples // 8
@@ -124,7 +129,7 @@
             pltpu.VMEM((2, nv, nv), jnp.bfloat16),
             pltpu.VMEM((nv, nv), jnp.float32),
             pltpu.VMEM((2, nv, nv // 2), jnp.float32),
-            pltpu.SemaphoreType.DMA((nq + 3,)),
+            pltpu.SemaphoreType.DMA((nq + 4,)),
         ],
         compiler_params=pltpu.CompilerParams(vmem_limit_bytes=VMEM_LIMIT),
         cost_estimate=pl.CostEstimate(
@@ -153,26 +158,44 @@
     return block
 
 
+def windows():
+    groups = []
+    for core in range(2):
+        for first in (2 * core, 2 * core + SIDE):
+            run = sorted(((first + i) % (2 * SIDE) for i in range(SIDE)), key=lambda z8: z8 % SIDE)
+            groups.append([
+                ((cell * SIDE + z8 % SIDE) * 2 + core) * 2 + z8 // SIDE for cell in range(SIDE * SIDE) for z8 in run
+            ])
+    return groups
+
+
 def shards(amplitudes, ladder, cholesky, pair_ids, occ_energy, vir_energy):
     n_pair, rows, n_virt = amplitudes.shape
     half_width = n_virt // lax.axis_size("aux")
     aux, core = lax.axis_index("aux"), lax.axis_index("core")
-    x, y = lax.axis_index("x"), lax.axis_index("y")
+    x, y, z = lax.axis_index("x"), lax.axis_index("y"), lax.axis_index("z")
     strip = half_width // (SIDE * SIDE)
 
     slot = (core * SIDE + x) * SIDE + y
     piece = lax.dynamic_slice_in_dim(cholesky, slot * strip, strip, 1)
     piece = lax.ppermute(piece, "aux", [(0, 1), (1, 0)])
 
-    mine = lax.dynamic_slice_in_dim(amplitudes, aux * half_width, half_width, 2)
     hole = jnp.dot(
-        ladder, mine.reshape(n_pair, -1), preferred_element_type=jnp.float32
+        ladder, amplitudes.reshape(n_pair, -1), preferred_element_type=jnp.float32
     ).astype(jnp.bfloat16)
-    packed = jnp.concatenate(
-        [amplitudes.reshape(-1, 2 * rows, n_virt), hole.reshape(-1, 2 * rows, half_width)], axis=2
+    blocks = (SIDE**3, 2, 2 * rows)
+    hole = hole.reshape(SIDE * SIDE, SIDE, *blocks[1:], n_virt)
+    ring = aux * SIDE + z
+    shifted = jnp.logical_and(ring >= 2, ring < 6) == (jnp.arange(SIDE) < 2)
+    upper = jnp.stack([jnp.broadcast_to(aux == 1, (SIDE,)), shifted], axis=1)
+    hole = jnp.where(upper[None, :, :, None, None], hole[..., half_width:], hole[..., :half_width])
+    packed = jnp.concatenate([amplitudes.reshape(*blocks, n_virt), hole.reshape(*blocks, half_width)], axis=3)
+    kept = lax.dynamic_slice_in_dim(packed, core, 1, 1)
+    passed = lax.ppermute(lax.dynamic_slice_in_dim(packed, 1 - core, 1, 1), "core", [(0, 1), (1, 0)])
+    packed = jnp.concatenate([kept, passed], axis=1)
+    got = lax.all_to_all(
+        packed, AXES, split_axis=0, concat_axis=0, tiled=True, axis_index_groups=windows()
     )
-    got = lax.all_to_all(packed, PAIR, split_axis=0, concat_axis=0, tiled=True)
-    got = got.reshape(-1, 2, *got.shape[1:])
     near = gather_plane(piece)
     far = lax.ppermute(near, "core", [(0, 1), (1, 0)])
 

time: 79.5 us -> 79.9 us (level)
  starting transfers between devices: 29.2 us -> 26.3 us
  waiting for transfers between devices: 28.2 us -> 30.7 us
    ppermute x0 -> x1, starting transfers between devices: none -> 3.33 us  [shards(): lax.ppermute(lax.dynamic_slice_in_dim(packed, 1 - core, 1, 1), 'core', [(...]
    ppermute x6, waiting for transfers between devices: 27 us -> 29.7 us  [plane_shift(): return lax.ppermute(block, ('x', 'y', 'core'), pairs)]
    all_to_all x1, starting transfers between devices: 11 us -> 8.35 us  [shards(): lax.all_to_all(packed, AXES, split_axis=0, concat_axis=0, tiled=True, axi...]
    ppermute x1, starting transfers between devices: 7.83 us -> 5.26 us  [shards(): piece = lax.ppermute(piece, 'aux', [(0, 1), (1, 0)])]
    ppermute x6, starting transfers between devices: 10 us -> 8.12 us  [plane_shift(): return lax.ppermute(block, ('x', 'y', 'core'), pairs)]
    ppermute x1, starting transfers between devices: 0.4 us -> 1.3 us  [shards(): far = lax.ppermute(near, 'core', [(0, 1), (1, 0)])]
  transfers between devices with their start and end apart: 9 -> 10, of which waited for: 6 -> 5; matrix products, arithmetic and copies ran while one was open for 9% -> 7% of each run, Pallas kernels for 0% -> 0%
where the time goes in v10:
time: 79.9 us; the launch traced here: 79.6 us
  waiting for transfers between devices  30.7 us (38%)
  starting transfers between devices  26.3 us (33%)
  Pallas kernels  13.5 us (17%)
  local copies, waits for them, and re-layouts  5 us (6%)
  other arithmetic  3.37 us (4%)
    ppermute x6, waiting for transfers between devices, plane_shift(): return lax.ppermute(block, ('x', 'y', 'core'), pairs)  29.7 us
    pallas_call x1, Pallas kernels, particle(): pl.pallas_call(particle_kernel, in_specs=[smem, smem, anywhere, anywhere,...  13.5 us
    all_to_all x1, starting transfers between devices, shards(): lax.all_to_all(packed, AXES, split_axis=0, concat_axis=0, tiled=True, axi...  8.35 us
    ppermute x6, starting transfers between devices, plane_shift(): return lax.ppermute(block, ('x', 'y', 'core'), pairs)  8.12 us
    ppermute x1, starting transfers between devices, shards(): piece = lax.ppermute(piece, 'aux', [(0, 1), (1, 0)])  5.26 us
    ppermute x1, starting transfers between devices, shards(): lax.ppermute(lax.dynamic_slice_in_dim(packed, 1 - core, 1, 1), 'core', [(...  3.33 us
  transfers between devices with their start and end apart: 10, of which 5 were waited for; matrix products, arithmetic and copies ran while one was open for 7% of the time, Pallas kernels for 0%

profile of v10, /device:TPU:1, one launch (start us, length us, event | category | flops | bytes accessed | tf_op | source)
XLA Modules:
  0.0 79.6 jit_solution(11782581380575081587)
XLA Ops:
  0.0 1.4 %reshape.50 = bf16[64,2,8,512]{3,2,1,0:T(8,128)(2,1)S(1)} reshape(bf16[256,4,512]{2,1,0:T(4,128)(2,1)} %param.6) | data formatting | bytes 2097152 | tf_op jit(solution)/shard_map/reshape | solution.py:192
  1.5 0.1 copy-done.1
  1.6 0.3 copy.9
  1.9 0.4 convolution_convert_fusion
  2.3 0.7 reshape.52
  3.0 0.1 stack.54
  3.1 0.1 slice_select_fusion
  3.2 0.1 fusion.1
  3.3 3.3 %collective-permute-start = (bf16[64,1,8,768]{3,2,1,0:T(8,128)(2,1)S(1)}, bf16[64,1,8,768]{3,2,1,0:T(8,128)(2,1)S(1)}, u32[]{:S(2)}, u32[]{:S(2)}) collective-permute-start(bf16[64,1,8,768]{3,2,1,0:T(8,128)(2,1)S(1)} %get-tuple-element.6), channel_id=1, source_target_pairs={{0,2},{2,0},{1,3},{3,1},{4,6},{6,4},{5,7},{7,5},{8,10},{10,8},{9,1... | collective-permute-start | bytes 2359304 | tf_op jit(solution)/shard_map/ppermute | solution.py:194
  6.7 0.9 %constant_dynamic-slice_fusion = bf16[8,16,512]{2,1,0:T(8,128)(2,1)S(1)} fusion(bf16[8,512,512]{2,1,0:T(8,128)(2,1)} %own_hbm.1, s32[]{:T(128)S(6)} %select_n.35), kind=kLoop, calls=%fused_computation.17 | loop fusion | bytes 262148 | tf_op jit(solution)/shard_map/dynamic_slice | solution.py:180
  7.6 5.3 %collective-permute-start.1 = (bf16[8,16,512]{2,1,0:T(8,128)(2,1)S(1)}, bf16[8,16,512]{2,1,0:T(8,128)(2,1)S(1)}, u32[]{:S(2)}, u32[]{:S(2)}) collective-permute-start(bf16[8,16,512]{2,1,0:T(8,128)(2,1)S(1)} %constant_dynamic-slice_fusion), channel_id=1, source_target_pairs={{0,1},{1,0},{2,3},{3,2},{4,5},{5,4},{6,7},{7,6},{8,9},{9,8},{10,11... | collective-permute-start | bytes 393224 | tf_op jit(solution)/shard_map/ppermute | solution.py:181
  12.8 1.3 %pad_maximum_fusion.1 = bf16[64,2,8,768]{3,2,1,0:T(8,128)(2,1)} fusion(bf16[64,1,8,768]{3,2,1,0:T(8,128)(2,1)S(1)} %collective-permute-done, bf16[64,1,8,768]{3,2,1,0:T(8,128)(2,1)S(1)} %get-tuple-element.5), kind=kLoop, calls=%fused_computation.6 | loop fusion | flops 786432 | bytes 3145728 | tf_op jit(solution)/shard_map/concatenate | solution.py:195
  14.2 8.3 %all-to-all-start = ((bf16[64,2,8,768]{3,2,1,0:T(8,128)(2,1)}), bf16[64,2,8,768]{3,2,1,0:T(8,128)(2,1)}, u32[]{:S(2)}, u32[]{:S(2)}) async-start(bf16[64,2,8,768]{3,2,1,0:T(8,128)(2,1)} %pad_maximum_fusion.1), calls=%async_computation | async-start | bytes 3145728 | tf_op jit(solution)/shard_map/all_to_all | solution.py:196
  22.5 2.2 %collective-permute-start.4 = (bf16[8,16,512]{2,1,0:T(8,128)(2,1)S(1)}, bf16[8,16,512]{2,1,0:T(8,128)(2,1)S(1)}, u32[]{:S(2)}, u32[]{:S(2)}) collective-permute-start(bf16[8,16,512]{2,1,0:T(8,128)(2,1)S(1)} %collective-permute-done.1), channel_id=1, source_target_pairs={{0,192},{2,50},{16,208},{18,2},{32,224},{34,18},{48,240},{50,34},{... | collective-permute-start | bytes 393224 | tf_op jit(solution)/shard_map/ppermute | solution.py:152
  24.8 0.6 collective-permute-start.3
  25.3 0.6 collective-permute-start.2
  25.9 13.0 %collective-permute-done.4 = bf16[8,16,512]{2,1,0:T(8,128)(2,1)S(1)} collective-permute-done((bf16[8,16,512]{2,1,0:T(8,128)(2,1)S(1)}, bf16[8,16,512]{2,1,0:T(8,128)(2,1)S(1)}, u32[]{:S(2)}, u32[]{:S(2)}) %collective-permute-start.4) | collective-permute-done | bytes 131104 | tf_op jit(solution)/shard_map/ppermute | solution.py:152
  38.9 2.7 %collective-permute-done.2 = bf16[8,16,512]{2,1,0:T(8,128)(2,1)S(1)} collective-permute-done((bf16[8,16,512]{2,1,0:T(8,128)(2,1)S(1)}, bf16[8,16,512]{2,1,0:T(8,128)(2,1)S(1)}, u32[]{:S(2)}, u32[]{:S(2)}) %collective-permute-start.2) | collective-permute-done | bytes 131104 | tf_op jit(solution)/shard_map/ppermute | solution.py:152
  41.6 0.1 fusion.6
  41.7 2.0 %collective-permute-start.6 = (bf16[4,8,16,512]{3,2,1,0:T(8,128)(2,1)S(1)}, bf16[4,8,16,512]{3,2,1,0:T(8,128)(2,1)S(1)}, u32[]{:S(2)}, u32[]{:S(2)}) collective-permute-start(bf16[4,8,16,512]{3,2,1,0:T(8,128)(2,1)S(1)} %get-tuple-element.8), channel_id=1, source_target_pairs={{0,32},{2,130},{16,48},{18,146},{32,0},{34,162},{48,16},{50,178},{... | collective-permute-start | bytes 1572872 | tf_op jit(solution)/shard_map/ppermute | solution.py:152
  43.8 0.6 collective-permute-start.5
  44.4 2.1 %collective-permute-start.7 = (bf16[4,8,16,512]{3,2,1,0:T(8,128)(2,1)S(1)}, bf16[4,8,16,512]{3,2,1,0:T(8,128)(2,1)S(1)}, u32[]{:S(2)}, u32[]{:S(2)}) collective-permute-start(bf16[4,8,16,512]{3,2,1,0:T(8,128)(2,1)S(1)} %get-tuple-element.8), channel_id=1, source_target_pairs={{0,48},{2,194},{16,0},{18,210},{32,16},{34,226},{48,32},{50,242},{... | collective-permute-start | bytes 1572872 | tf_op jit(solution)/shard_map/ppermute | solution.py:152
  46.5 8.5 %collective-permute-done.6 = bf16[4,8,16,512]{3,2,1,0:T(8,128)(2,1)S(1)} collective-permute-done((bf16[4,8,16,512]{3,2,1,0:T(8,128)(2,1)S(1)}, bf16[4,8,16,512]{3,2,1,0:T(8,128)(2,1)S(1)}, u32[]{:S(2)}, u32[]{:S(2)}) %collective-permute-start.6) | collective-permute-done | bytes 524320 | tf_op jit(solution)/shard_map/ppermute | solution.py:152
  55.0 5.5 %collective-permute-done.5 = bf16[4,8,16,512]{3,2,1,0:T(8,128)(2,1)S(1)} collective-permute-done((bf16[4,8,16,512]{3,2,1,0:T(8,128)(2,1)S(1)}, bf16[4,8,16,512]{3,2,1,0:T(8,128)(2,1)S(1)}, u32[]{:S(2)}, u32[]{:S(2)}) %collective-permute-start.5) | collective-permute-done | bytes 524320 | tf_op jit(solution)/shard_map/ppermute | solution.py:152
  60.5 0.3 pad_maximum_fusion.near_hbm
  60.7 1.3 %collective-permute-start.8 = (bf16[4,4,8,16,512]{4,3,2,1,0:T(8,128)(2,1)S(1)}, bf16[4,4,8,16,512]{4,3,2,1,0:T(8,128)(2,1)}, u32[]{:S(2)}, u32[]{:S(2)}) collective-permute-start(bf16[4,4,8,16,512]{4,3,2,1,0:T(8,128)(2,1)S(1)} %pad_maximum_fusion.near_hbm), channel_id=1, source_target_pairs={{0,2},{2,0},{1,3},{3,1},{4,6},{6,4},{5,7},{7,5},{8,10},{10,8},{9,1... | collective-permute-start | bytes 6291464 | tf_op jit(solution)/shard_map/ppermute | solution.py:200
  62.0 0.6 dynamic_slice.15
  62.7 0.9 %copy.8.rows_ref = f32[512,1]{1,0:T(8,128)} copy(f32[512,1]{0,1:T(1,128)S(1)} %bitcast.30) | data formatting | bytes 4096 | tf_op jit(solution)/shard_map/broadcast_in_dim | solution.py:209
  63.5 0.7 pad_add_fusion.place_ref
  64.2 0.8 fusion.5.occ_ref
  65.0 1.0 %collective-permute-done.8.far_hbm = bf16[4,4,8,16,512]{4,3,2,1,0:T(8,128)(2,1)} collective-permute-done((bf16[4,4,8,16,512]{4,3,2,1,0:T(8,128)(2,1)S(1)}, bf16[4,4,8,16,512]{4,3,2,1,0:T(8,128)(2,1)}, u32[]{:S(2)}, u32[]{:S(2)}) %collective-permute-start.8) | collective-permute-done | bytes 2097184 | tf_op jit(solution)/shard_map/ppermute | solution.py:200
  66.0 13.5 %particle.1 = f32[2,512,256]{2,1,0:T(8,128)} custom-call(s32[4]{0:T(128)} %pad_add_fusion.place_ref, f32[2]{0:T(128)} %fusion.5.occ_ref, bf16[64,2,8,768]{3,2,1,0:T(8,128)(2,1)} %all-to-all-done.got_hbm, bf16[8,512,512]{2,1,0:T(8,128)(2,1)} %own_hbm.1, bf16[4,4,8,16,512]{4,3,2,1,0:T(8,128)(2,1)} %copy-done.2, ...), custom_call_target="tpu_custom_call" | custom-call | flops 8589934592 | bytes 8388608 | tf_op jit(solution)/shard_map/particle/pallas_call | solution.py:119
  (18 shorter events, 0.1 us)
Async XLA Ops:
  0.0 1.9 %copy-start = (bf16[256,256]{1,0:T(8,128)(2,1)S(1)}, bf16[256,256]{1,0:T(8,128)(2,1)}, u32[]{:S(2)}) copy-start(bf16[256,256]{1,0:T(8,128)(2,1)} %param.7) | copy-start | bytes 393220
  0.0 1.6 %copy-start.1 = (bf16[256,4,512]{2,1,0:T(4,128)(2,1)S(1)}, bf16[256,4,512]{2,1,0:T(4,128)(2,1)}, u32[]{:S(2)}) copy-start(bf16[256,4,512]{2,1,0:T(4,128)(2,1)} %param.6) | copy-start | bytes 3145732
  3.3 9.5 %collective-permute-start = (bf16[64,1,8,768]{3,2,1,0:T(8,128)(2,1)S(1)}, bf16[64,1,8,768]{3,2,1,0:T(8,128)(2,1)S(1)}, u32[]{:S(2)}, u32[]{:S(2)}) collective-permute-start(bf16[64,1,8,768]{3,2,1,0:T(8,128)(2,1)S(1)} %get-tuple-element.6), channel_id=1, source_target_pairs={{0,2},{2,0},{1,3},{3,1},{4,6},{6,4},{5,7},{7,5},{8,10},{10,8},{9,1... | collective-permute-start | bytes 2359304 | tf_op jit(solution)/shard_map/ppermute | solution.py:194
  7.6 14.9 %collective-permute-start.1 = (bf16[8,16,512]{2,1,0:T(8,128)(2,1)S(1)}, bf16[8,16,512]{2,1,0:T(8,128)(2,1)S(1)}, u32[]{:S(2)}, u32[]{:S(2)}) collective-permute-start(bf16[8,16,512]{2,1,0:T(8,128)(2,1)S(1)} %constant_dynamic-slice_fusion), channel_id=1, source_target_pairs={{0,1},{1,0},{2,3},{3,2},{4,5},{5,4},{6,7},{7,6},{8,9},{9,8},{10,11... | collective-permute-start | bytes 393224 | tf_op jit(solution)/shard_map/ppermute | solution.py:181
  14.2 51.8 %all-to-all-start = ((bf16[64,2,8,768]{3,2,1,0:T(8,128)(2,1)}), bf16[64,2,8,768]{3,2,1,0:T(8,128)(2,1)}, u32[]{:S(2)}, u32[]{:S(2)}) async-start(bf16[64,2,8,768]{3,2,1,0:T(8,128)(2,1)} %pad_maximum_fusion.1), calls=%async_computation | async-start | bytes 3145728 | tf_op jit(solution)/shard_map/all_to_all | solution.py:196
  22.5 16.4 %collective-permute-start.4 = (bf16[8,16,512]{2,1,0:T(8,128)(2,1)S(1)}, bf16[8,16,512]{2,1,0:T(8,128)(2,1)S(1)}, u32[]{:S(2)}, u32[]{:S(2)}) collective-permute-start(bf16[8,16,512]{2,1,0:T(8,128)(2,1)S(1)} %collective-permute-done.1), channel_id=1, source_target_pairs={{0,192},{2,50},{16,208},{18,2},{32,224},{34,18},{48,240},{50,34},{... | collective-permute-start | bytes 393224 | tf_op jit(solution)/shard_map/ppermute | solution.py:152
  24.8 14.1 %collective-permute-start.3 = (bf16[8,16,512]{2,1,0:T(8,128)(2,1)S(1)}, bf16[8,16,512]{2,1,0:T(8,128)(2,1)S(1)}, u32[]{:S(2)}, u32[]{:S(2)}) collective-permute-start(bf16[8,16,512]{2,1,0:T(8,128)(2,1)S(1)} %collective-permute-done.1), channel_id=1, source_target_pairs={{0,128},{2,34},{16,144},{18,50},{32,160},{34,2},{48,176},{50,18},{... | collective-permute-start | bytes 393224 | tf_op jit(solution)/shard_map/ppermute | solution.py:152
  25.3 16.3 %collective-permute-start.2 = (bf16[8,16,512]{2,1,0:T(8,128)(2,1)S(1)}, bf16[8,16,512]{2,1,0:T(8,128)(2,1)S(1)}, u32[]{:S(2)}, u32[]{:S(2)}) collective-permute-start(bf16[8,16,512]{2,1,0:T(8,128)(2,1)S(1)} %collective-permute-done.1), channel_id=1, source_target_pairs={{0,64},{2,18},{16,80},{18,34},{32,96},{34,50},{48,112},{50,2},{64,... | collective-permute-start | bytes 393224 | tf_op jit(solution)/shard_map/ppermute | solution.py:152
  41.7 13.2 %collective-permute-start.6 = (bf16[4,8,16,512]{3,2,1,0:T(8,128)(2,1)S(1)}, bf16[4,8,16,512]{3,2,1,0:T(8,128)(2,1)S(1)}, u32[]{:S(2)}, u32[]{:S(2)}) collective-permute-start(bf16[4,8,16,512]{3,2,1,0:T(8,128)(2,1)S(1)} %get-tuple-element.8), channel_id=1, source_target_pairs={{0,32},{2,130},{16,48},{18,146},{32,0},{34,162},{48,16},{50,178},{... | collective-permute-start | bytes 1572872 | tf_op jit(solution)/shard_map/ppermute | solution.py:152
  43.8 16.6 %collective-permute-start.5 = (bf16[4,8,16,512]{3,2,1,0:T(8,128)(2,1)S(1)}, bf16[4,8,16,512]{3,2,1,0:T(8,128)(2,1)S(1)}, u32[]{:S(2)}, u32[]{:S(2)}) collective-permute-start(bf16[4,8,16,512]{3,2,1,0:T(8,128)(2,1)S(1)} %get-tuple-element.8), channel_id=1, source_target_pairs={{0,16},{2,66},{16,32},{18,82},{32,48},{34,98},{48,0},{50,114},{64,... | collective-permute-start | bytes 1572872 | tf_op jit(solution)/shard_map/ppermute | solution.py:152
  44.4 16.0 %collective-permute-start.7 = (bf16[4,8,16,512]{3,2,1,0:T(8,128)(2,1)S(1)}, bf16[4,8,16,512]{3,2,1,0:T(8,128)(2,1)S(1)}, u32[]{:S(2)}, u32[]{:S(2)}) collective-permute-start(bf16[4,8,16,512]{3,2,1,0:T(8,128)(2,1)S(1)} %get-tuple-element.8), channel_id=1, source_target_pairs={{0,48},{2,194},{16,0},{18,210},{32,16},{34,226},{48,32},{50,242},{... | collective-permute-start | bytes 1572872 | tf_op jit(solution)/shard_map/ppermute | solution.py:152
  60.4 1.6 %copy-start.3 = (f32[512]{0:T(512)S(1)}, f32[512]{0:T(512)}, u32[]{:S(2)}) copy-start(f32[512]{0:T(512)} %param.11) | copy-start | bytes 6148
  60.4 3.7 %copy-start.5 = (s32[2]{0:T(128)S(1)}, s32[2]{0:T(128)}, u32[]{:S(2)}) copy-start(s32[2]{0:T(128)} %param.9) | copy-start | bytes 28
  60.4 3.8 %copy-start.4 = (f32[16]{0:T(128)S(1)}, f32[16]{0:T(128)}, u32[]{:S(2)}) copy-start(f32[16]{0:T(128)} %param.10) | copy-start | bytes 196
  60.7 5.2 %copy-start.2 = (bf16[4,4,8,16,512]{4,3,2,1,0:T(8,128)(2,1)}, bf16[4,4,8,16,512]{4,3,2,1,0:T(8,128)(2,1)S(1)}, u32[]{:S(2)}) copy-start(bf16[4,4,8,16,512]{4,3,2,1,0:T(8,128)(2,1)S(1)} %pad_maximum_fusion.near_hbm) | copy-start | bytes 6291460
  60.7 5.2 %collective-permute-start.8 = (bf16[4,4,8,16,512]{4,3,2,1,0:T(8,128)(2,1)S(1)}, bf16[4,4,8,16,512]{4,3,2,1,0:T(8,128)(2,1)}, u32[]{:S(2)}, u32[]{:S(2)}) collective-permute-start(bf16[4,4,8,16,512]{4,3,2,1,0:T(8,128)(2,1)S(1)} %pad_maximum_fusion.near_hbm), channel_id=1, source_target_pairs={{0,2},{2,0},{1,3},{3,1},{4,6},{6,4},{5,7},{7,5},{8,10},{10,8},{9,1... | collective-permute-start | bytes 6291464 | tf_op jit(solution)/shard_map/ppermute | solution.py:200

commit v11 on v10

--- a/solution.py
+++ b/solution.py
@@ -152,10 +152,8 @@
     return lax.ppermute(block, ("x", "y", "core"), pairs)
 
 
-def gather_plane(block):
-    for stage in range(2):
-        block = jnp.stack([block] + [plane_shift(block, d, 1 - stage) for d in (1, 2, 3)])
-    return block
+def gather_stage(block, stage):
+    return jnp.stack([block] + [plane_shift(block, d, 1 - stage) for d in range(1, SIDE)])
 
 
 def windows():
@@ -191,12 +189,14 @@
     hole = jnp.where(upper[None, :, :, None, None], hole[..., half_width:], hole[..., :half_width])
     packed = jnp.concatenate([amplitudes.reshape(*blocks, n_virt), hole.reshape(*blocks, half_width)], axis=3)
     kept = lax.dynamic_slice_in_dim(packed, core, 1, 1)
-    passed = lax.ppermute(lax.dynamic_slice_in_dim(packed, 1 - core, 1, 1), "core", [(0, 1), (1, 0)])
+    passed, piece = lax.optimization_barrier((lax.dynamic_slice_in_dim(packed, 1 - core, 1, 1), piece))
+    passed = lax.ppermute(passed, "core", [(0, 1), (1, 0)])
     packed = jnp.concatenate([kept, passed], axis=1)
+    packed, first = lax.optimization_barrier((packed, gather_stage(piece, 0)))
     got = lax.all_to_all(
         packed, AXES, split_axis=0, concat_axis=0, tiled=True, axis_index_groups=windows()
     )
-    near = gather_plane(piece)
+    near = gather_stage(first, 1)
     far = lax.ppermute(near, "core", [(0, 1), (1, 0)])
 
     orbitals = jnp.arange(NO, dtype=jnp.int32)

time: 79.9 us -> 86.6 us (1.084)
  starting transfers between devices: 26.3 us -> 30 us
  waiting for transfers between devices: 30.7 us -> 33.9 us
    all_to_all x1, starting transfers between devices: 8.35 us -> 12.2 us  [shards(): lax.all_to_all(packed, AXES, split_axis=0, concat_axis=0, tiled=True, axi...]
    ppermute x6, waiting for transfers between devices: 29.7 us -> 32.9 us  [plane_shift(): return lax.ppermute(block, ('x', 'y', 'core'), pairs)]
    ppermute x1, starting transfers between devices: 5.26 us -> 7.83 us  [shards(): piece = lax.ppermute(piece, 'aux', [(0, 1), (1, 0)])]
    ppermute x1, starting transfers between devices: 3.33 us -> 1.42 us  [shards(): passed = lax.ppermute(passed, 'core', [(0, 1), (1, 0)])]
  transfers between devices with their start and end apart: 10 -> 10, of which waited for: 5 -> 7; matrix products, arithmetic and copies ran while one was open for 7% -> 7% of each run, Pallas kernels for 0% -> 0%
where the time goes in v11:
time: 86.6 us; the launch traced here: 86.3 us
  waiting for transfers between devices  33.9 us (39%)
  starting transfers between devices  30 us (35%)
  Pallas kernels  13.5 us (16%)
  local copies, waits for them, and re-layouts  4.88 us (6%)
  other arithmetic  3.23 us (4%)
    ppermute x6, waiting for transfers between devices, plane_shift(): return lax.ppermute(block, ('x', 'y', 'core'), pairs)  32.9 us
    pallas_call x1, Pallas kernels, particle(): pl.pallas_call(particle_kernel, in_specs=[smem, smem, anywhere, anywhere,...  13.5 us
    all_to_all x1, starting transfers between devices, shards(): lax.all_to_all(packed, AXES, split_axis=0, concat_axis=0, tiled=True, axi...  12.2 us
    ppermute x1, starting transfers between devices, shards(): piece = lax.ppermute(piece, 'aux', [(0, 1), (1, 0)])  7.83 us
    ppermute x6, starting transfers between devices, plane_shift(): return lax.ppermute(block, ('x', 'y', 'core'), pairs)  7.26 us
  transfers between devices with their start and end apart: 10, of which 7 were waited for; matrix products, arithmetic and copies ran while one was open for 7% of the time, Pallas kernels for 0%

profile of v11, /device:TPU:1, one launch (start us, length us, event | category | flops | bytes accessed | tf_op | source)
XLA Modules:
  0.0 86.3 jit_solution(9049535931284847723)
XLA Ops:
  0.0 1.0 %constant_dynamic-slice_fusion = bf16[8,16,512]{2,1,0:T(8,128)(2,1)S(1)} fusion(bf16[8,512,512]{2,1,0:T(8,128)(2,1)} %own_hbm.1, s32[]{:T(128)S(6)} %select_n.35), kind=kLoop, calls=%fused_computation.17 | loop fusion | bytes 262148 | tf_op jit(solution)/shard_map/dynamic_slice | solution.py:178
  1.0 7.8 %collective-permute-start = (bf16[8,16,512]{2,1,0:T(8,128)(2,1)S(1)}, bf16[8,16,512]{2,1,0:T(8,128)(2,1)S(1)}, u32[]{:S(2)}, u32[]{:S(2)}) collective-permute-start(bf16[8,16,512]{2,1,0:T(8,128)(2,1)S(1)} %constant_dynamic-slice_fusion), channel_id=1, source_target_pairs={{0,1},{1,0},{2,3},{3,2},{4,5},{5,4},{6,7},{7,6},{8,9},{9,8},{10,11... | collective-permute-start | bytes 393224 | tf_op jit(solution)/shard_map/ppermute | solution.py:179
  8.9 1.3 %reshape.50 = bf16[64,2,8,512]{3,2,1,0:T(8,128)(2,1)S(1)} reshape(bf16[256,4,512]{2,1,0:T(4,128)(2,1)} %param.6) | data formatting | bytes 2097152 | tf_op jit(solution)/shard_map/reshape | solution.py:190
  10.2 0.3 copy.9
  10.5 0.4 convolution_convert_fusion
  10.9 0.7 reshape.52
  11.6 0.1 stack.54
  11.7 0.1 slice_select_fusion
  11.8 0.1 fusion.1
  12.0 1.4 %collective-permute-start.1 = (bf16[64,1,8,768]{3,2,1,0:T(8,128)(2,1)S(1)}, bf16[64,1,8,768]{3,2,1,0:T(8,128)(2,1)S(1)}, u32[]{:S(2)}, u32[]{:S(2)}) collective-permute-start(bf16[64,1,8,768]{3,2,1,0:T(8,128)(2,1)S(1)} %get-tuple-element.9), channel_id=1, source_target_pairs={{0,2},{2,0},{1,3},{3,1},{4,6},{6,4},{5,7},{7,5},{8,10},{10,8},{9,1... | collective-permute-start | bytes 2359304 | tf_op jit(solution)/shard_map/ppermute | solution.py:193
  13.4 2.7 %collective-permute-start.4 = (bf16[8,16,512]{2,1,0:T(8,128)(2,1)S(1)}, bf16[8,16,512]{2,1,0:T(8,128)(2,1)S(1)}, u32[]{:S(2)}, u32[]{:S(2)}) collective-permute-start(bf16[8,16,512]{2,1,0:T(8,128)(2,1)S(1)} %collective-permute-done), channel_id=1, source_target_pairs={{0,192},{2,50},{16,208},{18,2},{32,224},{34,18},{48,240},{50,34},{... | collective-permute-start | bytes 393224 | tf_op jit(solution)/shard_map/ppermute | solution.py:152
  16.1 0.3 collective-permute-start.3
  16.5 0.7 collective-permute-start.2
  17.2 2.3 %collective-permute-done.4 = bf16[8,16,512]{2,1,0:T(8,128)(2,1)S(1)} collective-permute-done((bf16[8,16,512]{2,1,0:T(8,128)(2,1)S(1)}, bf16[8,16,512]{2,1,0:T(8,128)(2,1)S(1)}, u32[]{:S(2)}, u32[]{:S(2)}) %collective-permute-start.4) | collective-permute-done | bytes 131104 | tf_op jit(solution)/shard_map/ppermute | solution.py:152
  19.5 2.3 %collective-permute-done.3 = bf16[8,16,512]{2,1,0:T(8,128)(2,1)S(1)} collective-permute-done((bf16[8,16,512]{2,1,0:T(8,128)(2,1)S(1)}, bf16[8,16,512]{2,1,0:T(8,128)(2,1)S(1)}, u32[]{:S(2)}, u32[]{:S(2)}) %collective-permute-start.3) | collective-permute-done | bytes 131104 | tf_op jit(solution)/shard_map/ppermute | solution.py:152
  21.8 1.4 %collective-permute-done.2 = bf16[8,16,512]{2,1,0:T(8,128)(2,1)S(1)} collective-permute-done((bf16[8,16,512]{2,1,0:T(8,128)(2,1)S(1)}, bf16[8,16,512]{2,1,0:T(8,128)(2,1)S(1)}, u32[]{:S(2)}, u32[]{:S(2)}) %collective-permute-start.2) | collective-permute-done | bytes 131104 | tf_op jit(solution)/shard_map/ppermute | solution.py:152
  23.2 1.3 %pad_maximum_fusion.1 = bf16[64,2,8,768]{3,2,1,0:T(8,128)(2,1)} fusion(bf16[64,1,8,768]{3,2,1,0:T(8,128)(2,1)S(1)} %collective-permute-done.1, bf16[64,1,8,768]{3,2,1,0:T(8,128)(2,1)S(1)} %get-tuple-element.13), kind=kLoop, calls=%fused_computation.6 | loop fusion | flops 786432 | bytes 3145728 | tf_op jit(solution)/shard_map/concatenate | solution.py:194
  24.5 12.2 %all-to-all-start = ((bf16[64,2,8,768]{3,2,1,0:T(8,128)(2,1)}), bf16[64,2,8,768]{3,2,1,0:T(8,128)(2,1)}, u32[]{:S(2)}, u32[]{:S(2)}) async-start(bf16[64,2,8,768]{3,2,1,0:T(8,128)(2,1)} %pad_maximum_fusion.1), calls=%async_computation | async-start | bytes 3145728 | tf_op jit(solution)/shard_map/all_to_all | solution.py:196
  36.7 2.4 %collective-permute-start.7 = (bf16[4,8,16,512]{3,2,1,0:T(8,128)(2,1)S(1)}, bf16[4,8,16,512]{3,2,1,0:T(8,128)(2,1)S(1)}, u32[]{:S(2)}, u32[]{:S(2)}) collective-permute-start(bf16[4,8,16,512]{3,2,1,0:T(8,128)(2,1)S(1)} %pad_maximum_fusion.2), channel_id=1, source_target_pairs={{0,48},{2,194},{16,0},{18,210},{32,16},{34,226},{48,32},{50,242},{... | collective-permute-start | bytes 1572872 | tf_op jit(solution)/shard_map/ppermute | solution.py:152
  39.1 0.4 collective-permute-start.6
  39.5 0.7 collective-permute-start.5
  40.2 17.0 %collective-permute-done.7 = bf16[4,8,16,512]{3,2,1,0:T(8,128)(2,1)S(1)} collective-permute-done((bf16[4,8,16,512]{3,2,1,0:T(8,128)(2,1)S(1)}, bf16[4,8,16,512]{3,2,1,0:T(8,128)(2,1)S(1)}, u32[]{:S(2)}, u32[]{:S(2)}) %collective-permute-start.7) | collective-permute-done | bytes 524320 | tf_op jit(solution)/shard_map/ppermute | solution.py:152
  57.2 0.3 collective-permute-done.6
  57.4 9.6 %collective-permute-done.5 = bf16[4,8,16,512]{3,2,1,0:T(8,128)(2,1)S(1)} collective-permute-done((bf16[4,8,16,512]{3,2,1,0:T(8,128)(2,1)S(1)}, bf16[4,8,16,512]{3,2,1,0:T(8,128)(2,1)S(1)}, u32[]{:S(2)}, u32[]{:S(2)}) %collective-permute-start.5) | collective-permute-done | bytes 524320 | tf_op jit(solution)/shard_map/ppermute | solution.py:152
  67.1 0.3 pad_maximum_fusion.near_hbm
  67.4 1.4 %collective-permute-start.8 = (bf16[4,4,8,16,512]{4,3,2,1,0:T(8,128)(2,1)S(1)}, bf16[4,4,8,16,512]{4,3,2,1,0:T(8,128)(2,1)}, u32[]{:S(2)}, u32[]{:S(2)}) collective-permute-start(bf16[4,4,8,16,512]{4,3,2,1,0:T(8,128)(2,1)S(1)} %pad_maximum_fusion.near_hbm), channel_id=1, source_target_pairs={{0,2},{2,0},{1,3},{3,1},{4,6},{6,4},{5,7},{7,5},{8,10},{10,8},{9,1... | collective-permute-start | bytes 6291464 | tf_op jit(solution)/shard_map/ppermute | solution.py:200
  68.7 0.6 dynamic_slice.15
  69.4 0.8 copy.8.rows_ref
  70.2 0.6 pad_add_fusion.place_ref
  70.8 0.8 fusion.5.occ_ref
  71.6 1.1 %collective-permute-done.8.far_hbm = bf16[4,4,8,16,512]{4,3,2,1,0:T(8,128)(2,1)} collective-permute-done((bf16[4,4,8,16,512]{4,3,2,1,0:T(8,128)(2,1)S(1)}, bf16[4,4,8,16,512]{4,3,2,1,0:T(8,128)(2,1)}, u32[]{:S(2)}, u32[]{:S(2)}) %collective-permute-start.8) | collective-permute-done | bytes 2097184 | tf_op jit(solution)/shard_map/ppermute | solution.py:200
  72.7 13.5 %particle.1 = f32[2,512,256]{2,1,0:T(8,128)} custom-call(s32[4]{0:T(128)} %pad_add_fusion.place_ref, f32[2]{0:T(128)} %fusion.5.occ_ref, bf16[64,2,8,768]{3,2,1,0:T(8,128)(2,1)} %all-to-all-done.got_hbm, bf16[8,512,512]{2,1,0:T(8,128)(2,1)} %own_hbm.1, bf16[4,4,8,16,512]{4,3,2,1,0:T(8,128)(2,1)} %copy-done.2, ...), custom_call_target="tpu_custom_call" | custom-call | flops 8589934592 | bytes 8388608 | tf_op jit(solution)/shard_map/particle/pallas_call | solution.py:119
  (18 shorter events, 0.1 us)
Async XLA Ops:
  0.0 10.5 %copy-start = (bf16[256,256]{1,0:T(8,128)(2,1)S(1)}, bf16[256,256]{1,0:T(8,128)(2,1)}, u32[]{:S(2)}) copy-start(bf16[256,256]{1,0:T(8,128)(2,1)} %param.7) | copy-start | bytes 393220
  0.0 10.2 %copy-start.1 = (bf16[256,4,512]{2,1,0:T(4,128)(2,1)S(1)}, bf16[256,4,512]{2,1,0:T(4,128)(2,1)}, u32[]{:S(2)}) copy-start(bf16[256,4,512]{2,1,0:T(4,128)(2,1)} %param.6) | copy-start | bytes 3145732
  1.0 11.0 %collective-permute-start = (bf16[8,16,512]{2,1,0:T(8,128)(2,1)S(1)}, bf16[8,16,512]{2,1,0:T(8,128)(2,1)S(1)}, u32[]{:S(2)}, u32[]{:S(2)}) collective-permute-start(bf16[8,16,512]{2,1,0:T(8,128)(2,1)S(1)} %constant_dynamic-slice_fusion), channel_id=1, source_target_pairs={{0,1},{1,0},{2,3},{3,2},{4,5},{5,4},{6,7},{7,6},{8,9},{9,8},{10,11... | collective-permute-start | bytes 393224 | tf_op jit(solution)/shard_map/ppermute | solution.py:179
  12.0 11.3 %collective-permute-start.1 = (bf16[64,1,8,768]{3,2,1,0:T(8,128)(2,1)S(1)}, bf16[64,1,8,768]{3,2,1,0:T(8,128)(2,1)S(1)}, u32[]{:S(2)}, u32[]{:S(2)}) collective-permute-start(bf16[64,1,8,768]{3,2,1,0:T(8,128)(2,1)S(1)} %get-tuple-element.9), channel_id=1, source_target_pairs={{0,2},{2,0},{1,3},{3,1},{4,6},{6,4},{5,7},{7,5},{8,10},{10,8},{9,1... | collective-permute-start | bytes 2359304 | tf_op jit(solution)/shard_map/ppermute | solution.py:193
  13.4 6.1 %collective-permute-start.4 = (bf16[8,16,512]{2,1,0:T(8,128)(2,1)S(1)}, bf16[8,16,512]{2,1,0:T(8,128)(2,1)S(1)}, u32[]{:S(2)}, u32[]{:S(2)}) collective-permute-start(bf16[8,16,512]{2,1,0:T(8,128)(2,1)S(1)} %collective-permute-done), channel_id=1, source_target_pairs={{0,192},{2,50},{16,208},{18,2},{32,224},{34,18},{48,240},{50,34},{... | collective-permute-start | bytes 393224 | tf_op jit(solution)/shard_map/ppermute | solution.py:152
  16.1 5.6 %collective-permute-start.3 = (bf16[8,16,512]{2,1,0:T(8,128)(2,1)S(1)}, bf16[8,16,512]{2,1,0:T(8,128)(2,1)S(1)}, u32[]{:S(2)}, u32[]{:S(2)}) collective-permute-start(bf16[8,16,512]{2,1,0:T(8,128)(2,1)S(1)} %collective-permute-done), channel_id=1, source_target_pairs={{0,128},{2,34},{16,144},{18,50},{32,160},{34,2},{48,176},{50,18},{... | collective-permute-start | bytes 393224 | tf_op jit(solution)/shard_map/ppermute | solution.py:152
  16.5 6.7 %collective-permute-start.2 = (bf16[8,16,512]{2,1,0:T(8,128)(2,1)S(1)}, bf16[8,16,512]{2,1,0:T(8,128)(2,1)S(1)}, u32[]{:S(2)}, u32[]{:S(2)}) collective-permute-start(bf16[8,16,512]{2,1,0:T(8,128)(2,1)S(1)} %collective-permute-done), channel_id=1, source_target_pairs={{0,64},{2,18},{16,80},{18,34},{32,96},{34,50},{48,112},{50,2},{64,... | collective-permute-start | bytes 393224 | tf_op jit(solution)/shard_map/ppermute | solution.py:152
  24.5 48.1 %all-to-all-start = ((bf16[64,2,8,768]{3,2,1,0:T(8,128)(2,1)}), bf16[64,2,8,768]{3,2,1,0:T(8,128)(2,1)}, u32[]{:S(2)}, u32[]{:S(2)}) async-start(bf16[64,2,8,768]{3,2,1,0:T(8,128)(2,1)} %pad_maximum_fusion.1), calls=%async_computation | async-start | bytes 3145728 | tf_op jit(solution)/shard_map/all_to_all | solution.py:196
  36.7 20.4 %collective-permute-start.7 = (bf16[4,8,16,512]{3,2,1,0:T(8,128)(2,1)S(1)}, bf16[4,8,16,512]{3,2,1,0:T(8,128)(2,1)S(1)}, u32[]{:S(2)}, u32[]{:S(2)}) collective-permute-start(bf16[4,8,16,512]{3,2,1,0:T(8,128)(2,1)S(1)} %pad_maximum_fusion.2), channel_id=1, source_target_pairs={{0,48},{2,194},{16,0},{18,210},{32,16},{34,226},{48,32},{50,242},{... | collective-permute-start | bytes 1572872 | tf_op jit(solution)/shard_map/ppermute | solution.py:152
  39.1 18.3 %collective-permute-start.6 = (bf16[4,8,16,512]{3,2,1,0:T(8,128)(2,1)S(1)}, bf16[4,8,16,512]{3,2,1,0:T(8,128)(2,1)S(1)}, u32[]{:S(2)}, u32[]{:S(2)}) collective-permute-start(bf16[4,8,16,512]{3,2,1,0:T(8,128)(2,1)S(1)} %pad_maximum_fusion.2), channel_id=1, source_target_pairs={{0,32},{2,130},{16,48},{18,146},{32,0},{34,162},{48,16},{50,178},{... | collective-permute-start | bytes 1572872 | tf_op jit(solution)/shard_map/ppermute | solution.py:152
  39.5 27.5 %collective-permute-start.5 = (bf16[4,8,16,512]{3,2,1,0:T(8,128)(2,1)S(1)}, bf16[4,8,16,512]{3,2,1,0:T(8,128)(2,1)S(1)}, u32[]{:S(2)}, u32[]{:S(2)}) collective-permute-start(bf16[4,8,16,512]{3,2,1,0:T(8,128)(2,1)S(1)} %pad_maximum_fusion.2), channel_id=1, source_target_pairs={{0,16},{2,66},{16,32},{18,82},{32,48},{34,98},{48,0},{50,114},{64,... | collective-permute-start | bytes 1572872 | tf_op jit(solution)/shard_map/ppermute | solution.py:152
  67.1 1.7 %copy-start.3 = (f32[512]{0:T(512)S(1)}, f32[512]{0:T(512)}, u32[]{:S(2)}) copy-start(f32[512]{0:T(512)} %param.11) | copy-start | bytes 6148
  67.1 3.7 %copy-start.5 = (s32[2]{0:T(128)S(1)}, s32[2]{0:T(128)}, u32[]{:S(2)}) copy-start(s32[2]{0:T(128)} %param.9) | copy-start | bytes 28
  67.1 3.7 %copy-start.4 = (f32[16]{0:T(128)S(1)}, f32[16]{0:T(128)}, u32[]{:S(2)}) copy-start(f32[16]{0:T(128)} %param.10) | copy-start | bytes 196
  67.3 5.3 %copy-start.2 = (bf16[4,4,8,16,512]{4,3,2,1,0:T(8,128)(2,1)}, bf16[4,4,8,16,512]{4,3,2,1,0:T(8,128)(2,1)S(1)}, u32[]{:S(2)}) copy-start(bf16[4,4,8,16,512]{4,3,2,1,0:T(8,128)(2,1)S(1)} %pad_maximum_fusion.near_hbm) | copy-start | bytes 6291460
  67.4 5.3 %collective-permute-start.8 = (bf16[4,4,8,16,512]{4,3,2,1,0:T(8,128)(2,1)S(1)}, bf16[4,4,8,16,512]{4,3,2,1,0:T(8,128)(2,1)}, u32[]{:S(2)}, u32[]{:S(2)}) collective-permute-start(bf16[4,4,8,16,512]{4,3,2,1,0:T(8,128)(2,1)S(1)} %pad_maximum_fusion.near_hbm), channel_id=1, source_target_pairs={{0,2},{2,0},{1,3},{3,1},{4,6},{6,4},{5,7},{7,5},{8,10},{10,8},{9,1... | collective-permute-start | bytes 6291464 | tf_op jit(solution)/shard_map/ppermute | solution.py:200

commit v12 on v8

--- a/solution.py
+++ b/solution.py
@@ -11,7 +11,6 @@
 SIDE = 4
 OWN_LIMIT = 48 * 1024 * 1024
 OTHER_LIMIT = 48 * 1024 * 1024
-WEIGHT = 4
 NT = (((1,), (1,)), ((), ()))
 
 
@@ -49,12 +48,17 @@
 def own_kernel(place_ref, got_hbm, own_hbm, total, amps_ref, got_ref, own, right, sems):
     nq, nv, _ = own.shape
     half = nv // 2
-    fetch = pltpu.make_async_copy(got_hbm.at[:, :, :, pl.ds(0, nv)], got_ref, sems.at[nq])
-    fetch.start()
+    fetches = [
+        pltpu.make_async_copy(got_hbm.at[:, side, :, pl.ds(0, nv)], got_ref.at[:, which], sems.at[nq + side])
+        for side, which in ((0, place_ref[1]), (1, 1 - place_ref[1]))
+    ]
+    for fetch in fetches:
+        fetch.start()
     copies = [pltpu.make_async_copy(own_hbm.at[q], own.at[q], sems.at[q]) for q in range(nq)]
     for copy in copies:
         copy.start()
-    fetch.wait()
+    for fetch in fetches:
+        fetch.wait()
     couples, _, both, _ = got_ref.shape
     chunk = couples // 8
     for i in range(8):
@@ -71,29 +75,33 @@
 
 def other_kernel(*refs):
     place_ref, occ_ref, got_hbm, base_hbm, amps_hbm = refs[:5]
-    sources, (rows_ref, cols_ref, out_hbm) = refs[5 : 5 + 2 * SIDE], refs[5 + 2 * SIDE : 8 + 2 * SIDE]
-    got_ref, amps_ref, other, right, total, out_ref, sems = refs[8 + 2 * SIDE :]
+    sources, (rows_ref, cols_ref, out_hbm) = refs[5:7], refs[7:10]
+    got_ref, amps_ref, other, right, total, out_ref, sems = refs[10:]
     nq, slots, _, nv = other.shape
     half, part = nv // 2, nq // 2
     aux, core, x0, y0 = (place_ref[i] for i in range(4))
     load = pltpu.make_async_copy(amps_hbm, amps_ref, sems.at[6])
     load.start()
     for h in range(2):
-        for owner, blocks in ((core, sources[:SIDE]), (1 - core, sources[SIDE:])):
-            for outer, src in enumerate(blocks):
+        for owner, src in ((core, sources[0]), (1 - core, sources[1])):
+            for outer in range(SIDE):
                 for inner in range(SIDE):
                     dx = inner + owner * (outer - inner)
                     dy = outer + owner * (inner - outer)
                     x, y = lax.rem(x0 + SIDE - dx, SIDE), lax.rem(y0 + SIDE - dy, SIDE)
                     pltpu.make_async_copy(
-                        src.at[inner, pl.ds(h * part, part)],
+                        src.at[outer, inner, pl.ds(h * part, part)],
                         other.at[pl.ds(h * part, part), (owner * SIDE + x) * SIDE + y],
                         sems.at[h],
                     ).start()
     fill = pltpu.make_async_copy(base_hbm, total, sems.at[2])
     fill.start()
-    fetch = pltpu.make_async_copy(got_hbm.at[:, :, :, pl.ds(nv, half)], got_ref, sems.at[3])
-    fetch.start()
+    fetches = [
+        pltpu.make_async_copy(got_hbm.at[:, side, :, pl.ds(nv, half)], got_ref.at[:, which], sems.at[index])
+        for side, which, index in ((0, core, 3), (1, 1 - core, 7))
+    ]
+    for fetch in fetches:
+        fetch.start()
 
     def ready(q):
         if q % part == 0:
@@ -107,7 +115,8 @@
         lambda q: other[q, pl.ds(aux * (slots // 2), slots // 2)].reshape(half, nv),
         amps_ref, right, total, True,
     )
-    fetch.wait()
+    for fetch in fetches:
+        fetch.wait()
     level = rows_ref[...] + cols_ref[...]
     tiles = [got_ref[:, side].astype(jnp.float32) for side in range(2)]
     stores = []
@@ -143,19 +152,19 @@
             pltpu.VMEM((*got.shape[:3], nv), jnp.bfloat16),
             pltpu.VMEM((nq, nv, nv), jnp.bfloat16),
             pltpu.VMEM((2, nv, nv), jnp.bfloat16),
-            pltpu.SemaphoreType.DMA((nq + 1,)),
+            pltpu.SemaphoreType.DMA((nq + 2,)),
         ],
         compiler_params=pltpu.CompilerParams(vmem_limit_bytes=OWN_LIMIT),
-        cost_estimate=estimate(WEIGHT * nq, nv),
+        cost_estimate=pl.CostEstimate(flops=4 * nq * nv**3 // 16, bytes_accessed=2 * nq * nv * nv // 16, transcendentals=0),
         name="own_vectors",
     )(place, got, own)
 
 
 def other_vectors(place, occ_sum, got, base, amps, near, far, rows, cols):
-    nq, strip, nv = near[0].shape[1:]
+    nq, strip, nv = near.shape[2:]
     return pl.pallas_call(
         other_kernel,
-        in_specs=[SMEM, SMEM, *[ANYWHERE] * (3 + 2 * SIDE), VMEM, VMEM],
+        in_specs=[SMEM, SMEM, *[ANYWHERE] * 5, VMEM, VMEM],
         out_specs=ANYWHERE,
         out_shape=jax.ShapeDtypeStruct((2, nv, nv // 2), jnp.float32),
         scratch_shapes=[
@@ -165,12 +174,12 @@
             pltpu.VMEM((2, nv, nv), jnp.bfloat16),
             pltpu.VMEM((nv, nv), jnp.float32),
             pltpu.VMEM((2, nv, nv // 2), jnp.float32),
-            pltpu.SemaphoreType.DMA((7,)),
+            pltpu.SemaphoreType.DMA((8,)),
         ],
         compiler_params=pltpu.CompilerParams(vmem_limit_bytes=OTHER_LIMIT),
         cost_estimate=estimate(nq, nv),
         name="other_vectors",
-    )(place, occ_sum, got, base, amps, *near, *far, rows, cols)
+    )(place, occ_sum, got, base, amps, near, far, rows, cols)
 
 
 def plane_shift(block, shift, first_core_axis):
@@ -186,39 +195,48 @@
     return lax.ppermute(block, ("x", "y", "core"), pairs)
 
 
-def gather_plane(block):
-    shifts = range(1, SIDE)
-    block = jnp.stack([block] + [plane_shift(block, d, 1) for d in shifts])
-    return [block] + [plane_shift(block, d, 0) for d in shifts]
-
-
-def other_core(block):
-    return lax.ppermute(block, "core", [(0, 1), (1, 0)])
+def gather_stage(block, stage):
+    return jnp.stack([block] + [plane_shift(block, d, 1 - stage) for d in range(1, SIDE)])
+
+
+def windows():
+    groups = []
+    for core in range(2):
+        for first in (2 * core, 2 * core + SIDE):
+            run = sorted(((first + i) % (2 * SIDE) for i in range(SIDE)), key=lambda z8: z8 % SIDE)
+            groups.append([
+                ((cell * SIDE + z8 % SIDE) * 2 + core) * 2 + z8 // SIDE for cell in range(SIDE * SIDE) for z8 in run
+            ])
+    return groups
 
 
 def shards(amplitudes, ladder, cholesky, pair_ids, occ_energy, vir_energy):
     n_pair, rows, n_virt = amplitudes.shape
     half_width = n_virt // lax.axis_size("aux")
     aux, core = lax.axis_index("aux"), lax.axis_index("core")
-    x, y = lax.axis_index("x"), lax.axis_index("y")
+    x, y, z = lax.axis_index("x"), lax.axis_index("y"), lax.axis_index("z")
     strip = half_width // (SIDE * SIDE)
 
     slot = (core * SIDE + x) * SIDE + y
     piece = lax.dynamic_slice_in_dim(cholesky, slot * strip, strip, 1)
     piece = lax.ppermute(piece, "aux", [(0, 1), (1, 0)])
 
-    mine = lax.dynamic_slice_in_dim(amplitudes, aux * half_width, half_width, 2)
     hole = jnp.dot(
-        ladder, mine.reshape(n_pair, -1), preferred_element_type=jnp.float32
+        ladder, amplitudes.reshape(n_pair, -1), preferred_element_type=jnp.float32
     ).astype(jnp.bfloat16)
-    packed = jnp.concatenate(
-        [amplitudes.reshape(-1, 2 * rows, n_virt), hole.reshape(-1, 2 * rows, half_width)], axis=2
-    )
-    packed, piece = lax.optimization_barrier((packed, piece))
-    got = lax.all_to_all(packed, PAIR, split_axis=0, concat_axis=0, tiled=True)
-    got = got.reshape(-1, 2, *got.shape[1:])
-    near = gather_plane(piece)
-
+    blocks = (SIDE**3, 2, 2 * rows)
+    hole = hole.reshape(SIDE * SIDE, SIDE, *blocks[1:], n_virt)
+    ring = aux * SIDE + z
+    shifted = jnp.logical_and(ring >= 2, ring < 6) == (jnp.arange(SIDE) < 2)
+    upper = jnp.stack([jnp.broadcast_to(aux == 1, (SIDE,)), shifted], axis=1)
+    hole = jnp.where(upper[None, :, :, None, None], hole[..., half_width:], hole[..., :half_width])
+    packed = jnp.concatenate([amplitudes.reshape(*blocks, n_virt), hole.reshape(*blocks, half_width)], axis=3)
+    kept = lax.dynamic_slice_in_dim(packed, core, 1, 1)
+    passed = lax.ppermute(lax.dynamic_slice_in_dim(packed, 1 - core, 1, 1), "core", [(0, 1), (1, 0)])
+    packed = jnp.concatenate([kept, passed], axis=1)
+    got = lax.all_to_all(
+        packed, AXES, split_axis=0, concat_axis=0, tiled=True, axis_index_groups=windows()
+    )
     orbitals = jnp.arange(NO, dtype=jnp.int32)
     first_hot = (pair_ids[:, None] // NO == orbitals[None, :]).astype(jnp.float32)
     second_hot = (pair_ids[:, None] % NO == orbitals[None, :]).astype(jnp.float32)
@@ -226,13 +244,13 @@
     vir_cols = lax.dynamic_slice_in_dim(vir_energy, aux * half_width, half_width, 0)
     place = jnp.stack([aux, core, x, y]).astype(jnp.int32)
 
+    small = (place, occ_sum, vir_energy[:, None], vir_cols[None, :])
+    first, small = lax.optimization_barrier((gather_stage(piece, 0), small))
+    near = gather_stage(first, 1)
+    far = lax.ppermute(near, "core", [(0, 1), (1, 0)])
+    place, occ_sum, rows_energy, cols_energy = small
     base, pair_amps = own_vectors(place, got, cholesky)
-    *late, base = lax.optimization_barrier((*near[1:], base))
-    near = [near[0], *late]
-    far = [other_core(block) for block in near]
-    return other_vectors(
-        place, occ_sum, got, base, pair_amps, near, far, vir_energy[:, None], vir_cols[None, :]
-    )
+    return other_vectors(place, occ_sum, got, base, pair_amps, near, far, rows_energy, cols_energy)
 
 
 def solution(mesh):

time: 89.9 us -> 85.1 us (0.947)
  waiting for transfers between devices: 35.2 us -> 31.1 us
  local copies, waits for them, and re-layouts: 7.54 us -> 3.72 us
  other arithmetic: 1.62 us -> 3.52 us
  starting transfers between devices: 29.4 us -> 30.6 us
    all_to_all x1, waiting for transfers between devices: 19.5 us -> 0.01 us  [shards(): lax.all_to_all(packed, AXES, split_axis=0, concat_axis=0, tiled=True, axi...]
    ppermute x6, waiting for transfers between devices: 13.4 us -> 27.3 us  [plane_shift(): return lax.ppermute(block, ('x', 'y', 'core'), pairs)]
    ppermute x1, waiting for transfers between devices: 0.01 us -> 3.81 us  [shards(): piece = lax.ppermute(piece, 'aux', [(0, 1), (1, 0)])]
    unnamed x17 -> x11, local copies, waits for them, and re-layouts: 3.29 us -> 0.4 us
    ppermute x1, starting transfers between devices: 7.83 us -> 5.26 us  [shards(): piece = lax.ppermute(piece, 'aux', [(0, 1), (1, 0)])]
    ppermute x4 -> x2, starting transfers between devices: 2.02 us -> 4.37 us  [the longest x1 3.33 us: shards(): lax.ppermute(lax.dynamic_slice_in_dim(packed, 1 - core, 1, 1), 'core', [(...]
    ppermute x4 -> x2, waiting for transfers between devices: 2.28 us -> 0.01 us  [the longest x1 0.01 us: shards(): far = lax.ppermute(near, 'core', [(0, 1), (1, 0)])]
    all_to_all x1, starting transfers between devices: 12 us -> 13.6 us  [shards(): lax.all_to_all(packed, AXES, split_axis=0, concat_axis=0, tiled=True, axi...]
  transfers between devices with their start and end apart: 12 -> 10, of which waited for: 6 -> 4; matrix products, arithmetic and copies ran while one was open for 6% -> 5% of each run, Pallas kernels for 8% -> 8%
where the time goes in v12:
time: 85.1 us; the launch traced here: 84.9 us
  waiting for transfers between devices  31.1 us (37%)
  starting transfers between devices  30.6 us (36%)
  Pallas kernels  15.2 us (18%)
  local copies, waits for them, and re-layouts  3.72 us (4%)
  other arithmetic  3.52 us (4%)
    ppermute x6, waiting for transfers between devices, plane_shift(): return lax.ppermute(block, ('x', 'y', 'core'), pairs)  27.3 us
    all_to_all x1, starting transfers between devices, shards(): lax.all_to_all(packed, AXES, split_axis=0, concat_axis=0, tiled=True, axi...  13.6 us
    pallas_call x1, Pallas kernels, other_vectors(): pl.pallas_call(other_kernel, in_specs=[SMEM, SMEM, *[ANYWHERE] * 5, VMEM,...  8.16 us
    ppermute x6, starting transfers between devices, plane_shift(): return lax.ppermute(block, ('x', 'y', 'core'), pairs)  7.34 us
    pallas_call x1, Pallas kernels, own_vectors(): pl.pallas_call(own_kernel, in_specs=[SMEM, ANYWHERE, ANYWHERE], out_specs...  7.05 us
    ppermute x1, starting transfers between devices, shards(): piece = lax.ppermute(piece, 'aux', [(0, 1), (1, 0)])  5.26 us
    ppermute x1, waiting for transfers between devices, shards(): piece = lax.ppermute(piece, 'aux', [(0, 1), (1, 0)])  3.81 us
    ppermute x1, starting transfers between devices, shards(): lax.ppermute(lax.dynamic_slice_in_dim(packed, 1 - core, 1, 1), 'core', [(...  3.33 us
  transfers between devices with their start and end apart: 10, of which 4 were waited for; matrix products, arithmetic and copies ran while one was open for 5% of the time, Pallas kernels for 8%

profile of v12, /device:TPU:1, one launch (start us, length us, event | category | flops | bytes accessed | tf_op | source)
XLA Modules:
  0.0 84.9 jit_solution(15899800095211527489)
XLA Ops:
  0.0 1.4 %reshape.50 = bf16[64,2,8,512]{3,2,1,0:T(8,128)(2,1)S(1)} reshape(bf16[256,4,512]{2,1,0:T(4,128)(2,1)} %param.6) | data formatting | bytes 2097152 | tf_op jit(solution)/shard_map/reshape | solution.py:233
  1.5 0.1 copy-done.1
  1.6 0.3 copy.9
  1.9 0.4 convolution_convert_fusion
  2.3 0.7 reshape.52
  3.0 0.1 stack.59
  3.1 0.1 slice_select_fusion
  3.2 0.1 fusion.1
  3.3 3.3 %collective-permute-start.4 = (bf16[64,1,8,768]{3,2,1,0:T(8,128)(2,1)S(1)}, bf16[64,1,8,768]{3,2,1,0:T(8,128)(2,1)S(1)}, u32[]{:S(2)}, u32[]{:S(2)}) collective-permute-start(bf16[64,1,8,768]{3,2,1,0:T(8,128)(2,1)S(1)} %get-tuple-element.20), channel_id=1, source_target_pairs={{0,2},{2,0},{1,3},{3,1},{4,6},{6,4},{5,7},{7,5},{8,10},{10,8},{9,1... | collective-permute-start | bytes 2359304 | tf_op jit(solution)/shard_map/ppermute | solution.py:235
  6.7 0.9 %constant_dynamic-slice_fusion = bf16[8,16,512]{2,1,0:T(8,128)(2,1)S(1)} fusion(bf16[8,512,512]{2,1,0:T(8,128)(2,1)} %own_hbm.1, s32[]{:T(128)S(6)} %select_n.30), kind=kLoop, calls=%fused_computation.17 | loop fusion | bytes 262148 | tf_op jit(solution)/shard_map/dynamic_slice | solution.py:221
  7.6 5.3 %collective-permute-start = (bf16[8,16,512]{2,1,0:T(8,128)(2,1)S(1)}, bf16[8,16,512]{2,1,0:T(8,128)(2,1)S(1)}, u32[]{:S(2)}, u32[]{:S(2)}) collective-permute-start(bf16[8,16,512]{2,1,0:T(8,128)(2,1)S(1)} %constant_dynamic-slice_fusion), channel_id=1, source_target_pairs={{0,1},{1,0},{2,3},{3,2},{4,5},{5,4},{6,7},{7,6},{8,9},{9,8},{10,11... | collective-permute-start | bytes 393224 | tf_op jit(solution)/shard_map/ppermute | solution.py:222
  12.9 3.8 %collective-permute-done = bf16[8,16,512]{2,1,0:T(8,128)(2,1)S(1)} collective-permute-done((bf16[8,16,512]{2,1,0:T(8,128)(2,1)S(1)}, bf16[8,16,512]{2,1,0:T(8,128)(2,1)S(1)}, u32[]{:S(2)}, u32[]{:S(2)}) %collective-permute-start) | collective-permute-done | bytes 131104 | tf_op jit(solution)/shard_map/ppermute | solution.py:222
  16.7 2.7 %collective-permute-start.3 = (bf16[8,16,512]{2,1,0:T(8,128)(2,1)S(1)}, bf16[8,16,512]{2,1,0:T(8,128)(2,1)S(1)}, u32[]{:S(2)}, u32[]{:S(2)}) collective-permute-start(bf16[8,16,512]{2,1,0:T(8,128)(2,1)S(1)} %collective-permute-done), channel_id=1, source_target_pairs={{0,192},{2,50},{16,208},{18,2},{32,224},{34,18},{48,240},{50,34},{... | collective-permute-start | bytes 393224 | tf_op jit(solution)/shard_map/ppermute | solution.py:195
  19.4 0.3 collective-permute-start.2
  19.8 0.7 collective-permute-start.1
  20.5 1.3 %pad_maximum_fusion.1 = bf16[64,2,8,768]{3,2,1,0:T(8,128)(2,1)} fusion(bf16[64,1,8,768]{3,2,1,0:T(8,128)(2,1)S(1)} %collective-permute-done.4, bf16[64,1,8,768]{3,2,1,0:T(8,128)(2,1)S(1)} %get-tuple-element.19), kind=kLoop, calls=%fused_computation.6 | loop fusion | flops 786432 | bytes 3145728 | tf_op jit(solution)/shard_map/concatenate | solution.py:236
  21.8 13.6 %all-to-all-start = ((bf16[64,2,8,768]{3,2,1,0:T(8,128)(2,1)}), bf16[64,2,8,768]{3,2,1,0:T(8,128)(2,1)S(1)}, u32[]{:S(2)}, u32[]{:S(2)}) async-start(bf16[64,2,8,768]{3,2,1,0:T(8,128)(2,1)} %pad_maximum_fusion.1), calls=%async_computation | async-start | bytes 3145728 | tf_op jit(solution)/shard_map/all_to_all | solution.py:237
  35.4 0.1 pad_add_fusion.place_ref.refs_0_
  35.5 0.1 dynamic_slice.13
  35.5 0.2 fusion.5.refs_1_
  35.8 0.1 pad_maximum_fusion.2
  35.8 2.5 %collective-permute-start.7 = (bf16[4,8,16,512]{3,2,1,0:T(8,128)(2,1)S(1)}, bf16[4,8,16,512]{3,2,1,0:T(8,128)(2,1)S(1)}, u32[]{:S(2)}, u32[]{:S(2)}) collective-permute-start(bf16[4,8,16,512]{3,2,1,0:T(8,128)(2,1)S(1)} %pad_maximum_fusion.2), channel_id=1, source_target_pairs={{0,48},{2,194},{16,0},{18,210},{32,16},{34,226},{48,32},{50,242},{... | collective-permute-start | bytes 1572872 | tf_op jit(solution)/shard_map/ppermute | solution.py:195
  38.3 0.4 collective-permute-start.6
  38.7 0.7 collective-permute-start.5
  39.4 17.4 %collective-permute-done.7 = bf16[4,8,16,512]{3,2,1,0:T(8,128)(2,1)S(1)} collective-permute-done((bf16[4,8,16,512]{3,2,1,0:T(8,128)(2,1)S(1)}, bf16[4,8,16,512]{3,2,1,0:T(8,128)(2,1)S(1)}, u32[]{:S(2)}, u32[]{:S(2)}) %collective-permute-start.7) | collective-permute-done | bytes 524320 | tf_op jit(solution)/shard_map/ppermute | solution.py:195
  56.8 0.3 collective-permute-done.6
  57.0 9.6 %collective-permute-done.5 = bf16[4,8,16,512]{3,2,1,0:T(8,128)(2,1)S(1)} collective-permute-done((bf16[4,8,16,512]{3,2,1,0:T(8,128)(2,1)S(1)}, bf16[4,8,16,512]{3,2,1,0:T(8,128)(2,1)S(1)}, u32[]{:S(2)}, u32[]{:S(2)}) %collective-permute-start.5) | collective-permute-done | bytes 524320 | tf_op jit(solution)/shard_map/ppermute | solution.py:195
  66.7 1.6 %pad_maximum_fusion.refs_5_ = bf16[4,4,8,16,512]{4,3,2,1,0:T(8,128)(2,1)} fusion(bf16[1,4,8,16,512]{4,3,2,1,0:T(8,128)(2,1)S(1)} %bitcast.24, bf16[1,4,8,16,512]{4,3,2,1,0:T(8,128)(2,1)S(1)} %bitcast.25, bf16[1,4,8,16,512]{4,3,2,1,0:T(8,128)(2,1)S(1)} %bitcast.26, bf16[1,4,8,16,512]{4,3,2,1,0:T(8,128)(2,1)S(1)} %bitcast.23), kind=kLoop, calls=%fused_computation.1 | loop fusion | flops 3145728 | bytes 4194304 | tf_op jit(solution)/shard_map/stack | solution.py:199
  68.3 1.0 %collective-permute-start.8 = (bf16[4,4,8,16,512]{4,3,2,1,0:T(8,128)(2,1)}, bf16[4,4,8,16,512]{4,3,2,1,0:T(8,128)(2,1)}, u32[]{:S(2)}, u32[]{:S(2)}) collective-permute-start(bf16[4,4,8,16,512]{4,3,2,1,0:T(8,128)(2,1)} %pad_maximum_fusion.refs_5_), channel_id=1, source_target_pairs={{0,2},{2,0},{1,3},{3,1},{4,6},{6,4},{5,7},{7,5},{8,10},{10,8},{9,1... | collective-permute-start | bytes 6291464 | tf_op jit(solution)/shard_map/ppermute | solution.py:250
  69.3 0.1 copy.8.refs_7_
  69.5 7.0 %own_vectors.1 = (f32[512,512]{1,0:T(8,128)S(1)}, bf16[1024,512]{1,0:T(8,128)(2,1)S(1)}) custom-call(s32[4]{0:T(128)S(1)} %pad_add_fusion.place_ref.refs_0_, bf16[64,2,8,768]{3,2,1,0:T(8,128)(2,1)S(1)} %all-to-all-done.got_hbm.refs_2_, bf16[8,512,512]{2,1,0:T(8,128)(2,1)} %own_hbm.1), custom_call_target="tpu_custom_call" | custom-call | flops 268435456 | bytes 262144 | tf_op jit(solution)/shard_map/own_vectors/pallas_call | solution.py:143
  76.5 8.2 %other_vectors.1 = f32[2,512,256]{2,1,0:T(8,128)} custom-call(s32[4]{0:T(128)S(1)} %pad_add_fusion.place_ref.refs_0_, f32[2]{0:T(128)S(1)} %fusion.5.refs_1_, bf16[64,2,8,768]{3,2,1,0:T(8,128)(2,1)S(1)} %all-to-all-done.got_hbm.refs_2_, f32[512,512]{1,0:T(8,128)S(1)} %get-tuple-element.14.refs_3_, bf16[1024,512]{1,0:T(8,128)(2,1)S(1)} %get-tuple-element.15.refs_4_, ...), custom_call_target="tpu_custom_call" | custom-call | flops 4294967296 | bytes 4194304 | tf_op jit(solution)/shard_map/other_vectors/pallas_call | solution.py:165
  (17 shorter events, 0.1 us)
Async XLA Ops:
  0.0 1.9 %copy-start = (bf16[256,256]{1,0:T(8,128)(2,1)S(1)}, bf16[256,256]{1,0:T(8,128)(2,1)}, u32[]{:S(2)}) copy-start(bf16[256,256]{1,0:T(8,128)(2,1)} %param.7) | copy-start | bytes 393220
  0.0 1.6 %copy-start.1 = (bf16[256,4,512]{2,1,0:T(4,128)(2,1)S(1)}, bf16[256,4,512]{2,1,0:T(4,128)(2,1)}, u32[]{:S(2)}) copy-start(bf16[256,4,512]{2,1,0:T(4,128)(2,1)} %param.6) | copy-start | bytes 3145732
  3.2 9.7 %copy-start.4 = (s32[2]{0:T(128)S(1)}, s32[2]{0:T(128)}, u32[]{:S(2)}) copy-start(s32[2]{0:T(128)} %param.9) | copy-start | bytes 28
  3.3 17.1 %collective-permute-start.4 = (bf16[64,1,8,768]{3,2,1,0:T(8,128)(2,1)S(1)}, bf16[64,1,8,768]{3,2,1,0:T(8,128)(2,1)S(1)}, u32[]{:S(2)}, u32[]{:S(2)}) collective-permute-start(bf16[64,1,8,768]{3,2,1,0:T(8,128)(2,1)S(1)} %get-tuple-element.20), channel_id=1, source_target_pairs={{0,2},{2,0},{1,3},{3,1},{4,6},{6,4},{5,7},{7,5},{8,10},{10,8},{9,1... | collective-permute-start | bytes 2359304 | tf_op jit(solution)/shard_map/ppermute | solution.py:235
  7.6 9.1 %collective-permute-start = (bf16[8,16,512]{2,1,0:T(8,128)(2,1)S(1)}, bf16[8,16,512]{2,1,0:T(8,128)(2,1)S(1)}, u32[]{:S(2)}, u32[]{:S(2)}) collective-permute-start(bf16[8,16,512]{2,1,0:T(8,128)(2,1)S(1)} %constant_dynamic-slice_fusion), channel_id=1, source_target_pairs={{0,1},{1,0},{2,3},{3,2},{4,5},{5,4},{6,7},{7,6},{8,9},{9,8},{10,11... | collective-permute-start | bytes 393224 | tf_op jit(solution)/shard_map/ppermute | solution.py:222
  16.7 19.1 %collective-permute-start.3 = (bf16[8,16,512]{2,1,0:T(8,128)(2,1)S(1)}, bf16[8,16,512]{2,1,0:T(8,128)(2,1)S(1)}, u32[]{:S(2)}, u32[]{:S(2)}) collective-permute-start(bf16[8,16,512]{2,1,0:T(8,128)(2,1)S(1)} %collective-permute-done), channel_id=1, source_target_pairs={{0,192},{2,50},{16,208},{18,2},{32,224},{34,18},{48,240},{50,34},{... | collective-permute-start | bytes 393224 | tf_op jit(solution)/shard_map/ppermute | solution.py:195
  19.4 16.3 %collective-permute-start.2 = (bf16[8,16,512]{2,1,0:T(8,128)(2,1)S(1)}, bf16[8,16,512]{2,1,0:T(8,128)(2,1)S(1)}, u32[]{:S(2)}, u32[]{:S(2)}) collective-permute-start(bf16[8,16,512]{2,1,0:T(8,128)(2,1)S(1)} %collective-permute-done), channel_id=1, source_target_pairs={{0,128},{2,34},{16,144},{18,50},{32,160},{34,2},{48,176},{50,18},{... | collective-permute-start | bytes 393224 | tf_op jit(solution)/shard_map/ppermute | solution.py:195
  19.8 16.0 %collective-permute-start.1 = (bf16[8,16,512]{2,1,0:T(8,128)(2,1)S(1)}, bf16[8,16,512]{2,1,0:T(8,128)(2,1)S(1)}, u32[]{:S(2)}, u32[]{:S(2)}) collective-permute-start(bf16[8,16,512]{2,1,0:T(8,128)(2,1)S(1)} %collective-permute-done), channel_id=1, source_target_pairs={{0,64},{2,18},{16,80},{18,34},{32,96},{34,50},{48,112},{50,2},{64,... | collective-permute-start | bytes 393224 | tf_op jit(solution)/shard_map/ppermute | solution.py:195
  21.8 13.7 %copy-start.2 = (f32[512]{0:T(512)S(1)}, f32[512]{0:T(512)}, u32[]{:S(2)}) copy-start(f32[512]{0:T(512)} %param.11) | copy-start | bytes 6148
  21.8 13.8 %copy-start.3 = (f32[16]{0:T(128)S(1)}, f32[16]{0:T(128)}, u32[]{:S(2)}) copy-start(f32[16]{0:T(128)} %param.10) | copy-start | bytes 196
  21.8 47.7 %all-to-all-start = ((bf16[64,2,8,768]{3,2,1,0:T(8,128)(2,1)}), bf16[64,2,8,768]{3,2,1,0:T(8,128)(2,1)S(1)}, u32[]{:S(2)}, u32[]{:S(2)}) async-start(bf16[64,2,8,768]{3,2,1,0:T(8,128)(2,1)} %pad_maximum_fusion.1), calls=%async_computation | async-start | bytes 3145728 | tf_op jit(solution)/shard_map/all_to_all | solution.py:237
  35.8 20.9 %collective-permute-start.7 = (bf16[4,8,16,512]{3,2,1,0:T(8,128)(2,1)S(1)}, bf16[4,8,16,512]{3,2,1,0:T(8,128)(2,1)S(1)}, u32[]{:S(2)}, u32[]{:S(2)}) collective-permute-start(bf16[4,8,16,512]{3,2,1,0:T(8,128)(2,1)S(1)} %pad_maximum_fusion.2), channel_id=1, source_target_pairs={{0,48},{2,194},{16,0},{18,210},{32,16},{34,226},{48,32},{50,242},{... | collective-permute-start | bytes 1572872 | tf_op jit(solution)/shard_map/ppermute | solution.py:195
  38.3 18.7 %collective-permute-start.6 = (bf16[4,8,16,512]{3,2,1,0:T(8,128)(2,1)S(1)}, bf16[4,8,16,512]{3,2,1,0:T(8,128)(2,1)S(1)}, u32[]{:S(2)}, u32[]{:S(2)}) collective-permute-start(bf16[4,8,16,512]{3,2,1,0:T(8,128)(2,1)S(1)} %pad_maximum_fusion.2), channel_id=1, source_target_pairs={{0,32},{2,130},{16,48},{18,146},{32,0},{34,162},{48,16},{50,178},{... | collective-permute-start | bytes 1572872 | tf_op jit(solution)/shard_map/ppermute | solution.py:195
  38.7 28.0 %collective-permute-start.5 = (bf16[4,8,16,512]{3,2,1,0:T(8,128)(2,1)S(1)}, bf16[4,8,16,512]{3,2,1,0:T(8,128)(2,1)S(1)}, u32[]{:S(2)}, u32[]{:S(2)}) collective-permute-start(bf16[4,8,16,512]{3,2,1,0:T(8,128)(2,1)S(1)} %pad_maximum_fusion.2), channel_id=1, source_target_pairs={{0,16},{2,66},{16,32},{18,82},{32,48},{34,98},{48,0},{50,114},{64,... | collective-permute-start | bytes 1572872 | tf_op jit(solution)/shard_map/ppermute | solution.py:195
  68.3 8.3 %collective-permute-start.8 = (bf16[4,4,8,16,512]{4,3,2,1,0:T(8,128)(2,1)}, bf16[4,4,8,16,512]{4,3,2,1,0:T(8,128)(2,1)}, u32[]{:S(2)}, u32[]{:S(2)}) collective-permute-start(bf16[4,4,8,16,512]{4,3,2,1,0:T(8,128)(2,1)} %pad_maximum_fusion.refs_5_), channel_id=1, source_target_pairs={{0,2},{2,0},{1,3},{3,1},{4,6},{6,4},{5,7},{7,5},{8,10},{10,8},{9,1... | collective-permute-start | bytes 6291464 | tf_op jit(solution)/shard_map/ppermute | solution.py:250

commit v13 on v9

--- a/solution.py
+++ b/solution.py
@@ -9,7 +9,7 @@
 AXES = ("x", "y", "z", "core", "aux")
 PAIR = AXES[:4]
 SIDE = 4
-VMEM_LIMIT = 56 * 1024 * 1024
+VMEM_LIMIT = 48 * 1024 * 1024
 NT = (((1,), (1,)), ((), ()))
 
 

time: 79.5 us -> 79.1 us (level)
  waiting for transfers between devices: 28.2 us -> 30.6 us
  local copies, waits for them, and re-layouts: 4.83 us -> 3.39 us
  other arithmetic: 2.91 us -> 1.89 us
    ppermute x1, waiting for transfers between devices: 1.2 us -> 3.64 us  [shards(): far = lax.ppermute(near, 'core', [(0, 1), (1, 0)])]
  transfers between devices with their start and end apart: 9 -> 9, of which waited for: 6 -> 6; matrix products, arithmetic and copies ran while one was open for 9% -> 6% of each run, Pallas kernels for 0% -> 0%
where the time goes in v13:
time: 79.1 us; the launch traced here: 78.9 us
  waiting for transfers between devices  30.6 us (39%)
  starting transfers between devices  29.2 us (37%)
  Pallas kernels  13.1 us (17%)
  local copies, waits for them, and re-layouts  3.39 us (4%)
  other arithmetic  1.89 us (2%)
    ppermute x6, waiting for transfers between devices, plane_shift(): return lax.ppermute(block, ('x', 'y', 'core'), pairs)  27 us
    pallas_call x1, Pallas kernels, particle(): pl.pallas_call(particle_kernel, in_specs=[smem, smem, anywhere, anywhere,...  13.1 us
    all_to_all x1, starting transfers between devices, shards(): got = lax.all_to_all(packed, PAIR, split_axis=0, concat_axis=0, tiled=True)  11 us
    ppermute x6, starting transfers between devices, plane_shift(): return lax.ppermute(block, ('x', 'y', 'core'), pairs)  10 us
    ppermute x1, starting transfers between devices, shards(): piece = lax.ppermute(piece, 'aux', [(0, 1), (1, 0)])  7.83 us
    ppermute x1, waiting for transfers between devices, shards(): far = lax.ppermute(near, 'core', [(0, 1), (1, 0)])  3.64 us
  transfers between devices with their start and end apart: 9, of which 6 were waited for; matrix products, arithmetic and copies ran while one was open for 6% of the time, Pallas kernels for 0%

profile of v13, /device:TPU:1, one launch (start us, length us, event | category | flops | bytes accessed | tf_op | source)
XLA Modules:
  0.0 78.9 jit_solution(18261755059488629338)
XLA Ops:
  0.0 1.0 %constant_dynamic-slice_fusion = bf16[8,16,512]{2,1,0:T(8,128)(2,1)S(1)} fusion(bf16[8,512,512]{2,1,0:T(8,128)(2,1)} %own_hbm.1, s32[]{:T(128)S(6)} %select_n.24), kind=kLoop, calls=%fused_computation.16 | loop fusion | bytes 262148 | tf_op jit(solution)/shard_map/dynamic_slice | solution.py:164
  1.0 7.8 %collective-permute-start = (bf16[8,16,512]{2,1,0:T(8,128)(2,1)S(1)}, bf16[8,16,512]{2,1,0:T(8,128)(2,1)S(1)}, u32[]{:S(2)}, u32[]{:S(2)}) collective-permute-start(bf16[8,16,512]{2,1,0:T(8,128)(2,1)S(1)} %constant_dynamic-slice_fusion), channel_id=1, source_target_pairs={{0,1},{1,0},{2,3},{3,2},{4,5},{5,4},{6,7},{7,6},{8,9},{9,8},{10,11... | collective-permute-start | bytes 393224 | tf_op jit(solution)/shard_map/ppermute | solution.py:165
  8.8 1.3 %reshape.39 = bf16[128,8,512]{2,1,0:T(8,128)(2,1)S(1)} reshape(bf16[256,4,512]{2,1,0:T(4,128)(2,1)} %param.6) | data formatting | bytes 2097152 | tf_op jit(solution)/shard_map/reshape | solution.py:172
  10.2 0.2 constant_dynamic-slice_fusion.1
  10.4 0.1 copy.11
  10.5 0.4 fusion
  10.9 0.2 copy.9
  11.1 0.3 reshape.41
  11.4 1.3 %pad_maximum_fusion.1 = bf16[128,8,768]{2,1,0:T(8,128)(2,1)} fusion(bf16[128,8,256]{2,1,0:T(8,128)(2,1)S(1)} %reshape.41, bf16[128,8,512]{2,1,0:T(8,128)(2,1)S(1)} %reshape.39), kind=kLoop, calls=%fused_computation.1 | loop fusion | flops 3145728 | bytes 3145728 | tf_op jit(solution)/shard_map/concatenate | solution.py:171
  12.7 11.0 %all-to-all-start = ((bf16[128,8,768]{2,1,0:T(8,128)(2,1)}), bf16[128,8,768]{2,1,0:T(8,128)(2,1)}, u32[]{:S(2)}, u32[]{:S(2)}) async-start(bf16[128,8,768]{2,1,0:T(8,128)(2,1)} %pad_maximum_fusion.1), calls=%async_computation | async-start | bytes 3145728 | tf_op jit(solution)/shard_map/all_to_all | solution.py:174
  23.7 2.7 %collective-permute-start.3 = (bf16[8,16,512]{2,1,0:T(8,128)(2,1)S(1)}, bf16[8,16,512]{2,1,0:T(8,128)(2,1)S(1)}, u32[]{:S(2)}, u32[]{:S(2)}) collective-permute-start(bf16[8,16,512]{2,1,0:T(8,128)(2,1)S(1)} %collective-permute-done), channel_id=1, source_target_pairs={{0,192},{2,50},{16,208},{18,2},{32,224},{34,18},{48,240},{50,34},{... | collective-permute-start | bytes 393224 | tf_op jit(solution)/shard_map/ppermute | solution.py:147
  26.4 0.5 collective-permute-start.2
  26.9 0.6 collective-permute-start.1
  27.5 7.7 %collective-permute-done.3 = bf16[8,16,512]{2,1,0:T(8,128)(2,1)S(1)} collective-permute-done((bf16[8,16,512]{2,1,0:T(8,128)(2,1)S(1)}, bf16[8,16,512]{2,1,0:T(8,128)(2,1)S(1)}, u32[]{:S(2)}, u32[]{:S(2)}) %collective-permute-start.3) | collective-permute-done | bytes 131104 | tf_op jit(solution)/shard_map/ppermute | solution.py:147
  35.2 3.2 %collective-permute-done.2 = bf16[8,16,512]{2,1,0:T(8,128)(2,1)S(1)} collective-permute-done((bf16[8,16,512]{2,1,0:T(8,128)(2,1)S(1)}, bf16[8,16,512]{2,1,0:T(8,128)(2,1)S(1)}, u32[]{:S(2)}, u32[]{:S(2)}) %collective-permute-start.2) | collective-permute-done | bytes 131104 | tf_op jit(solution)/shard_map/ppermute | solution.py:147
  38.4 2.3 %collective-permute-done.1 = bf16[8,16,512]{2,1,0:T(8,128)(2,1)S(1)} collective-permute-done((bf16[8,16,512]{2,1,0:T(8,128)(2,1)S(1)}, bf16[8,16,512]{2,1,0:T(8,128)(2,1)S(1)}, u32[]{:S(2)}, u32[]{:S(2)}) %collective-permute-start.1) | collective-permute-done | bytes 131104 | tf_op jit(solution)/shard_map/ppermute | solution.py:147
  40.7 0.1 fusion.4
  40.8 3.5 %collective-permute-start.5 = (bf16[4,8,16,512]{3,2,1,0:T(8,128)(2,1)S(1)}, bf16[4,8,16,512]{3,2,1,0:T(8,128)(2,1)S(1)}, u32[]{:S(2)}, u32[]{:S(2)}) collective-permute-start(bf16[4,8,16,512]{3,2,1,0:T(8,128)(2,1)S(1)} %get-tuple-element.6), channel_id=1, source_target_pairs={{0,32},{2,130},{16,48},{18,146},{32,0},{34,162},{48,16},{50,178},{... | collective-permute-start | bytes 1572872 | tf_op jit(solution)/shard_map/ppermute | solution.py:147
  44.3 0.0 collective-permute-start.4
  44.3 2.7 %collective-permute-start.6 = (bf16[4,8,16,512]{3,2,1,0:T(8,128)(2,1)S(1)}, bf16[4,8,16,512]{3,2,1,0:T(8,128)(2,1)S(1)}, u32[]{:S(2)}, u32[]{:S(2)}) collective-permute-start(bf16[4,8,16,512]{3,2,1,0:T(8,128)(2,1)S(1)} %get-tuple-element.6), channel_id=1, source_target_pairs={{0,48},{2,194},{16,0},{18,210},{32,16},{34,226},{48,32},{50,242},{... | collective-permute-start | bytes 1572872 | tf_op jit(solution)/shard_map/ppermute | solution.py:147
  47.0 6.2 %collective-permute-done.5 = bf16[4,8,16,512]{3,2,1,0:T(8,128)(2,1)S(1)} collective-permute-done((bf16[4,8,16,512]{3,2,1,0:T(8,128)(2,1)S(1)}, bf16[4,8,16,512]{3,2,1,0:T(8,128)(2,1)S(1)}, u32[]{:S(2)}, u32[]{:S(2)}) %collective-permute-start.5) | collective-permute-done | bytes 524320 | tf_op jit(solution)/shard_map/ppermute | solution.py:147
  53.2 7.6 %collective-permute-done.4 = bf16[4,8,16,512]{3,2,1,0:T(8,128)(2,1)S(1)} collective-permute-done((bf16[4,8,16,512]{3,2,1,0:T(8,128)(2,1)S(1)}, bf16[4,8,16,512]{3,2,1,0:T(8,128)(2,1)S(1)}, u32[]{:S(2)}, u32[]{:S(2)}) %collective-permute-start.4) | collective-permute-done | bytes 524320 | tf_op jit(solution)/shard_map/ppermute | solution.py:147
  60.8 0.0 collective-permute-done.6
  60.8 0.3 pad_maximum_fusion.near_hbm
  61.0 0.4 collective-permute-start.7
  61.4 0.1 dynamic_slice.11
  61.5 0.1 copy.10.rows_ref
  61.7 0.1 pad_add_fusion.place_ref
  61.8 0.2 fusion.3.occ_ref
  62.0 3.6 %collective-permute-done.7.far_hbm = bf16[4,4,8,16,512]{4,3,2,1,0:T(8,128)(2,1)} collective-permute-done((bf16[4,4,8,16,512]{4,3,2,1,0:T(8,128)(2,1)S(1)}, bf16[4,4,8,16,512]{4,3,2,1,0:T(8,128)(2,1)}, u32[]{:S(2)}, u32[]{:S(2)}) %collective-permute-start.7) | collective-permute-done | bytes 2097184 | tf_op jit(solution)/shard_map/ppermute | solution.py:177
  65.6 0.0 all-to-all-done
  65.6 13.1 %particle.1 = f32[2,512,256]{2,1,0:T(8,128)} custom-call(s32[4]{0:T(128)S(1)} %pad_add_fusion.place_ref, f32[2]{0:T(128)S(1)} %fusion.3.occ_ref, bf16[64,2,8,768]{3,2,1,0:T(8,128)(2,1)} %bitcast.5.got_hbm, bf16[8,512,512]{2,1,0:T(8,128)(2,1)} %own_hbm.1, bf16[4,4,8,16,512]{4,3,2,1,0:T(8,128)(2,1)S(1)} %pad_maximum_fusion.near_hbm, ...), custom_call_target="tpu_custom_call" | custom-call | flops 8589934592 | bytes 8388608 | tf_op jit(solution)/shard_map/particle/pallas_call | solution.py:114
  (12 shorter events, 0.0 us)
Async XLA Ops:
  0.0 10.5 %copy-start = (bf16[256,256]{1,0:T(8,128)(2,1)S(1)}, bf16[256,256]{1,0:T(8,128)(2,1)}, u32[]{:S(2)}) copy-start(bf16[256,256]{1,0:T(8,128)(2,1)} %param.7) | copy-start | bytes 393220
  0.0 10.2 %copy-start.1 = (bf16[256,4,512]{2,1,0:T(4,128)(2,1)S(1)}, bf16[256,4,512]{2,1,0:T(4,128)(2,1)}, u32[]{:S(2)}) copy-start(bf16[256,4,512]{2,1,0:T(4,128)(2,1)} %param.6) | copy-start | bytes 3145732
  1.0 22.7 %collective-permute-start = (bf16[8,16,512]{2,1,0:T(8,128)(2,1)S(1)}, bf16[8,16,512]{2,1,0:T(8,128)(2,1)S(1)}, u32[]{:S(2)}, u32[]{:S(2)}) collective-permute-start(bf16[8,16,512]{2,1,0:T(8,128)(2,1)S(1)} %constant_dynamic-slice_fusion), channel_id=1, source_target_pairs={{0,1},{1,0},{2,3},{3,2},{4,5},{5,4},{6,7},{7,6},{8,9},{9,8},{10,11... | collective-permute-start | bytes 393224 | tf_op jit(solution)/shard_map/ppermute | solution.py:165
  12.7 52.9 %all-to-all-start = ((bf16[128,8,768]{2,1,0:T(8,128)(2,1)}), bf16[128,8,768]{2,1,0:T(8,128)(2,1)}, u32[]{:S(2)}, u32[]{:S(2)}) async-start(bf16[128,8,768]{2,1,0:T(8,128)(2,1)} %pad_maximum_fusion.1), calls=%async_computation | async-start | bytes 3145728 | tf_op jit(solution)/shard_map/all_to_all | solution.py:174
  23.7 11.5 %collective-permute-start.3 = (bf16[8,16,512]{2,1,0:T(8,128)(2,1)S(1)}, bf16[8,16,512]{2,1,0:T(8,128)(2,1)S(1)}, u32[]{:S(2)}, u32[]{:S(2)}) collective-permute-start(bf16[8,16,512]{2,1,0:T(8,128)(2,1)S(1)} %collective-permute-done), channel_id=1, source_target_pairs={{0,192},{2,50},{16,208},{18,2},{32,224},{34,18},{48,240},{50,34},{... | collective-permute-start | bytes 393224 | tf_op jit(solution)/shard_map/ppermute | solution.py:147
  26.4 12.0 %collective-permute-start.2 = (bf16[8,16,512]{2,1,0:T(8,128)(2,1)S(1)}, bf16[8,16,512]{2,1,0:T(8,128)(2,1)S(1)}, u32[]{:S(2)}, u32[]{:S(2)}) collective-permute-start(bf16[8,16,512]{2,1,0:T(8,128)(2,1)S(1)} %collective-permute-done), channel_id=1, source_target_pairs={{0,128},{2,34},{16,144},{18,50},{32,160},{34,2},{48,176},{50,18},{... | collective-permute-start | bytes 393224 | tf_op jit(solution)/shard_map/ppermute | solution.py:147
  26.9 13.8 %collective-permute-start.1 = (bf16[8,16,512]{2,1,0:T(8,128)(2,1)S(1)}, bf16[8,16,512]{2,1,0:T(8,128)(2,1)S(1)}, u32[]{:S(2)}, u32[]{:S(2)}) collective-permute-start(bf16[8,16,512]{2,1,0:T(8,128)(2,1)S(1)} %collective-permute-done), channel_id=1, source_target_pairs={{0,64},{2,18},{16,80},{18,34},{32,96},{34,50},{48,112},{50,2},{64,... | collective-permute-start | bytes 393224 | tf_op jit(solution)/shard_map/ppermute | solution.py:147
  40.8 12.3 %collective-permute-start.5 = (bf16[4,8,16,512]{3,2,1,0:T(8,128)(2,1)S(1)}, bf16[4,8,16,512]{3,2,1,0:T(8,128)(2,1)S(1)}, u32[]{:S(2)}, u32[]{:S(2)}) collective-permute-start(bf16[4,8,16,512]{3,2,1,0:T(8,128)(2,1)S(1)} %get-tuple-element.6), channel_id=1, source_target_pairs={{0,32},{2,130},{16,48},{18,146},{32,0},{34,162},{48,16},{50,178},{... | collective-permute-start | bytes 1572872 | tf_op jit(solution)/shard_map/ppermute | solution.py:147
  44.3 16.4 %collective-permute-start.4 = (bf16[4,8,16,512]{3,2,1,0:T(8,128)(2,1)S(1)}, bf16[4,8,16,512]{3,2,1,0:T(8,128)(2,1)S(1)}, u32[]{:S(2)}, u32[]{:S(2)}) collective-permute-start(bf16[4,8,16,512]{3,2,1,0:T(8,128)(2,1)S(1)} %get-tuple-element.6), channel_id=1, source_target_pairs={{0,16},{2,66},{16,32},{18,82},{32,48},{34,98},{48,0},{50,114},{64,... | collective-permute-start | bytes 1572872 | tf_op jit(solution)/shard_map/ppermute | solution.py:147
  44.3 16.4 %collective-permute-start.6 = (bf16[4,8,16,512]{3,2,1,0:T(8,128)(2,1)S(1)}, bf16[4,8,16,512]{3,2,1,0:T(8,128)(2,1)S(1)}, u32[]{:S(2)}, u32[]{:S(2)}) collective-permute-start(bf16[4,8,16,512]{3,2,1,0:T(8,128)(2,1)S(1)} %get-tuple-element.6), channel_id=1, source_target_pairs={{0,48},{2,194},{16,0},{18,210},{32,16},{34,226},{48,32},{50,242},{... | collective-permute-start | bytes 1572872 | tf_op jit(solution)/shard_map/ppermute | solution.py:147
  60.8 0.7 copy-start.2
  60.8 1.0 %copy-start.4 = (s32[2]{0:T(128)S(1)}, s32[2]{0:T(128)}, u32[]{:S(2)}) copy-start(s32[2]{0:T(128)} %param.9) | copy-start | bytes 28
  60.8 1.0 %copy-start.3 = (f32[16]{0:T(128)S(1)}, f32[16]{0:T(128)}, u32[]{:S(2)}) copy-start(f32[16]{0:T(128)} %param.10) | copy-start | bytes 196
  61.0 4.6 %collective-permute-start.7 = (bf16[4,4,8,16,512]{4,3,2,1,0:T(8,128)(2,1)S(1)}, bf16[4,4,8,16,512]{4,3,2,1,0:T(8,128)(2,1)}, u32[]{:S(2)}, u32[]{:S(2)}) collective-permute-start(bf16[4,4,8,16,512]{4,3,2,1,0:T(8,128)(2,1)S(1)} %pad_maximum_fusion.near_hbm), channel_id=1, source_target_pairs={{0,2},{2,0},{1,3},{3,1},{4,6},{6,4},{5,7},{7,5},{8,10},{10,8},{9,1... | collective-permute-start | bytes 6291464 | tf_op jit(solution)/shard_map/ppermute | solution.py:177
